TPU v7x, 128 devices: a whole 4x4x4 slice. The times are simulated.
128 devices in a mesh: wide: 32 (over y_lo, x, z), narrow: 4 (over y_hi, core).
Axes of the slice: x: 4, y: 4 (y_hi: 2, y_lo: 2; y = y_hi * 2 + y_lo), z: 4, core: 2. Of those that a mesh axis runs over, the one named last changes fastest.
Arguments:
- trial_x: float32 [262144, 128], P(('wide', 'narrow')), may hold values from -6 to 6
- trial_y: float32 [262144, 128], P(('wide', 'narrow')), may hold values from -6 to 6
- energy: float32 [262144], P(('wide', 'narrow')), may hold values from 1 to 4
- level_shift: float32 [128], replicated, may hold values from 0.1 to 0.5
- resonant_kernel: bfloat16 [1024, 8, 256, 256], P(('wide', 'narrow')), may hold values from -0.0625 to 0.0625
- resonant_list: int32 [1024, 8], P(('wide', 'narrow')), may hold values from 0 to 31, all different within a row
- coupling_kernel: bfloat16 [1024, 8, 256, 256], P(('wide', 'narrow')), may hold values from -0.0625 to 0.0625
- coupling_list: int32 [1024, 8], P(('wide', 'narrow')), may hold values from 0 to 31, all different within a row
- partner: int32 [32, 8192], P('wide'), may hold values from 0 to 8191, each once within a row
- exchange_basis: bfloat16 [262144, 1024], P(('wide', 'narrow')), may hold values from -0.0234375 to 0.0234375
Outputs:
- new_x: float32 [262144, 128], P(('wide', 'narrow'))
- new_y: float32 [262144, 128], P(('wide', 'narrow'))
Inputs may be any that keep to these rules, and one draw needn't show every extreme that they name: `resonant_list`: each row lists 8 different column blocks. `coupling_list`: each row lists 8 different column blocks. `partner`: each row is a permutation of the patch rows.
All inputs are finite; a program needn't handle non-finite values.
Results may differ from a plain program's by a relative error of at most 0.0038.
Values may be sent and summed in bfloat16 or wider, within the bound.
No kernel may reach another device: no remote copies, remote signals or barrier semaphores. Data moves between devices by JAX's collectives and lax.ppermute only.
A program may use at most 128 MiB of HBM per device.

v0:
```python
import jax
import jax.numpy as jnp
from jax import lax
from jax.sharding import PartitionSpec as P

BLK = 256
APPS = 2


def swapped(array, axis, stride):
    return lax.ppermute(array, axis, [(i, i ^ 1 << stride) for i in range(lax.axis_size(axis))])


def block_product(kernel, source, indices):
    columns = source.shape[1]
    tiles = source[indices]
    result = jnp.einsum("bnij,bnjc->bic", kernel, tiles, preferred_element_type=jnp.float32)
    return result.reshape(-1, columns)


def mirror_rows(stacked):
    top_bit = lax.axis_size("wide").bit_length() - 2
    moved = swapped(stacked, "wide", top_bit)
    return lax.all_gather(moved, "narrow", axis=0, tiled=True)


def exchange_term(summed, exchange_basis):
    partial_sum = lax.dot_general(
        exchange_basis, summed, (((0,), (0,)), ((), ())), preferred_element_type=jnp.float32
    )
    weights = lax.psum(partial_sum, ("wide", "narrow"))
    return jnp.dot(exchange_basis, weights.astype(jnp.bfloat16), preferred_element_type=jnp.float32)


def apply_once(
    trial_x,
    trial_y,
    energy,
    level_shift,
    resonant_kernel,
    resonant_list,
    coupling_kernel,
    coupling_list,
    partner,
    exchange_basis,
):
    vectors = trial_x.shape[1]
    stacked = jnp.concatenate([trial_x.astype(jnp.bfloat16), trial_y.astype(jnp.bfloat16)], axis=1)
    own_patch = lax.all_gather(stacked, "narrow", axis=0, tiled=True)
    mirror_patch = mirror_rows(stacked)
    offsets = jnp.arange(BLK, dtype=jnp.int32)
    own_indices = resonant_list[:, :, None] * BLK + offsets
    resonant = block_product(resonant_kernel, own_patch, own_indices)
    partner_indices = partner[0].reshape(-1, BLK)[coupling_list]
    coupling = block_product(coupling_kernel, mirror_patch, partner_indices)
    summed = (trial_x + trial_y).astype(jnp.bfloat16)
    exchange = exchange_term(summed, exchange_basis)
    levels = energy[:, None]
    shifts = level_shift[None, :]
    image_x = levels * trial_x + resonant[:, :vectors] + coupling[:, vectors:] + exchange
    image_y = -(levels * trial_y + resonant[:, vectors:] + coupling[:, :vectors] + exchange)
    next_x = (image_x - shifts * trial_x) / (levels - shifts)
    next_y = -(image_y - shifts * trial_y) / (levels + shifts)
    return (next_x, next_y)


def on_device(
    trial_x,
    trial_y,
    energy,
    level_shift,
    resonant_kernel,
    resonant_list,
    coupling_kernel,
    coupling_list,
    partner,
    exchange_basis,
):
    current_x, current_y = (trial_x, trial_y)
    for app_index in range(APPS):
        current_x, current_y = apply_once(
            current_x,
            current_y,
            energy,
            level_shift,
            resonant_kernel,
            resonant_list,
            coupling_kernel,
            coupling_list,
            partner,
            exchange_basis,
        )
    return (current_x, current_y)


def solution(mesh):
    return jax.shard_map(
        on_device,
        mesh=mesh,
        in_specs=(
            P(("wide", "narrow"), None),
            P(("wide", "narrow"), None),
            P(("wide", "narrow")),
            P(),
            P(("wide", "narrow"), None, None, None),
            P(("wide", "narrow"), None),
            P(("wide", "narrow"), None, None, None),
            P(("wide", "narrow"), None),
            P("wide", None),
            P(("wide", "narrow"), None),
        ),
        out_specs=(P(("wide", "narrow"), None), P(("wide", "narrow"), None)),
        check_vma=False,
    )
```

profile of v0, /device:TPU:1, one launch (start us, length us, event | category | flops | bytes accessed | tf_op | source)
XLA Modules:
  0.0 613.9 jit_solution(15115098581168945599)
XLA Ops:
  7.3 1.4 convert_element_type.24
  8.7 1.3 convert_element_type.25
  10.0 1.1 pad_maximum_fusion
  11.1 2.2 collective-permute-start
  13.3 32.0 %collective-permute-done = bf16[2048,256]{1,0:T(8,128)(2,1)S(1)} collective-permute-done((bf16[2048,256]{1,0:T(8,128)(2,1)}, bf16[2048,256]{1,0:T(8,128)(2,1)S(1)}, u32[]{:S(2)}, u32[]{:S(2)}) %collective-permute-start) | collective-permute-done | bytes 1048608 | tf_op jit(solution)/shard_map/ppermute | solution.py:11
  45.3 1.0 copy-done.3
  46.3 0.0 all-gather.9.cloned.1.call-start
  46.3 2.6 copy.12
  48.9 1.3 copy.16
  50.2 0.5 broadcast.86
  50.7 0.7 reduce.3
  51.5 0.1 reshape.62
  51.6 0.7 gather_fusion.1
  52.3 0.1 fusion.2
  52.4 2.9 convolution_bitcast_fusion.3
  55.4 96.2 %all-reduce.2 = bf16[1024,128]{0,1:T(8,128)(2,1)S(1)} all-reduce(f32[1024,128]{0,1:T(8,128)S(1)} %convolution_bitcast_fusion.3), channel_id=1, replica_groups=mesh['wide'=32,'narrow'=4] {'wide','narrow'}, use_global_device_ids=true, to_apply=%region_0.0 | all-reduce | flops 131072 | bytes 786432 | tf_op jit(solution)/shard_map/psum | solution.py:31
  151.6 63.6 %gather_fusion = bf16[16384,256]{1,0:T(8,128)(2,1)} fusion(bf16[8192,256]{1,0:T(8,128)(2,1)} %all-gather.5.cloned.1.call-done, s32[16384]{0:T(1024)S(1)} %broadcast_clamp_fusion.1), kind=kCustom, calls=%fused_computation | custom fusion | bytes 16842752 | tf_op jit(solution)/shard_map/gather | solution.py:16
  215.2 8.1 %fusion.10 = f32[8,256,256,1]{1,2,3,0:T(8,128)S(1)} fusion(bf16[8,8,256,256]{3,2,1,0:T(8,128)(2,1)} %param.14, bf16[8,8,256,256]{3,2,1,0:T(8,128)(2,1)} %bitcast.62), kind=kOutput, calls=%fused_computation.34 | convolution fusion | flops 2147483648 | bytes 18874368 | tf_op jit(solution)/shard_map/bnij,bnjc->bic/dot_general | solution.py:17
  223.3 0.1 fusion.8
  223.5 1.4 copy.32
  224.8 1.3 copy.34
  226.1 63.6 %gather_fusion.2 = bf16[16384,256]{1,0:T(8,128)(2,1)} fusion(bf16[8192,256]{1,0:T(8,128)(2,1)} %all-gather.7.cloned.1.call-done, s32[16384]{0:T(1024)S(1)} %broadcast_clamp_fusion), kind=kCustom, calls=%fused_computation.2 | custom fusion | bytes 16842752 | tf_op jit(solution)/shard_map/gather | solution.py:16
  289.8 8.1 %fusion.11 = f32[8,256,256,1]{1,2,3,0:T(8,128)S(1)} fusion(bf16[8,8,256,256]{3,2,1,0:T(8,128)(2,1)} %param.16, bf16[8,8,256,256]{3,2,1,0:T(8,128)(2,1)} %bitcast.63), kind=kOutput, calls=%fused_computation.35 | convolution fusion | flops 2147483648 | bytes 18874368 | tf_op jit(solution)/shard_map/bnij,bnjc->bic/dot_general | solution.py:17
  297.9 0.1 fusion.9
  298.0 1.3 copy.33
  299.4 0.3 copy.35
  299.7 6.6 %fusion.5 = (bf16[2048,128]{0,1:T(8,128)(2,1)S(1)}, f32[2048,128]{0,1:T(8,128)}, bf16[2048,128]{0,1:T(8,128)(2,1)S(1)}, f32[2048,128]{0,1:T(8,128)}) fusion(f32[2048,128]{0,1:T(8,128)} %copy.16, f32[128]{0:T(128)S(1)} %copy-done.9, f32[2048,128]{0,1:T(8,128)S(1)} %copy.35, f32[2048,128]{0,1:T(8,128)} %copy.34, f32[2048]{0:T(1024)S(1)} %copy-done.8, ...), kind=kOutput, calls=%fused_computation.29 | convolution fusion | flops 542113792 | bytes 13902336 | tf_op jit(solution)/shard_map/dot_general | solution.py:32
  306.4 1.0 pad_maximum_fusion.1
  307.5 0.3 collective-permute-start.1
  307.7 40.2 %collective-permute-done.1 = bf16[2048,256]{0,1:T(8,128)(2,1)S(1)} collective-permute-done((bf16[2048,256]{0,1:T(8,128)(2,1)}, bf16[2048,256]{0,1:T(8,128)(2,1)S(1)}, u32[]{:S(2)}, u32[]{:S(2)}) %collective-permute-start.1) | collective-permute-done | bytes 1048608 | tf_op jit(solution)/shard_map/ppermute | solution.py:11
  348.0 1.0 copy-done.4
  349.0 3.5 convolution_bitcast_fusion.2
  352.5 84.9 %all-reduce.3 = bf16[1024,128]{0,1:T(8,128)(2,1)S(1)} all-reduce(f32[1024,128]{0,1:T(8,128)S(1)} %convolution_bitcast_fusion.2), channel_id=1, replica_groups=mesh['wide'=32,'narrow'=4] {'wide','narrow'}, use_global_device_ids=true, to_apply=%region_1.0 | all-reduce | flops 131072 | bytes 786432 | tf_op jit(solution)/shard_map/psum | solution.py:31
  437.5 6.4 %copy.20 = bf16[8192,256]{1,0:T(8,128)(2,1)} copy(bf16[8192,256]{0,1:T(8,128)(2,1)} %all-gather.9.cloned.1.call-done) | data formatting | bytes 8388608 | tf_op jit(solution)/shard_map/all_gather | solution.py:49
  443.9 63.6 %gather_fusion.3 = bf16[16384,256]{1,0:T(8,128)(2,1)} fusion(bf16[8192,256]{1,0:T(8,128)(2,1)} %copy.20, s32[16384]{0:T(1024)S(1)} %broadcast_clamp_fusion.1), kind=kCustom, calls=%fused_computation.3 | custom fusion | bytes 16842752 | tf_op jit(solution)/shard_map/gather | solution.py:16
  507.5 8.1 %fusion.12 = f32[8,256,256,1]{1,2,3,0:T(8,128)S(1)} fusion(bf16[8,8,256,256]{3,2,1,0:T(8,128)(2,1)} %param.14, bf16[8,8,256,256]{3,2,1,0:T(8,128)(2,1)} %bitcast.60), kind=kOutput, calls=%fused_computation.36 | convolution fusion | flops 2147483648 | bytes 18874368 | tf_op jit(solution)/shard_map/bnij,bnjc->bic/dot_general | solution.py:17
  515.6 0.1 fusion.6
  515.7 0.3 copy.36
  516.1 1.3 copy.38
  517.4 6.4 %copy.22 = bf16[8192,256]{1,0:T(8,128)(2,1)} copy(bf16[8192,256]{0,1:T(8,128)(2,1)} %all-gather.11.cloned.1.call-done) | data formatting | bytes 8388608 | tf_op jit(solution)/shard_map/all_gather | solution.py:24
  523.7 63.6 %gather_fusion.4 = bf16[16384,256]{1,0:T(8,128)(2,1)} fusion(bf16[8192,256]{1,0:T(8,128)(2,1)} %copy.22, s32[16384]{0:T(1024)S(1)} %broadcast_clamp_fusion), kind=kCustom, calls=%fused_computation.4 | custom fusion | bytes 16842752 | tf_op jit(solution)/shard_map/gather | solution.py:16
  587.4 8.1 %fusion.13 = f32[8,256,256,1]{1,2,3,0:T(8,128)S(1)} fusion(bf16[8,8,256,256]{3,2,1,0:T(8,128)(2,1)} %param.16, bf16[8,8,256,256]{3,2,1,0:T(8,128)(2,1)} %bitcast.61), kind=kOutput, calls=%fused_computation.37 | convolution fusion | flops 2147483648 | bytes 18874368 | tf_op jit(solution)/shard_map/bnij,bnjc->bic/dot_general | solution.py:17
  595.5 0.1 fusion.7
  595.6 1.3 copy.37
  596.9 0.3 copy.39
  597.3 6.2 %add_divide_fusion = (f32[2048,128]{0,1:T(8,128)S(1)}, f32[2048,128]{0,1:T(8,128)}) fusion(f32[2048,128]{0,1:T(8,128)} %get-tuple-element.7, f32[2048,128]{0,1:T(8,128)S(1)} %copy.39, f32[2048,128]{0,1:T(8,128)} %copy.38, f32[128]{0:T(128)S(1)} %copy-done.9, f32[2048]{0:T(1024)S(1)} %copy-done.8, f32[2048,128]{0,1:T(8,128)} %get-tuple-element.19, ...), kind=kOutput, calls=%fused_computation.7 | convolution fusion | flops 541589504 | bytes 12853760 | tf_op jit(solution)/shard_map/dot_general | solution.py:32
  603.5 2.5 copy.24
  606.0 1.3 copy.25
  (38 shorter events, 0.4 us)
Async XLA Ops:
  7.2 45.3 %copy-start.1 = (f32[2048,128]{1,0:T(8,128)S(1)}, f32[2048,128]{1,0:T(8,128)}, u32[]{:S(2)}) copy-start(f32[2048,128]{1,0:T(8,128)} %param.10) | copy-start | bytes 3145732
  7.2 41.7 %copy-start = (f32[2048,128]{1,0:T(8,128)S(1)}, f32[2048,128]{1,0:T(8,128)}, u32[]{:S(2)}) copy-start(f32[2048,128]{1,0:T(8,128)} %param.11) | copy-start | bytes 3145732
  7.2 43.5 %copy-start.5 = (s32[1,8192]{1,0:T(1,128)S(1)}, s32[1,8192]{1,0:T(1,128)}, u32[]{:S(2)}) copy-start(s32[1,8192]{1,0:T(1,128)} %param.18) | copy-start | bytes 98308
  7.2 44.2 %copy-start.6 = (s32[8,8]{1,0:T(8,128)S(1)}, s32[8,8]{1,0:T(8,128)}, u32[]{:S(2)}) copy-start(s32[8,8]{1,0:T(8,128)} %param.17) | copy-start | bytes 772
  7.2 45.1 %copy-start.7 = (s32[8,8]{1,0:T(8,128)S(1)}, s32[8,8]{1,0:T(8,128)}, u32[]{:S(2)}) copy-start(s32[8,8]{1,0:T(8,128)} %param.15) | copy-start | bytes 772
  7.2 144.4 %all-gather.5.cloned.1.call-start = ((), (), s32[]{:S(2)}) async-start(), calls=%async_computation | async-start | bytes 5242880 | tf_op jit(solution)/shard_map/all_gather | solution.py:49
  11.1 215.1 %all-gather.7.cloned.1.call-start = ((), (), s32[]{:S(2)}) async-start(), calls=%async_computation.1 | async-start | bytes 5242880 | tf_op jit(solution)/shard_map/all_gather | solution.py:24
  11.1 34.2 %collective-permute-start = (bf16[2048,256]{1,0:T(8,128)(2,1)}, bf16[2048,256]{1,0:T(8,128)(2,1)S(1)}, u32[]{:S(2)}, u32[]{:S(2)}) collective-permute-start(bf16[2048,256]{1,0:T(8,128)(2,1)} %pad_maximum_fusion), channel_id=1, source_target_pairs={{0,64},{4,68},{8,72},{12,76},{16,80},{20,84},{24,88},{28,92},{32,9... | collective-permute-start | bytes 3145736 | tf_op jit(solution)/shard_map/ppermute | solution.py:11
  45.3 1.0 copy-start.3
  46.3 391.2 %all-gather.9.cloned.1.call-start = ((), (), s32[]{:S(2)}) async-start(), calls=%async_computation.2 | async-start | bytes 5242880 | tf_op jit(solution)/shard_map/all_gather | solution.py:49
  297.8 1.8 copy-start.2
  297.9 1.8 copy-start.8
  297.9 1.8 copy-start.9
  307.4 209.9 %all-gather.11.cloned.1.call-start = ((), (), s32[]{:S(2)}) async-start(), calls=%async_computation.3 | async-start | bytes 5242880 | tf_op jit(solution)/shard_map/all_gather | solution.py:24
  307.5 40.5 %collective-permute-start.1 = (bf16[2048,256]{0,1:T(8,128)(2,1)}, bf16[2048,256]{0,1:T(8,128)(2,1)S(1)}, u32[]{:S(2)}, u32[]{:S(2)}) collective-permute-start(bf16[2048,256]{0,1:T(8,128)(2,1)} %pad_maximum_fusion.1), channel_id=1, source_target_pairs={{0,64},{4,68},{8,72},{12,76},{16,80},{20,84},{24,88},{28,92},{32,9... | collective-permute-start | bytes 3145736 | tf_op jit(solution)/shard_map/ppermute | solution.py:11
  348.0 1.0 copy-start.4
Sparse Core Ops, SparseCore 0:
  11.2 52.8 all-gather.4
  65.7 38.9 all-gather.6
  307.5 51.1 all-gather.8
  360.3 35.7 all-gather.10
where the time goes:
time: 615 us; the launch traced here: 614 us
  local copies, waits for them, and re-layouts  286 us (47%)
  blocking collectives  181 us (29%)
  waiting for transfers between devices  72.3 us (12%)
  matrix products  51.7 us (8%)
  between operations  14.1 us (2%)
    gather x4, local copies, waits for them, and re-layouts, block_product(): tiles = source[indices]  254 us
    psum x2, blocking collectives, exchange_term(): weights = lax.psum(partial_sum, ('wide', 'narrow'))  181 us
    ppermute x2, waiting for transfers between devices, swapped(): lax.ppermute(array, axis, [(i, i ^ 1 << stride) for i in range(lax.axis_s...  72.2 us
    dot_general x4, matrix products, block_product(): jnp.einsum('bnij,bnjc->bic', kernel, tiles, preferred_element_type=jnp.fl...  32.4 us
    unnamed x35, local copies, waits for them, and re-layouts  17.9 us
    dot_general x2, matrix products, exchange_term(): jnp.dot(exchange_basis, weights.astype(jnp.bfloat16), preferred_element_t...  12.9 us
  transfers between devices with their start and end apart: 6, of which 2 were waited for; matrix products, arithmetic and copies ran while one was open for 27% of the time, Pallas kernels for 0%

commit v1 on v0

v1 whole, which is shorter than its diff:
```python
import jax
import jax.numpy as jnp
from jax import lax
from jax.experimental import pallas as pl
from jax.experimental.pallas import tpu as pltpu
from jax.sharding import PartitionSpec as P

BLK = 256
NV = 128
NBLK = 8
APPS = 2
AXES = ("wide", "narrow")
BF16 = jnp.bfloat16
F32 = jnp.float32
MIB = 1 << 20

VMEM_SPEC = pl.BlockSpec(memory_space=pltpu.VMEM)
SMEM_SPEC = pl.BlockSpec(memory_space=pltpu.SMEM)
ANY_SPEC = pl.BlockSpec(memory_space=pl.ANY)


def toggled(array, mask):
    return lax.ppermute(array, AXES, [(i, i ^ mask) for i in range(lax.axis_size(AXES))])


def interleave(x, y, scratch):
    scratch[pl.ds(0, BLK, stride=2), :] = x
    scratch[pl.ds(1, BLK, stride=2), :] = y
    return scratch[...].astype(BF16)


def split_matrix():
    row = lax.broadcasted_iota(jnp.int32, (BLK, BLK), 0)
    col = lax.broadcasted_iota(jnp.int32, (BLK, BLK), 1)
    half = BLK // 2
    hit = (col == 2 * row) | (col == 2 * (row - half) + 1)
    return jnp.where(hit, 1.0, 0.0).astype(F32).astype(BF16)


def split_block(flat, block, out, select):
    base = pl.multiple_of(block * 2 * BLK, 2 * BLK)
    half = BLK // 2
    pair = jnp.concatenate([flat[pl.ds(base, BLK), :], flat[pl.ds(base + BLK, BLK), :]], axis=1)
    parts = jnp.dot(select, pair, preferred_element_type=F32).astype(BF16)
    out[block, 0:half, 0:NV] = parts[0:half, 0:NV]
    out[block, half:BLK, 0:NV] = parts[0:half, NV:]
    out[block, 0:half, NV:] = parts[half:, 0:NV]
    out[block, half:BLK, NV:] = parts[half:, NV:]


def pack_body(x_ref, y_ref, out_ref, scratch):
    out_ref[...] = interleave(x_ref[...], y_ref[...], scratch)


def pack(x, y):
    rows = x.shape[0]
    block = pl.BlockSpec((BLK, NV), lambda b: (b, 0))
    return pl.pallas_call(
        pack_body,
        grid=(rows // BLK,),
        in_specs=[block, block],
        out_specs=pl.BlockSpec((2 * BLK, NV), lambda b: (b, 0)),
        out_shape=jax.ShapeDtypeStruct((2 * rows, NV), BF16),
        scratch_shapes=[pltpu.VMEM((2 * BLK, NV), F32)],
        name="pack",
    )(x, y)


def project_body(x_ref, y_ref, basis_ref, out_ref):
    @pl.when(pl.program_id(0) == 0)
    def _():
        out_ref[...] = jnp.zeros_like(out_ref)

    summed = (x_ref[...] + y_ref[...]).astype(BF16)
    out_ref[...] += lax.dot_general(
        basis_ref[...], summed, (((0,), (0,)), ((), ())), preferred_element_type=F32
    )


def project(x, y, basis):
    rows, rank = basis.shape
    block = pl.BlockSpec((BLK, NV), lambda b: (b, 0))
    return pl.pallas_call(
        project_body,
        grid=(rows // BLK,),
        in_specs=[block, block, pl.BlockSpec((BLK, rank), lambda b: (b, 0))],
        out_specs=pl.BlockSpec((rank, NV), lambda b: (0, 0)),
        out_shape=jax.ShapeDtypeStruct((rank, NV), F32),
        name="project",
    )(x, y, basis)


def mirror_body(slot_ref, partner_ref, list_ref, *refs):
    chunks = refs[:8]
    kernel_hbm, out_ref, source, gathered, columns, kernel, chunk_sems, kernel_sems = refs[8:]
    rows = chunks[0].shape[0]
    flat = source.reshape(2 * source.shape[0], NV)
    copies = []
    for k in range(8):
        slot = slot_ref[0] ^ (k // 2)
        start = pl.multiple_of(slot * 2 * rows + (k % 2) * rows, rows)
        copies.append(pltpu.make_async_copy(chunks[k], flat.at[pl.ds(start, rows)], chunk_sems.at[k]))
        copies[-1].start()
    blocks = kernel.shape[0]
    loads = [pltpu.make_async_copy(kernel_hbm.at[b], kernel.at[b], kernel_sems.at[b]) for b in range(blocks)]
    for load in loads:
        load.start()
    for copy in copies:
        copy.wait()
    unroll = 64

    def gather(step, carry):
        base = step * unroll
        for u in range(unroll):
            gathered[base + u] = source[partner_ref[0, base + u]]
        return carry

    lax.fori_loop(0, source.shape[0] // unroll, gather, 0)
    select = split_matrix()
    flat_out = gathered.reshape(2 * gathered.shape[0], NV)

    def split(block, carry):
        split_block(flat_out, block, columns, select)
        return carry

    lax.fori_loop(0, columns.shape[0], split, 0, unroll=2)
    for load in loads:
        load.wait()

    def product(b, carry):
        total = jnp.dot(kernel[b, 0], columns[list_ref[b, 0]], preferred_element_type=F32)
        for n in range(1, NBLK):
            total += jnp.dot(kernel[b, n], columns[list_ref[b, n]], preferred_element_type=F32)
        out_ref[b] = total
        return carry

    lax.fori_loop(0, blocks, product, 0)


def mirror_product(slot, partner, indices, chunks, kernel):
    patch = partner.shape[1]
    blocks = kernel.shape[0]
    return pl.pallas_call(
        mirror_body,
        in_specs=[SMEM_SPEC] * 3 + [ANY_SPEC] * 9,
        out_specs=VMEM_SPEC,
        out_shape=jax.ShapeDtypeStruct((blocks, BLK, 2 * NV), F32),
        scratch_shapes=[
            pltpu.VMEM((patch, 2, NV), BF16),
            pltpu.VMEM((patch, 2, NV), BF16),
            pltpu.VMEM((patch // BLK, BLK, 2 * NV), BF16),
            pltpu.VMEM(kernel.shape, BF16),
            pltpu.SemaphoreType.DMA((8,)),
            pltpu.SemaphoreType.DMA((blocks,)),
        ],
        compiler_params=pltpu.CompilerParams(vmem_limit_bytes=40 * MIB),
        name="mirror_product",
    )(slot, partner, indices, *chunks, kernel)


def column_of(row):
    return jnp.broadcast_to(row, (NV, NV)).T


def finish_body(last, slot_ref, list_ref, *refs):
    chunks = refs[:8]
    rest = refs[8:]
    x_ref, y_ref, energy_ref, shift_ref, kernel_ref, basis_ref, weight_ref, mirror_ref = rest[:8]
    if last:
        next_x_ref, next_y_ref, flat, columns, chunk_sems = rest[8:]
    else:
        next_x_ref, next_y_ref, packed_ref, project_ref, flat, columns, chunk_sems, scratch = rest[8:]
    b = pl.program_id(0)
    rows = chunks[0].shape[0]

    @pl.when(b == 0)
    def _():
        copies = []
        for k in range(8):
            slot = slot_ref[0] ^ (k // 2)
            start = pl.multiple_of(slot * 2 * rows + (k % 2) * rows, rows)
            copies.append(pltpu.make_async_copy(chunks[k], flat.at[pl.ds(start, rows)], chunk_sems.at[k]))
            copies[-1].start()
        for copy in copies:
            copy.wait()
        select = split_matrix()

        def split(block, carry):
            split_block(flat, block, columns, select)
            return carry

        lax.fori_loop(0, columns.shape[0], split, 0, unroll=2)
        if not last:
            project_ref[...] = jnp.zeros_like(project_ref)

    total = mirror_ref[0]
    exchange = jnp.dot(basis_ref[...], weight_ref[...], preferred_element_type=F32)
    direct = jnp.dot(kernel_ref[0, 0], columns[list_ref[b, 0]], preferred_element_type=F32)
    for n in range(1, NBLK):
        direct += jnp.dot(kernel_ref[0, n], columns[list_ref[b, n]], preferred_element_type=F32)
    shifts = shift_ref[...]
    half = BLK // 2
    levels = jnp.concatenate([column_of(energy_ref[0, 0:1, 0:half]), column_of(energy_ref[0, 0:1, half:])], axis=0)
    next_x = x_ref[...] + (direct[:, :NV] + total[:, NV:] + exchange) / (levels - shifts)
    next_y = y_ref[...] + (direct[:, NV:] + total[:, :NV] + exchange) / (levels + shifts)
    next_x_ref[...] = next_x
    next_y_ref[...] = next_y
    if not last:
        packed_ref[...] = interleave(next_x, next_y, scratch)
        project_ref[...] += lax.dot_general(
            basis_ref[...], (next_x + next_y).astype(BF16), (((0,), (0,)), ((), ())), preferred_element_type=F32
        )


def finish(last, slot, indices, chunks, x, y, energy, shift, kernel, basis, weights, mirrored):
    rows, rank = basis.shape
    blocks = kernel.shape[0]
    patch = 4 * rows
    vector = pl.BlockSpec((BLK, NV), lambda b: (b, 0))
    out_specs = [vector, vector]
    out_shape = [jax.ShapeDtypeStruct((rows, NV), F32)] * 2
    scratch = [
        pltpu.VMEM((2 * patch, NV), BF16),
        pltpu.VMEM((patch // BLK, BLK, 2 * NV), BF16),
        pltpu.SemaphoreType.DMA((8,)),
    ]
    if not last:
        out_specs += [pl.BlockSpec((2 * BLK, NV), lambda b: (b, 0)), pl.BlockSpec((rank, NV), lambda b: (0, 0))]
        out_shape += [jax.ShapeDtypeStruct((2 * rows, NV), BF16), jax.ShapeDtypeStruct((rank, NV), F32)]
        scratch += [pltpu.VMEM((2 * BLK, NV), F32)]

    def body(*refs):
        finish_body(last, *refs)

    return pl.pallas_call(
        body,
        grid=(blocks,),
        in_specs=[SMEM_SPEC] * 2
        + [ANY_SPEC] * 8
        + [
            vector,
            vector,
            pl.BlockSpec((1, 1, BLK), lambda b: (b, 0, 0)),
            pl.BlockSpec((1, NV), lambda b: (0, 0)),
            pl.BlockSpec((1, NBLK, BLK, BLK), lambda b: (b, 0, 0, 0)),
            pl.BlockSpec((BLK, rank), lambda b: (b, 0)),
            pl.BlockSpec((rank, NV), lambda b: (0, 0)),
            pl.BlockSpec((1, BLK, 2 * NV), lambda b: (b, 0, 0)),
        ],
        out_specs=out_specs,
        out_shape=out_shape,
        scratch_shapes=scratch,
        compiler_params=pltpu.CompilerParams(vmem_limit_bytes=40 * MIB),
        name="finish_last" if last else "finish",
    )(slot, indices, *chunks, x, y, energy, shift, kernel, basis, weights, mirrored)


def total_weights(partial):
    size = lax.axis_size(AXES)
    rank, vectors = partial.shape
    part = rank // size
    pieces = lax.all_to_all(partial.reshape(size, part, vectors), AXES, 0, 0, tiled=True)
    own = jnp.sum(pieces, axis=0).astype(BF16)
    spread = lax.all_to_all(jnp.broadcast_to(own[None], (size, part, vectors)), AXES, 0, 0, tiled=True)
    return spread.reshape(rank, vectors)


def on_device(x, y, energy, shift, res_kernel, res_list, cp_kernel, cp_list, partner, basis):
    size = lax.axis_size(AXES)
    narrow = lax.axis_size("narrow")
    near = size // 2
    far = near | (narrow // 2)
    slot = lax.axis_index("narrow").astype(jnp.int32).reshape(1)
    blocks = res_kernel.shape[0]
    levels = energy.reshape(blocks, 1, BLK)
    shifts = shift.reshape(1, NV)
    packed = pack(x, y)
    partial = project(x, y, basis)
    for app in range(APPS):
        last = app == APPS - 1
        half = packed.shape[0] // 2
        low, high = packed[:half], packed[half:]
        far_low = toggled(low, far)
        near_high = toggled(high, near)
        far_high = toggled(high, far)
        near_low = toggled(low, near)
        own_low, own_high = toggled(low, 1), toggled(high, 1)
        across_low = toggled(far_low, near)
        across_high = toggled(near_high, far)
        first = [near_low, near_high]
        second = [far_low, far_high]
        mirror_chunks = first + [toggled(c, 1) for c in first] + second + [toggled(c, 1) for c in second]
        across = [across_low, across_high]
        own_chunks = [low, high, own_low, own_high] + across + [toggled(c, 1) for c in across]
        weights = total_weights(partial)
        mirrored = mirror_product(slot, partner, cp_list, mirror_chunks, cp_kernel)
        out = finish(
            last, slot, res_list, own_chunks, x, y, levels, shifts, res_kernel, basis, weights, mirrored
        )
        if last:
            return tuple(out)
        x, y, packed, partial = out


def solution(mesh):
    return jax.shard_map(
        on_device,
        mesh=mesh,
        in_specs=(
            P(AXES, None),
            P(AXES, None),
            P(AXES),
            P(),
            P(AXES, None, None, None),
            P(AXES, None),
            P(AXES, None, None, None),
            P(AXES, None),
            P("wide", None),
            P(AXES, None),
        ),
        out_specs=(P(AXES, None), P(AXES, None)),
        check_vma=False,
    )
```

time: 615 us -> 226 us (0.37)
  local copies, waits for them, and re-layouts: 286 us -> 18.8 us
  blocking collectives: 181 us -> 0 us
  Pallas kernels: 0 us -> 86.8 us
  starting transfers between devices: 2.62 us -> 68 us
  matrix products: 51.7 us -> 0 us
  waiting for transfers between devices: 72.3 us -> 47.5 us
  between operations: 14.1 us -> 1.19 us
    gather x5 -> x0, local copies, waits for them, and re-layouts: 255 us -> none  [the longest x4 254 us: block_product(): tiles = source[indices]]
    psum x2 -> x0, blocking collectives: 181 us -> none  [exchange_term(): weights = lax.psum(partial_sum, ('wide', 'narrow'))]
    pallas_call x0 -> x6, Pallas kernels: none -> 86.8 us  [the longest x2 41.4 us: mirror_product(): pl.pallas_call(mirror_body, in_specs=[SMEM_SPEC] * 3 + [ANY_SPEC] * 9, ou...]
    dot_general x8 -> x0, matrix products: 51.7 us -> none  [the longest x4 32.4 us: block_product(): jnp.einsum('bnij,bnjc->bic', kernel, tiles, preferred_element_type=jnp.fl...]
    ppermute x2 -> x28, waiting for transfers between devices: 72.2 us -> 31.2 us  [toggled(): lax.ppermute(array, AXES, [(i, i ^ mask) for i in range(lax.axis_size(AXE...]
    ppermute x2 -> x28, starting transfers between devices: 2.46 us -> 38.8 us  [toggled(): lax.ppermute(array, AXES, [(i, i ^ mask) for i in range(lax.axis_size(AXE...]
    all_to_all x0 -> x4, starting transfers between devices: none -> 29.2 us  [the longest x2 18.6 us: total_weights(): lax.all_to_all(partial.reshape(size, part, vectors), AXES, 0, 0, tiled=True)]
    all_to_all x0 -> x4, waiting for transfers between devices: none -> 16.3 us  [the longest x2 16.3 us: total_weights(): lax.all_to_all(partial.reshape(size, part, vectors), AXES, 0, 0, tiled=True)]
  transfers between devices with their start and end apart: 6 -> 32, of which waited for: 2 -> 7; matrix products, arithmetic and copies ran while one was open for 27% -> 2% of each run, Pallas kernels for 0% -> 22%
where the time goes in v1:
time: 226 us; the launch traced here: 225 us
  Pallas kernels  86.8 us (38%)
  starting transfers between devices  68 us (30%)
  waiting for transfers between devices  47.5 us (21%)
  local copies, waits for them, and re-layouts  18.8 us (8%)
  other arithmetic  2.36 us (1%)
    pallas_call x2, Pallas kernels, mirror_product(): pl.pallas_call(mirror_body, in_specs=[SMEM_SPEC] * 3 + [ANY_SPEC] * 9, ou...  41.4 us
    ppermute x28, starting transfers between devices, toggled(): lax.ppermute(array, AXES, [(i, i ^ mask) for i in range(lax.axis_size(AXE...  38.8 us
    pallas_call x2, Pallas kernels, finish(): pl.pallas_call(body, grid=(blocks,), in_specs=[SMEM_SPEC] * 2 + [ANY_SPEC...  32.4 us
    ppermute x28, waiting for transfers between devices, toggled(): lax.ppermute(array, AXES, [(i, i ^ mask) for i in range(lax.axis_size(AXE...  31.2 us
    all_to_all x2, starting transfers between devices, total_weights(): lax.all_to_all(partial.reshape(size, part, vectors), AXES, 0, 0, tiled=True)  18.6 us
    all_to_all x2, waiting for transfers between devices, total_weights(): lax.all_to_all(partial.reshape(size, part, vectors), AXES, 0, 0, tiled=True)  16.3 us
    unnamed x62, local copies, waits for them, and re-layouts  15.9 us
    all_to_all x2, starting transfers between devices, total_weights(): lax.all_to_all(jnp.broadcast_to(own[None], (size, part, vectors)), AXES,...  10.6 us
  transfers between devices with their start and end apart: 32, of which 7 were waited for; matrix products, arithmetic and copies ran while one was open for 2% of the time, Pallas kernels for 22%

profile of v1, /device:TPU:1, one launch (start us, length us, event | category | flops | bytes accessed | tf_op | source)
XLA Modules:
  0.0 224.7 jit_solution(4477611897462310112)
XLA Ops:
  0.6 5.6 %pack.1 = bf16[4096,128]{1,0:T(8,128)(2,1)} custom-call(f32[2048,128]{1,0:T(8,128)} %refs_10_.1, f32[2048,128]{1,0:T(8,128)} %refs_11_.1), custom_call_target="tpu_custom_call" | custom-call | tf_op jit(solution)/shard_map/pack/pallas_call | solution.py:58
  6.2 1.3 fusion.1
  7.5 2.2 collective-permute-start.4
  9.7 1.9 collective-permute-start.2
  12.3 8.6 %collective-permute-done.4.refs_1_ = bf16[2048,128]{1,0:T(8,128)(2,1)S(1)} collective-permute-done((bf16[2048,128]{1,0:T(8,128)(2,1)S(1)}, bf16[2048,128]{1,0:T(8,128)(2,1)S(1)}, u32[]{:S(2)}, u32[]{:S(2)}) %collective-permute-start.4) | collective-permute-done | bytes 524320 | tf_op jit(solution)/shard_map/ppermute | solution.py:23
  20.9 2.8 %collective-permute-start.10 = (bf16[2048,128]{1,0:T(8,128)(2,1)S(1)}, bf16[2048,128]{1,0:T(8,128)(2,1)}, u32[]{:S(2)}, u32[]{:S(2)}) collective-permute-start(bf16[2048,128]{1,0:T(8,128)(2,1)S(1)} %collective-permute-done.4.refs_1_), channel_id=1, source_target_pairs={{0,1},{1,0},{2,3},{3,2},{4,5},{5,4},{6,7},{7,6},{8,9},{9,8},{10,11... | collective-permute-start | bytes 1572872 | tf_op jit(solution)/shard_map/ppermute | solution.py:23
  23.7 2.9 %collective-permute-start.12 = (bf16[2048,128]{1,0:T(8,128)(2,1)S(1)}, bf16[2048,128]{1,0:T(8,128)(2,1)}, u32[]{:S(2)}, u32[]{:S(2)}) collective-permute-start(bf16[2048,128]{1,0:T(8,128)(2,1)S(1)} %collective-permute-done.2.refs_4_), channel_id=1, source_target_pairs={{0,1},{1,0},{2,3},{3,2},{4,5},{5,4},{6,7},{7,6},{8,9},{9,8},{10,11... | collective-permute-start | bytes 1572872 | tf_op jit(solution)/shard_map/ppermute | solution.py:23
  26.6 8.0 %collective-permute-done.11.refs_5_ = bf16[2048,128]{1,0:T(8,128)(2,1)S(1)} collective-permute-done((bf16[2048,128]{1,0:T(8,128)(2,1)S(1)}, bf16[2048,128]{1,0:T(8,128)(2,1)S(1)}, u32[]{:S(2)}, u32[]{:S(2)}) %collective-permute-start.11) | collective-permute-done | bytes 524320 | tf_op jit(solution)/shard_map/ppermute | solution.py:23
  34.6 1.8 collective-permute-start.13
  36.5 2.0 collective-permute-start.5
  38.4 7.4 %project.1 = f32[1024,128]{1,0:T(8,128)} custom-call(f32[2048,128]{1,0:T(8,128)} %refs_10_.1, f32[2048,128]{1,0:T(8,128)} %refs_11_.1, bf16[2048,1024]{1,0:T(8,128)(2,1)} %refs_15_.3), custom_call_target="tpu_custom_call" | custom-call | tf_op jit(solution)/shard_map/project/pallas_call | solution.py:83
  45.8 9.4 %all-to-all-start = ((f32[128,8,128]{2,1,0:T(8,128)}), f32[128,8,128]{2,1,0:T(8,128)}, u32[]{:S(2)}, u32[]{:S(2)}) async-start(f32[128,8,128]{2,1,0:T(8,128)} %bitcast.14), calls=%async_computation | async-start | bytes 1048576 | tf_op jit(solution)/shard_map/all_to_all | solution.py:262
  55.2 1.2 collective-permute-start.9
  57.5 11.0 %all-to-all-done = f32[128,8,128]{2,1,0:T(8,128)} async-done(((f32[128,8,128]{2,1,0:T(8,128)}), f32[128,8,128]{2,1,0:T(8,128)}, u32[]{:S(2)}, u32[]{:S(2)}) %all-to-all-start) | async-done | bytes 524320 | tf_op jit(solution)/shard_map/all_to_all | solution.py:262
  68.5 1.2 reduce_sum.18
  70.4 4.6 %all-to-all-start.1 = ((bf16[128,8,128]{2,1,0:T(8,128)(2,1)}), bf16[128,8,128]{2,1,0:T(8,128)(2,1)S(1)}, u32[]{:S(2)}, u32[]{:S(2)}) async-start(bf16[128,8,128]{2,1,0:T(8,128)(2,1)} %broadcast_in_dim.4), calls=%async_computation.1 | async-start | bytes 524288 | tf_op jit(solution)/shard_map/all_to_all | solution.py:264
  75.1 1.0 copy-done.10
  76.2 1.0 copy-done.12
  77.2 1.0 copy-done.16
  78.3 1.0 copy-done.18
  79.3 20.7 %mirror_product.2.refs_17_ = f32[8,256,256]{2,1,0:T(8,128)S(1)} custom-call(s32[1]{0:T(128)} %bitcast.slot_ref.refs_0_, s32[1,8192]{1,0:T(1,128)S(1)} %copy-done.26, s32[8,8]{1,0:T(8,128)S(1)} %copy-done.28, bf16[2048,128]{1,0:T(8,128)(2,1)S(1)} %copy-done.18, bf16[2048,128]{1,0:T(8,128)(2,1)S(1)} %copy-done.10, ...), custom_call_target="tpu_custom_call" | custom-call | tf_op jit(solution)/shard_map/mirror_product/pallas_call | solution.py:143
  100.0 1.3 copy-done.3
  101.4 1.6 copy-done.4
  103.0 17.4 %finish.1 = (f32[2048,128]{1,0:T(8,128)S(1)}, f32[2048,128]{1,0:T(8,128)S(1)}, bf16[4096,128]{1,0:T(8,128)(2,1)S(1)}, f32[1024,128]{1,0:T(8,128)S(1)}) custom-call(s32[1]{0:T(128)} %bitcast.slot_ref.refs_0_, s32[8,8]{1,0:T(8,128)S(1)} %copy-done.29, bf16[2048,128]{1,0:T(8,128)(2,1)S(1)} %get-tuple-element.13.refs_2_, ...), custom_call_target="tpu_custom_call" | custom-call | tf_op jit(solution)/shard_map/finish/pallas_call | solution.py:235
  120.5 1.4 collective-permute-start.18
  122.0 1.8 collective-permute-start.16
  124.7 8.3 %collective-permute-done.18.refs_1_ = bf16[2048,128]{1,0:T(8,128)(2,1)S(1)} collective-permute-done((bf16[2048,128]{1,0:T(8,128)(2,1)S(1)}, bf16[2048,128]{1,0:T(8,128)(2,1)S(1)}, u32[]{:S(2)}, u32[]{:S(2)}) %collective-permute-start.18) | collective-permute-done | bytes 524320 | tf_op jit(solution)/shard_map/ppermute | solution.py:23
  133.0 3.5 %collective-permute-start.24 = (bf16[2048,128]{1,0:T(8,128)(2,1)S(1)}, bf16[2048,128]{1,0:T(8,128)(2,1)}, u32[]{:S(2)}, u32[]{:S(2)}) collective-permute-start(bf16[2048,128]{1,0:T(8,128)(2,1)S(1)} %collective-permute-done.18.refs_1_), channel_id=1, source_target_pairs={{0,1},{1,0},{2,3},{3,2},{4,5},{5,4},{6,7},{7,6},{8,9},{9,8},{10,11... | collective-permute-start | bytes 1572872 | tf_op jit(solution)/shard_map/ppermute | solution.py:23
  136.5 2.2 collective-permute-start.26
  138.6 5.6 %collective-permute-done.22.refs_0_ = bf16[2048,128]{1,0:T(8,128)(2,1)S(1)} collective-permute-done((bf16[2048,128]{1,0:T(8,128)(2,1)S(1)}, bf16[2048,128]{1,0:T(8,128)(2,1)S(1)}, u32[]{:S(2)}, u32[]{:S(2)}) %collective-permute-start.22) | collective-permute-done | bytes 524320 | tf_op jit(solution)/shard_map/ppermute | solution.py:23
  144.3 1.9 collective-permute-start.23
  146.2 1.4 collective-permute-start.17
  147.5 1.9 collective-permute-start.19
  149.4 9.2 %all-to-all-start.2 = ((f32[128,8,128]{2,1,0:T(8,128)}), f32[128,8,128]{2,1,0:T(8,128)}, u32[]{:S(2)}, u32[]{:S(2)}) async-start(f32[128,8,128]{2,1,0:T(8,128)} %bitcast.9), calls=%async_computation.2 | async-start | bytes 1048576 | tf_op jit(solution)/shard_map/all_to_all | solution.py:262
  158.6 1.2 collective-permute-start.14
  161.3 5.3 %collective-permute-start.21 = (bf16[2048,128]{1,0:T(8,128)(2,1)}, bf16[2048,128]{1,0:T(8,128)(2,1)}, u32[]{:S(2)}, u32[]{:S(2)}) collective-permute-start(bf16[2048,128]{1,0:T(8,128)(2,1)} %collective-permute-done.19.refs_7_), channel_id=1, source_target_pairs={{0,1},{1,0},{2,3},{3,2},{4,5},{5,4},{6,7},{7,6},{8,9},{9,8},{10,11... | collective-permute-start | bytes 1572872 | tf_op jit(solution)/shard_map/ppermute | solution.py:23
  166.6 5.3 %all-to-all-done.2 = f32[128,8,128]{2,1,0:T(8,128)} async-done(((f32[128,8,128]{2,1,0:T(8,128)}), f32[128,8,128]{2,1,0:T(8,128)}, u32[]{:S(2)}, u32[]{:S(2)}) %all-to-all-start.2) | async-done | bytes 524320 | tf_op jit(solution)/shard_map/all_to_all | solution.py:262
  171.9 1.2 reduce_sum.19
  173.8 6.0 %all-to-all-start.3 = ((bf16[128,8,128]{2,1,0:T(8,128)(2,1)}), bf16[128,8,128]{2,1,0:T(8,128)(2,1)S(1)}, u32[]{:S(2)}, u32[]{:S(2)}) async-start(bf16[128,8,128]{2,1,0:T(8,128)(2,1)} %broadcast_in_dim.5), calls=%async_computation.3 | async-start | bytes 524288 | tf_op jit(solution)/shard_map/all_to_all | solution.py:264
  179.9 1.0 copy-done.14
  180.9 1.0 copy-done.20
  182.0 1.0 copy-done.22
  183.0 1.0 copy-done.24
  184.1 20.7 %mirror_product.3.refs_17_ = f32[8,256,256]{2,1,0:T(8,128)S(1)} custom-call(s32[1]{0:T(128)} %bitcast.slot_ref.refs_0_, s32[1,8192]{1,0:T(1,128)S(1)} %copy-done.26, s32[8,8]{1,0:T(8,128)S(1)} %copy-done.28, bf16[2048,128]{1,0:T(8,128)(2,1)S(1)} %copy-done.22, bf16[2048,128]{1,0:T(8,128)(2,1)S(1)} %copy-done.14, ...), custom_call_target="tpu_custom_call" | custom-call | tf_op jit(solution)/shard_map/mirror_product/pallas_call | solution.py:143
  204.8 2.2 copy-done
  207.0 1.2 copy-done.6
  208.2 1.2 copy-done.8
  209.4 15.1 %finish_last.1 = (f32[2048,128]{1,0:T(8,128)}, f32[2048,128]{1,0:T(8,128)}) custom-call(s32[1]{0:T(128)} %bitcast.slot_ref.refs_0_, s32[8,8]{1,0:T(8,128)S(1)} %copy-done.29, bf16[2048,128]{1,0:T(8,128)(2,1)S(1)} %get-tuple-element.11.refs_2_, bf16[2048,128]{1,0:T(8,128)(2,1)S(1)} %get-tuple-element.10.refs_3_, ...), custom_call_target="tpu_custom_call" | custom-call | tf_op jit(solution)/shard_map/finish_last/pallas_call | solution.py:235
  (90 shorter events, 5.9 us)
Async XLA Ops:
  7.5 13.5 %collective-permute-start.4 = (bf16[2048,128]{1,0:T(8,128)(2,1)S(1)}, bf16[2048,128]{1,0:T(8,128)(2,1)S(1)}, u32[]{:S(2)}, u32[]{:S(2)}) collective-permute-start(bf16[2048,128]{1,0:T(8,128)(2,1)S(1)} %get-tuple-element.12.refs_3_), channel_id=1, source_target_pairs={{0,64},{1,65},{2,66},{3,67},{4,68},{5,69},{6,70},{7,71},{8,72},{9,... | collective-permute-start | bytes 1572872 | tf_op jit(solution)/shard_map/ppermute | solution.py:23
  9.7 65.4 %copy-start.26 = (s32[1,8192]{1,0:T(1,128)S(1)}, s32[1,8192]{1,0:T(1,128)}, u32[]{:S(2)}) copy-start(s32[1,8192]{1,0:T(1,128)} %partner_ref.3) | copy-start | bytes 98308
  9.7 65.5 %copy-start.28 = (s32[8,8]{1,0:T(8,128)S(1)}, s32[8,8]{1,0:T(8,128)}, u32[]{:S(2)}) copy-start(s32[8,8]{1,0:T(8,128)} %list_ref.3) | copy-start | bytes 772
  9.7 14.1 %collective-permute-start.2 = (bf16[2048,128]{1,0:T(8,128)(2,1)S(1)}, bf16[2048,128]{1,0:T(8,128)(2,1)S(1)}, u32[]{:S(2)}, u32[]{:S(2)}) collective-permute-start(bf16[2048,128]{1,0:T(8,128)(2,1)S(1)} %get-tuple-element.13.refs_2_), channel_id=1, source_target_pairs={{0,66},{1,67},{2,64},{3,65},{4,70},{5,71},{6,68},{7,69},{8,74},{9,... | collective-permute-start | bytes 1572872 | tf_op jit(solution)/shard_map/ppermute | solution.py:23
  11.6 23.1 %collective-permute-start.11 = (bf16[2048,128]{1,0:T(8,128)(2,1)S(1)}, bf16[2048,128]{1,0:T(8,128)(2,1)S(1)}, u32[]{:S(2)}, u32[]{:S(2)}) collective-permute-start(bf16[2048,128]{1,0:T(8,128)(2,1)S(1)} %get-tuple-element.12.refs_3_), channel_id=1, source_target_pairs={{0,66},{1,67},{2,64},{3,65},{4,70},{5,71},{6,68},{7,69},{8,74},{9,... | collective-permute-start | bytes 1572872 | tf_op jit(solution)/shard_map/ppermute | solution.py:23
  12.3 24.1 %collective-permute-start.8 = (bf16[2048,128]{1,0:T(8,128)(2,1)S(1)}, bf16[2048,128]{1,0:T(8,128)(2,1)S(1)}, u32[]{:S(2)}, u32[]{:S(2)}) collective-permute-start(bf16[2048,128]{1,0:T(8,128)(2,1)S(1)} %get-tuple-element.13.refs_2_), channel_id=1, source_target_pairs={{0,64},{1,65},{2,66},{3,67},{4,68},{5,69},{6,70},{7,71},{8,72},{9,... | collective-permute-start | bytes 1572872 | tf_op jit(solution)/shard_map/ppermute | solution.py:23
  20.9 48.7 %copy-start.9 = (bf16[2048,128]{1,0:T(8,128)(2,1)}, bf16[2048,128]{1,0:T(8,128)(2,1)S(1)}, u32[]{:S(2)}) copy-start(bf16[2048,128]{1,0:T(8,128)(2,1)S(1)} %collective-permute-done.4.refs_1_) | copy-start | bytes 1572868
  20.9 34.3 %collective-permute-start.10 = (bf16[2048,128]{1,0:T(8,128)(2,1)S(1)}, bf16[2048,128]{1,0:T(8,128)(2,1)}, u32[]{:S(2)}, u32[]{:S(2)}) collective-permute-start(bf16[2048,128]{1,0:T(8,128)(2,1)S(1)} %collective-permute-done.4.refs_1_), channel_id=1, source_target_pairs={{0,1},{1,0},{2,3},{3,2},{4,5},{5,4},{6,7},{7,6},{8,9},{9,8},{10,11... | collective-permute-start | bytes 1572872 | tf_op jit(solution)/shard_map/ppermute | solution.py:23
  23.7 46.0 %copy-start.11 = (bf16[2048,128]{1,0:T(8,128)(2,1)}, bf16[2048,128]{1,0:T(8,128)(2,1)S(1)}, u32[]{:S(2)}) copy-start(bf16[2048,128]{1,0:T(8,128)(2,1)S(1)} %collective-permute-done.2.refs_4_) | copy-start | bytes 1572868
  23.7 32.7 %collective-permute-start.12 = (bf16[2048,128]{1,0:T(8,128)(2,1)S(1)}, bf16[2048,128]{1,0:T(8,128)(2,1)}, u32[]{:S(2)}, u32[]{:S(2)}) collective-permute-start(bf16[2048,128]{1,0:T(8,128)(2,1)S(1)} %collective-permute-done.2.refs_4_), channel_id=1, source_target_pairs={{0,1},{1,0},{2,3},{3,2},{4,5},{5,4},{6,7},{7,6},{8,9},{9,8},{10,11... | collective-permute-start | bytes 1572872 | tf_op jit(solution)/shard_map/ppermute | solution.py:23
  34.6 35.1 %copy-start.15 = (bf16[2048,128]{1,0:T(8,128)(2,1)}, bf16[2048,128]{1,0:T(8,128)(2,1)S(1)}, u32[]{:S(2)}) copy-start(bf16[2048,128]{1,0:T(8,128)(2,1)S(1)} %collective-permute-done.11.refs_5_) | copy-start | bytes 1572868
  34.6 21.9 %collective-permute-start.13 = (bf16[2048,128]{1,0:T(8,128)(2,1)S(1)}, bf16[2048,128]{1,0:T(8,128)(2,1)}, u32[]{:S(2)}, u32[]{:S(2)}) collective-permute-start(bf16[2048,128]{1,0:T(8,128)(2,1)S(1)} %collective-permute-done.11.refs_5_), channel_id=1, source_target_pairs={{0,1},{1,0},{2,3},{3,2},{4,5},{5,4},{6,7},{7,6},{8,9},{9,8},{10,11... | collective-permute-start | bytes 1572872 | tf_op jit(solution)/shard_map/ppermute | solution.py:23
  36.4 20.5 %collective-permute-start.3 = (bf16[2048,128]{1,0:T(8,128)(2,1)S(1)}, bf16[2048,128]{1,0:T(8,128)(2,1)}, u32[]{:S(2)}, u32[]{:S(2)}) collective-permute-start(bf16[2048,128]{1,0:T(8,128)(2,1)S(1)} %collective-permute-done.2.refs_4_), channel_id=1, source_target_pairs={{0,64},{1,65},{2,66},{3,67},{4,68},{5,69},{6,70},{7,71},{8,72},{9,... | collective-permute-start | bytes 1572872 | tf_op jit(solution)/shard_map/ppermute | solution.py:23
  36.5 33.2 %copy-start.17 = (bf16[2048,128]{1,0:T(8,128)(2,1)}, bf16[2048,128]{1,0:T(8,128)(2,1)S(1)}, u32[]{:S(2)}) copy-start(bf16[2048,128]{1,0:T(8,128)(2,1)S(1)} %collective-permute-done.8.refs_0_) | copy-start | bytes 1572868
  36.5 20.6 %collective-permute-start.5 = (bf16[2048,128]{1,0:T(8,128)(2,1)S(1)}, bf16[2048,128]{1,0:T(8,128)(2,1)}, u32[]{:S(2)}, u32[]{:S(2)}) collective-permute-start(bf16[2048,128]{1,0:T(8,128)(2,1)S(1)} %collective-permute-done.4.refs_1_), channel_id=1, source_target_pairs={{0,66},{1,67},{2,64},{3,65},{4,70},{5,71},{6,68},{7,69},{8,74},{9,... | collective-permute-start | bytes 1572872 | tf_op jit(solution)/shard_map/ppermute | solution.py:23
  45.8 22.6 %all-to-all-start = ((f32[128,8,128]{2,1,0:T(8,128)}), f32[128,8,128]{2,1,0:T(8,128)}, u32[]{:S(2)}, u32[]{:S(2)}) async-start(f32[128,8,128]{2,1,0:T(8,128)} %bitcast.14), calls=%async_computation | async-start | bytes 1048576 | tf_op jit(solution)/shard_map/all_to_all | solution.py:262
  55.2 19.9 %collective-permute-start.9 = (bf16[2048,128]{1,0:T(8,128)(2,1)S(1)}, bf16[2048,128]{1,0:T(8,128)(2,1)}, u32[]{:S(2)}, u32[]{:S(2)}) collective-permute-start(bf16[2048,128]{1,0:T(8,128)(2,1)S(1)} %collective-permute-done.8.refs_0_), channel_id=1, source_target_pairs={{0,1},{1,0},{2,3},{3,2},{4,5},{5,4},{6,7},{7,6},{8,9},{9,8},{10,11... | collective-permute-start | bytes 1572872 | tf_op jit(solution)/shard_map/ppermute | solution.py:23
  56.5 44.9 %collective-permute-start = (bf16[2048,128]{1,0:T(8,128)(2,1)S(1)}, bf16[2048,128]{1,0:T(8,128)(2,1)}, u32[]{:S(2)}, u32[]{:S(2)}) collective-permute-start(bf16[2048,128]{1,0:T(8,128)(2,1)S(1)} %get-tuple-element.13.refs_2_), channel_id=1, source_target_pairs={{0,1},{1,0},{2,3},{3,2},{4,5},{5,4},{6,7},{7,6},{8,9},{9,8},{10,11... | collective-permute-start | bytes 1572872 | tf_op jit(solution)/shard_map/ppermute | solution.py:23
  56.6 44.8 %collective-permute-start.1 = (bf16[2048,128]{1,0:T(8,128)(2,1)S(1)}, bf16[2048,128]{1,0:T(8,128)(2,1)}, u32[]{:S(2)}, u32[]{:S(2)}) collective-permute-start(bf16[2048,128]{1,0:T(8,128)(2,1)S(1)} %get-tuple-element.12.refs_3_), channel_id=1, source_target_pairs={{0,1},{1,0},{2,3},{3,2},{4,5},{5,4},{6,7},{7,6},{8,9},{9,8},{10,11... | collective-permute-start | bytes 1572872 | tf_op jit(solution)/shard_map/ppermute | solution.py:23
  57.0 44.4 %collective-permute-start.6 = (bf16[2048,128]{1,0:T(8,128)(2,1)}, bf16[2048,128]{1,0:T(8,128)(2,1)}, u32[]{:S(2)}, u32[]{:S(2)}) collective-permute-start(bf16[2048,128]{1,0:T(8,128)(2,1)} %collective-permute-done.3.refs_6_), channel_id=1, source_target_pairs={{0,1},{1,0},{2,3},{3,2},{4,5},{5,4},{6,7},{7,6},{8,9},{9,8},{10,11... | collective-permute-start | bytes 1572872 | tf_op jit(solution)/shard_map/ppermute | solution.py:23
  57.1 44.3 %collective-permute-start.7 = (bf16[2048,128]{1,0:T(8,128)(2,1)}, bf16[2048,128]{1,0:T(8,128)(2,1)}, u32[]{:S(2)}, u32[]{:S(2)}) collective-permute-start(bf16[2048,128]{1,0:T(8,128)(2,1)} %collective-permute-done.5.refs_7_), channel_id=1, source_target_pairs={{0,1},{1,0},{2,3},{3,2},{4,5},{5,4},{6,7},{7,6},{8,9},{9,8},{10,11... | collective-permute-start | bytes 1572872 | tf_op jit(solution)/shard_map/ppermute | solution.py:23
  70.4 30.9 %all-to-all-start.1 = ((bf16[128,8,128]{2,1,0:T(8,128)(2,1)}), bf16[128,8,128]{2,1,0:T(8,128)(2,1)S(1)}, u32[]{:S(2)}, u32[]{:S(2)}) async-start(bf16[128,8,128]{2,1,0:T(8,128)(2,1)} %broadcast_in_dim.4), calls=%async_computation.1 | async-start | bytes 524288 | tf_op jit(solution)/shard_map/all_to_all | solution.py:264
  79.3 22.1 %copy-start.27 = (f32[2048]{0:T(1024)S(1)}, f32[2048]{0:T(1024)}, u32[]{:S(2)}) copy-start(f32[2048]{0:T(1024)} %param.12) | copy-start | bytes 24580
  79.3 22.1 %copy-start.29 = (s32[8,8]{1,0:T(8,128)S(1)}, s32[8,8]{1,0:T(8,128)}, u32[]{:S(2)}) copy-start(s32[8,8]{1,0:T(8,128)} %refs_1_.3) | copy-start | bytes 772
  79.3 22.1 %copy-start.30 = (f32[128]{0:T(128)S(1)}, f32[128]{0:T(128)}, u32[]{:S(2)}) copy-start(f32[128]{0:T(128)} %param.13) | copy-start | bytes 1540
  120.4 27.1 %copy-start.5 = (f32[2048,128]{1,0:T(8,128)}, f32[2048,128]{1,0:T(8,128)S(1)}, u32[]{:S(2)}) copy-start(f32[2048,128]{1,0:T(8,128)S(1)} %get-tuple-element.7.refs_10_) | copy-start | bytes 3145732
  120.4 29.0 %copy-start.7 = (f32[2048,128]{1,0:T(8,128)}, f32[2048,128]{1,0:T(8,128)S(1)}, u32[]{:S(2)}) copy-start(f32[2048,128]{1,0:T(8,128)S(1)} %get-tuple-element.8.refs_11_) | copy-start | bytes 3145732
  120.4 29.0 %copy-start.25 = (f32[1024,128]{1,0:T(8,128)}, f32[1024,128]{1,0:T(8,128)S(1)}, u32[]{:S(2)}) copy-start(f32[1024,128]{1,0:T(8,128)S(1)} %get-tuple-element.9) | copy-start | bytes 1572868
  120.5 12.5 %collective-permute-start.18 = (bf16[2048,128]{1,0:T(8,128)(2,1)S(1)}, bf16[2048,128]{1,0:T(8,128)(2,1)S(1)}, u32[]{:S(2)}, u32[]{:S(2)}) collective-permute-start(bf16[2048,128]{1,0:T(8,128)(2,1)S(1)} %get-tuple-element.10.refs_3_), channel_id=1, source_target_pairs={{0,64},{1,65},{2,66},{3,67},{4,68},{5,69},{6,70},{7,71},{8,72},{9,... | collective-permute-start | bytes 1572872 | tf_op jit(solution)/shard_map/ppermute | solution.py:23
  122.0 14.5 %collective-permute-start.16 = (bf16[2048,128]{1,0:T(8,128)(2,1)S(1)}, bf16[2048,128]{1,0:T(8,128)(2,1)S(1)}, u32[]{:S(2)}, u32[]{:S(2)}) collective-permute-start(bf16[2048,128]{1,0:T(8,128)(2,1)S(1)} %get-tuple-element.11.refs_2_), channel_id=1, source_target_pairs={{0,66},{1,67},{2,64},{3,65},{4,70},{5,71},{6,68},{7,69},{8,74},{9,... | collective-permute-start | bytes 1572872 | tf_op jit(solution)/shard_map/ppermute | solution.py:23
  123.7 20.5 %collective-permute-start.22 = (bf16[2048,128]{1,0:T(8,128)(2,1)S(1)}, bf16[2048,128]{1,0:T(8,128)(2,1)S(1)}, u32[]{:S(2)}, u32[]{:S(2)}) collective-permute-start(bf16[2048,128]{1,0:T(8,128)(2,1)S(1)} %get-tuple-element.11.refs_2_), channel_id=1, source_target_pairs={{0,64},{1,65},{2,66},{3,67},{4,68},{5,69},{6,70},{7,71},{8,72},{9,... | collective-permute-start | bytes 1572872 | tf_op jit(solution)/shard_map/ppermute | solution.py:23
  124.1 23.5 %collective-permute-start.25 = (bf16[2048,128]{1,0:T(8,128)(2,1)S(1)}, bf16[2048,128]{1,0:T(8,128)(2,1)S(1)}, u32[]{:S(2)}, u32[]{:S(2)}) collective-permute-start(bf16[2048,128]{1,0:T(8,128)(2,1)S(1)} %get-tuple-element.10.refs_3_), channel_id=1, source_target_pairs={{0,66},{1,67},{2,64},{3,65},{4,70},{5,71},{6,68},{7,69},{8,74},{9,... | collective-permute-start | bytes 1572872 | tf_op jit(solution)/shard_map/ppermute | solution.py:23
  133.0 46.8 %copy-start.13 = (bf16[2048,128]{1,0:T(8,128)(2,1)}, bf16[2048,128]{1,0:T(8,128)(2,1)S(1)}, u32[]{:S(2)}) copy-start(bf16[2048,128]{1,0:T(8,128)(2,1)S(1)} %collective-permute-done.18.refs_1_) | copy-start | bytes 1572868
  133.0 25.6 %collective-permute-start.24 = (bf16[2048,128]{1,0:T(8,128)(2,1)S(1)}, bf16[2048,128]{1,0:T(8,128)(2,1)}, u32[]{:S(2)}, u32[]{:S(2)}) collective-permute-start(bf16[2048,128]{1,0:T(8,128)(2,1)S(1)} %collective-permute-done.18.refs_1_), channel_id=1, source_target_pairs={{0,1},{1,0},{2,3},{3,2},{4,5},{5,4},{6,7},{7,6},{8,9},{9,8},{10,11... | collective-permute-start | bytes 1572872 | tf_op jit(solution)/shard_map/ppermute | solution.py:23
  136.5 43.4 %copy-start.19 = (bf16[2048,128]{1,0:T(8,128)(2,1)}, bf16[2048,128]{1,0:T(8,128)(2,1)S(1)}, u32[]{:S(2)}) copy-start(bf16[2048,128]{1,0:T(8,128)(2,1)S(1)} %collective-permute-done.16.refs_4_) | copy-start | bytes 1572868
  136.5 23.4 %collective-permute-start.26 = (bf16[2048,128]{1,0:T(8,128)(2,1)S(1)}, bf16[2048,128]{1,0:T(8,128)(2,1)}, u32[]{:S(2)}, u32[]{:S(2)}) collective-permute-start(bf16[2048,128]{1,0:T(8,128)(2,1)S(1)} %collective-permute-done.16.refs_4_), channel_id=1, source_target_pairs={{0,1},{1,0},{2,3},{3,2},{4,5},{5,4},{6,7},{7,6},{8,9},{9,8},{10,11... | collective-permute-start | bytes 1572872 | tf_op jit(solution)/shard_map/ppermute | solution.py:23
  144.3 35.6 %copy-start.21 = (bf16[2048,128]{1,0:T(8,128)(2,1)}, bf16[2048,128]{1,0:T(8,128)(2,1)S(1)}, u32[]{:S(2)}) copy-start(bf16[2048,128]{1,0:T(8,128)(2,1)S(1)} %collective-permute-done.22.refs_0_) | copy-start | bytes 1572868
  144.3 15.9 %collective-permute-start.23 = (bf16[2048,128]{1,0:T(8,128)(2,1)S(1)}, bf16[2048,128]{1,0:T(8,128)(2,1)}, u32[]{:S(2)}, u32[]{:S(2)}) collective-permute-start(bf16[2048,128]{1,0:T(8,128)(2,1)S(1)} %collective-permute-done.22.refs_0_), channel_id=1, source_target_pairs={{0,1},{1,0},{2,3},{3,2},{4,5},{5,4},{6,7},{7,6},{8,9},{9,8},{10,11... | collective-permute-start | bytes 1572872 | tf_op jit(solution)/shard_map/ppermute | solution.py:23
  146.2 14.2 %collective-permute-start.17 = (bf16[2048,128]{1,0:T(8,128)(2,1)S(1)}, bf16[2048,128]{1,0:T(8,128)(2,1)}, u32[]{:S(2)}, u32[]{:S(2)}) collective-permute-start(bf16[2048,128]{1,0:T(8,128)(2,1)S(1)} %collective-permute-done.16.refs_4_), channel_id=1, source_target_pairs={{0,64},{1,65},{2,66},{3,67},{4,68},{5,69},{6,70},{7,71},{8,72},{9,... | collective-permute-start | bytes 1572872 | tf_op jit(solution)/shard_map/ppermute | solution.py:23
  147.5 32.3 %copy-start.23 = (bf16[2048,128]{1,0:T(8,128)(2,1)}, bf16[2048,128]{1,0:T(8,128)(2,1)S(1)}, u32[]{:S(2)}) copy-start(bf16[2048,128]{1,0:T(8,128)(2,1)S(1)} %collective-permute-done.25.refs_5_) | copy-start | bytes 1572868
  147.5 13.7 %collective-permute-start.19 = (bf16[2048,128]{1,0:T(8,128)(2,1)S(1)}, bf16[2048,128]{1,0:T(8,128)(2,1)}, u32[]{:S(2)}, u32[]{:S(2)}) collective-permute-start(bf16[2048,128]{1,0:T(8,128)(2,1)S(1)} %collective-permute-done.18.refs_1_), channel_id=1, source_target_pairs={{0,66},{1,67},{2,64},{3,65},{4,70},{5,71},{6,68},{7,69},{8,74},{9,... | collective-permute-start | bytes 1572872 | tf_op jit(solution)/shard_map/ppermute | solution.py:23
  149.4 22.5 %all-to-all-start.2 = ((f32[128,8,128]{2,1,0:T(8,128)}), f32[128,8,128]{2,1,0:T(8,128)}, u32[]{:S(2)}, u32[]{:S(2)}) async-start(f32[128,8,128]{2,1,0:T(8,128)} %bitcast.9), calls=%async_computation.2 | async-start | bytes 1048576 | tf_op jit(solution)/shard_map/all_to_all | solution.py:262
  158.6 46.1 %collective-permute-start.14 = (bf16[2048,128]{1,0:T(8,128)(2,1)S(1)}, bf16[2048,128]{1,0:T(8,128)(2,1)}, u32[]{:S(2)}, u32[]{:S(2)}) collective-permute-start(bf16[2048,128]{1,0:T(8,128)(2,1)S(1)} %get-tuple-element.11.refs_2_), channel_id=1, source_target_pairs={{0,1},{1,0},{2,3},{3,2},{4,5},{5,4},{6,7},{7,6},{8,9},{9,8},{10,11... | collective-permute-start | bytes 1572872 | tf_op jit(solution)/shard_map/ppermute | solution.py:23
  159.9 20.0 %collective-permute-start.27 = (bf16[2048,128]{1,0:T(8,128)(2,1)S(1)}, bf16[2048,128]{1,0:T(8,128)(2,1)}, u32[]{:S(2)}, u32[]{:S(2)}) collective-permute-start(bf16[2048,128]{1,0:T(8,128)(2,1)S(1)} %collective-permute-done.25.refs_5_), channel_id=1, source_target_pairs={{0,1},{1,0},{2,3},{3,2},{4,5},{5,4},{6,7},{7,6},{8,9},{9,8},{10,11... | collective-permute-start | bytes 1572872 | tf_op jit(solution)/shard_map/ppermute | solution.py:23
  160.1 44.6 %collective-permute-start.15 = (bf16[2048,128]{1,0:T(8,128)(2,1)S(1)}, bf16[2048,128]{1,0:T(8,128)(2,1)}, u32[]{:S(2)}, u32[]{:S(2)}) collective-permute-start(bf16[2048,128]{1,0:T(8,128)(2,1)S(1)} %get-tuple-element.10.refs_3_), channel_id=1, source_target_pairs={{0,1},{1,0},{2,3},{3,2},{4,5},{5,4},{6,7},{7,6},{8,9},{9,8},{10,11... | collective-permute-start | bytes 1572872 | tf_op jit(solution)/shard_map/ppermute | solution.py:23
  160.4 44.4 %collective-permute-start.20 = (bf16[2048,128]{1,0:T(8,128)(2,1)}, bf16[2048,128]{1,0:T(8,128)(2,1)}, u32[]{:S(2)}, u32[]{:S(2)}) collective-permute-start(bf16[2048,128]{1,0:T(8,128)(2,1)} %collective-permute-done.17.refs_6_), channel_id=1, source_target_pairs={{0,1},{1,0},{2,3},{3,2},{4,5},{5,4},{6,7},{7,6},{8,9},{9,8},{10,11... | collective-permute-start | bytes 1572872 | tf_op jit(solution)/shard_map/ppermute | solution.py:23
  161.3 43.5 %collective-permute-start.21 = (bf16[2048,128]{1,0:T(8,128)(2,1)}, bf16[2048,128]{1,0:T(8,128)(2,1)}, u32[]{:S(2)}, u32[]{:S(2)}) collective-permute-start(bf16[2048,128]{1,0:T(8,128)(2,1)} %collective-permute-done.19.refs_7_), channel_id=1, source_target_pairs={{0,1},{1,0},{2,3},{3,2},{4,5},{5,4},{6,7},{7,6},{8,9},{9,8},{10,11... | collective-permute-start | bytes 1572872 | tf_op jit(solution)/shard_map/ppermute | solution.py:23
  173.8 30.9 %all-to-all-start.3 = ((bf16[128,8,128]{2,1,0:T(8,128)(2,1)}), bf16[128,8,128]{2,1,0:T(8,128)(2,1)S(1)}, u32[]{:S(2)}, u32[]{:S(2)}) async-start(bf16[128,8,128]{2,1,0:T(8,128)(2,1)} %broadcast_in_dim.5), calls=%async_computation.3 | async-start | bytes 524288 | tf_op jit(solution)/shard_map/all_to_all | solution.py:264
  (15 other events, 60.1 us)

commit v2 on v1

v2 whole, which is shorter than its diff:
```python
import jax
import jax.numpy as jnp
from jax import lax
from jax.experimental import pallas as pl
from jax.experimental.pallas import tpu as pltpu
from jax.sharding import PartitionSpec as P


BLK = 256
NV = 128
NBLK = 8
APPS = 2
AXES = ("wide", "narrow")
BF16 = jnp.bfloat16
F32 = jnp.float32
MIB = 1 << 20


VMEM_SPEC = pl.BlockSpec(memory_space=pltpu.VMEM)
SMEM_SPEC = pl.BlockSpec(memory_space=pltpu.SMEM)
ANY_SPEC = pl.BlockSpec(memory_space=pl.ANY)


def toggled(array, mask):
    return lax.ppermute(array, AXES, [(i, i ^ mask) for i in range(lax.axis_size(AXES))])


def interleave(x, y, scratch):
    scratch[pl.ds(0, x.shape[0], stride=2), :] = x
    scratch[pl.ds(1, x.shape[0], stride=2), :] = y
    return scratch[...].astype(BF16)


def in_hbm(*arrays):
    return [pltpu.with_memory_space_constraint(a, pltpu.HBM) for a in arrays]


def block_rows(b, size=BLK):
    return pl.ds(pl.multiple_of(b * size, size), size)


def split_matrix():
    row = lax.broadcasted_iota(jnp.int32, (BLK, BLK), 0)
    col = lax.broadcasted_iota(jnp.int32, (BLK, BLK), 1)
    half = BLK // 2
    hit = (col == 2 * row) | (col == 2 * (row - half) + 1)
    return jnp.where(hit, 1.0, 0.0).astype(F32).astype(BF16)


def split_block(flat, block, out, select):
    base = pl.multiple_of(block * 2 * BLK, 2 * BLK)
    half = BLK // 2
    pair = jnp.concatenate([flat[pl.ds(base, BLK), :], flat[pl.ds(base + BLK, BLK), :]], axis=1)
    parts = jnp.dot(select, pair, preferred_element_type=F32).astype(BF16)
    out[block, 0:half, 0:NV] = parts[0:half, 0:NV]
    out[block, half:BLK, 0:NV] = parts[0:half, NV:]
    out[block, 0:half, NV:] = parts[half:, 0:NV]
    out[block, half:BLK, NV:] = parts[half:, NV:]


def pack_body(x_hbm, y_hbm, low_ref, high_ref, x, y, scratch, sems):
    size = scratch.shape[0] // 2
    parts = x.shape[0] // size
    loads = []
    for p in range(parts):
        for t, (source, target) in enumerate(((x_hbm, x), (y_hbm, y))):
            rows = pl.ds(p * size, size)
            loads.append(pltpu.make_async_copy(source.at[rows], target.at[rows], sems.at[2 * p + t]))
            loads[-1].start()
    for p in range(parts):
        loads[2 * p].wait()
        loads[2 * p + 1].wait()
        rows = pl.ds(p * size, size)
        out, place = (low_ref, p) if p < parts // 2 else (high_ref, p - parts // 2)
        out[pl.ds(place * 2 * size, 2 * size), :] = interleave(x[rows, :], y[rows, :], scratch)


def pack(x, y):
    rows = x.shape[0]
    parts = 4
    return pl.pallas_call(
        pack_body,
        in_specs=[ANY_SPEC, ANY_SPEC],
        out_specs=[VMEM_SPEC, VMEM_SPEC],
        out_shape=[jax.ShapeDtypeStruct((rows, NV), BF16)] * 2,
        scratch_shapes=[
            pltpu.VMEM((rows, NV), F32),
            pltpu.VMEM((rows, NV), F32),
            pltpu.VMEM((2 * rows // parts, NV), F32),
            pltpu.SemaphoreType.DMA((2 * parts,)),
        ],
        compiler_params=pltpu.CompilerParams(vmem_limit_bytes=8 * MIB),
        name="pack",
    )(*in_hbm(x, y))


def add_projection(total, first, x, y, basis):
    value = jnp.dot((x + y).T.astype(BF16), basis, preferred_element_type=F32)

    @pl.when(first)
    def _():
        total[...] = value

    @pl.when(jnp.logical_not(first))
    def _():
        total[...] += value


def store_projection(total, out_ref):
    for r in range(total.shape[1] // NV):
        out_ref[r * NV : (r + 1) * NV, :] = total[:, r * NV : (r + 1) * NV].T.astype(BF16)


def project_body(x_hbm, y_hbm, basis_hbm, out_ref, x, y, basis, total, sems):
    size = BLK
    blocks = x.shape[0] // size
    triples = ((x_hbm, x), (y_hbm, y), (basis_hbm, basis))

    def load(b, t):
        source, target = triples[t]
        rows = block_rows(b)
        return pltpu.make_async_copy(source.at[rows], target.at[rows], sems.at[t, b])

    for b in range(blocks):
        for t in range(3):
            load(b, t).start()

    def step(b, carry):
        for t in range(3):
            load(b, t).wait()
        rows = block_rows(b)
        add_projection(total, b == 0, x[rows, :], y[rows, :], basis[rows, :])
        return carry

    lax.fori_loop(0, blocks, step, 0)
    store_projection(total, out_ref)


def project(x, y, basis):
    rows, rank = basis.shape
    return pl.pallas_call(
        project_body,
        in_specs=[ANY_SPEC] * 3,
        out_specs=VMEM_SPEC,
        out_shape=pltpu.HBM((rank, NV), BF16),
        scratch_shapes=[
            pltpu.VMEM((rows, NV), F32),
            pltpu.VMEM((rows, NV), F32),
            pltpu.VMEM((rows, rank), BF16),
            pltpu.VMEM((NV, rank), F32),
            pltpu.SemaphoreType.DMA((3, rows // BLK)),
        ],
        compiler_params=pltpu.CompilerParams(vmem_limit_bytes=12 * MIB),
        name="project",
    )(*in_hbm(x, y, basis))


def list_product(kernel, columns, list_ref, b):
    left = jnp.concatenate([kernel[b, n] for n in range(NBLK)], axis=1)
    right = jnp.concatenate([columns[list_ref[b, n]] for n in range(NBLK)], axis=0)
    return jnp.dot(left, right, preferred_element_type=F32)


def load_patch(slot_ref, chunks, flat, sems):
    rows = chunks[0].shape[0]
    copies = []
    for k, chunk in enumerate(chunks):
        slot = slot_ref[0] ^ (k // 2)
        start = pl.multiple_of(slot * 2 * rows + (k % 2) * rows, rows)
        copies.append(pltpu.make_async_copy(chunk, flat.at[pl.ds(start, rows)], sems.at[k]))
        copies[-1].start()
    return copies


def gather_body(slot_ref, partner_ref, *refs):
    chunks = refs[:8]
    columns_ref, source, gathered, sems = refs[8:]
    for copy in load_patch(slot_ref, chunks, source.reshape(2 * source.shape[0], NV), sems):
        copy.wait()
    unroll = 64

    def gather(step, carry):
        base = step * unroll
        for u in range(unroll):
            gathered[base + u] = source[partner_ref[0, base + u]]
        return carry

    lax.fori_loop(0, source.shape[0] // unroll, gather, 0)
    select = split_matrix()
    flat_out = gathered.reshape(2 * gathered.shape[0], NV)

    def split(block, carry):
        split_block(flat_out, block, columns_ref, select)
        return carry

    lax.fori_loop(0, columns_ref.shape[0], split, 0, unroll=8)


def mirror_columns(slot, partner, chunks):
    patch = partner.shape[1]
    return pl.pallas_call(
        gather_body,
        in_specs=[SMEM_SPEC] * 2 + [ANY_SPEC] * 8,
        out_specs=VMEM_SPEC,
        out_shape=jax.ShapeDtypeStruct((patch // BLK, BLK, 2 * NV), BF16),
        scratch_shapes=[
            pltpu.VMEM((patch, 2, NV), BF16),
            pltpu.VMEM((patch, 2, NV), BF16),
            pltpu.SemaphoreType.DMA((8,)),
        ],
        compiler_params=pltpu.CompilerParams(vmem_limit_bytes=16 * MIB),
        name="mirror_columns",
    )(slot, partner, *in_hbm(*chunks))


def product_body(list_ref, columns_ref, kernel_hbm, out_ref, kernel, sems):
    blocks = kernel.shape[0]

    def load(b):
        return pltpu.make_async_copy(kernel_hbm.at[b], kernel.at[b], sems.at[b])

    for b in range(blocks):
        load(b).start()

    def step(b, carry):
        load(b).wait()
        out_ref[b] = list_product(kernel, columns_ref, list_ref, b)
        return carry

    lax.fori_loop(0, blocks, step, 0)


def mirror_product(indices, columns, kernel):
    blocks = kernel.shape[0]
    return pl.pallas_call(
        product_body,
        in_specs=[SMEM_SPEC, VMEM_SPEC, ANY_SPEC],
        out_specs=VMEM_SPEC,
        out_shape=jax.ShapeDtypeStruct((blocks, BLK, 2 * NV), F32),
        scratch_shapes=[pltpu.VMEM(kernel.shape, BF16), pltpu.SemaphoreType.DMA((blocks,))],
        compiler_params=pltpu.CompilerParams(vmem_limit_bytes=16 * MIB),
        name="mirror_product",
    )(indices, columns, *in_hbm(kernel))


def column_of(row):
    return jnp.broadcast_to(row, (NV, NV)).T


def finish_body(last, slot_ref, list_ref, *refs):
    chunks = refs[:8]
    x_hbm, y_hbm, energy_ref, shift_ref, kernel_hbm, basis_hbm, weight_ref, mirror_ref = refs[8:16]
    rest = refs[16:]
    if last:
        next_x_hbm, next_y_hbm = rest[:2]
        flat, columns, kernel, basis, x, y, chunk_sems, sems = rest[2:]
    else:
        next_x_hbm, next_y_hbm, low_ref, high_ref, project_ref = rest[:5]
        flat, columns, kernel, basis, x, y, chunk_sems, sems, scratch, total = rest[5:]
    blocks = kernel.shape[0]
    copies = load_patch(slot_ref, chunks, flat, chunk_sems)

    def load(b, t):
        if t == 0:
            return pltpu.make_async_copy(kernel_hbm.at[b], kernel.at[b], sems.at[0, b])
        source, target = ((basis_hbm, basis), (x_hbm, x), (y_hbm, y))[t - 1]
        part = block_rows(b)
        return pltpu.make_async_copy(source.at[part], target.at[part], sems.at[t, b])

    def save(b, t):
        source, target = ((x, next_x_hbm), (y, next_y_hbm))[t]
        part = block_rows(b)
        return pltpu.make_async_copy(source.at[part], target.at[part], sems.at[2 + t, b])

    for b in range(blocks):
        for t in range(4):
            load(b, t).start()
    for copy in copies:
        copy.wait()
    select = split_matrix()

    def split(block, carry):
        split_block(flat, block, columns, select)
        return carry

    lax.fori_loop(0, columns.shape[0], split, 0, unroll=8)
    shifts = shift_ref[...]
    half = BLK // 2

    def step(b, carry):
        for t in range(4):
            load(b, t).wait()
        part = block_rows(b)
        mirrored = mirror_ref[b]
        exchange = jnp.dot(basis[part, :], weight_ref[...], preferred_element_type=F32)
        direct = list_product(kernel, columns, list_ref, b)
        row = energy_ref[b]
        levels = jnp.concatenate([column_of(row[:, 0:half]), column_of(row[:, half:])], axis=0)
        next_x = x[part, :] + (direct[:, :NV] + mirrored[:, NV:] + exchange) / (levels - shifts)
        next_y = y[part, :] + (direct[:, NV:] + mirrored[:, :NV] + exchange) / (levels + shifts)
        x[part, :] = next_x
        y[part, :] = next_y
        for t in range(2):
            save(b, t).start()
        if not last:
            mixed = interleave(next_x, next_y, scratch)
            place = pl.ds(pl.multiple_of((b % (blocks // 2)) * 2 * BLK, 2 * BLK), 2 * BLK)

            @pl.when(b < blocks // 2)
            def _():
                low_ref[place, :] = mixed

            @pl.when(b >= blocks // 2)
            def _():
                high_ref[place, :] = mixed

            add_projection(total, b == 0, next_x, next_y, basis[part, :])
        return carry

    lax.fori_loop(0, blocks, step, 0)
    if not last:
        store_projection(total, project_ref)
    for b in range(blocks):
        for t in range(2):
            save(b, t).wait()


def finish(last, slot, indices, chunks, x, y, energy, shift, kernel, basis, weights, mirrored):
    rows, rank = basis.shape
    blocks = kernel.shape[0]
    patch = 4 * rows
    out_specs = [ANY_SPEC, ANY_SPEC]
    out_shape = [pltpu.HBM((rows, NV), F32)] * 2
    scratch = [
        pltpu.VMEM((2 * patch, NV), BF16),
        pltpu.VMEM((patch // BLK, BLK, 2 * NV), BF16),
        pltpu.VMEM(kernel.shape, BF16),
        pltpu.VMEM(basis.shape, BF16),
        pltpu.VMEM((rows, NV), F32),
        pltpu.VMEM((rows, NV), F32),
        pltpu.SemaphoreType.DMA((8,)),
        pltpu.SemaphoreType.DMA((4, blocks)),
    ]
    if not last:
        out_specs += [VMEM_SPEC] * 3
        out_shape += [jax.ShapeDtypeStruct((rows, NV), BF16)] * 2 + [pltpu.HBM((rank, NV), BF16)]
        scratch += [pltpu.VMEM((2 * BLK, NV), F32), pltpu.VMEM((NV, rank), F32)]

    def body(*refs):
        finish_body(last, *refs)

    return pl.pallas_call(
        body,
        in_specs=[SMEM_SPEC] * 2 + [ANY_SPEC] * 10 + [VMEM_SPEC] * 2 + [ANY_SPEC] * 2 + [VMEM_SPEC] * 2,
        out_specs=out_specs,
        out_shape=out_shape,
        scratch_shapes=scratch,
        compiler_params=pltpu.CompilerParams(vmem_limit_bytes=32 * MIB),
        name="finish_last" if last else "finish",
    )(slot, indices, *in_hbm(*chunks, x, y), energy, shift, *in_hbm(kernel, basis), weights, mirrored)


def total_weights(partial):
    size = lax.axis_size(AXES)
    rank, vectors = partial.shape
    part = rank // size
    pieces = lax.all_to_all(partial.reshape(size, part, vectors), AXES, 0, 0, tiled=True)
    own = jnp.sum(pieces.astype(F32), axis=0).astype(BF16)
    spread = lax.all_to_all(jnp.broadcast_to(own[None], (size, part, vectors)), AXES, 0, 0, tiled=True)
    return spread.reshape(rank, vectors)


def on_device(x, y, energy, shift, res_kernel, res_list, cp_kernel, cp_list, partner, basis):
    size = lax.axis_size(AXES)
    narrow = lax.axis_size("narrow")
    near = size // 2
    far = near | (narrow // 2)
    slot = lax.axis_index("narrow").astype(jnp.int32).reshape(1)
    blocks = res_kernel.shape[0]
    levels = energy.reshape(blocks, 1, BLK)
    shifts = shift.reshape(1, NV)
    for app in range(APPS):
        last = app == APPS - 1
        if app == 0:
            low, high = pack(x, y)
            partial = project(x, y, basis)
        far_low = toggled(low, far)
        near_high = toggled(high, near)
        far_high = toggled(high, far)
        near_low = toggled(low, near)
        own = [toggled(low, 1), toggled(high, 1)]
        across = [toggled(far_low, near), toggled(near_high, far)]
        mirror_chunks = [near_low, near_high]
        mirror_chunks += [toggled(c, 1) for c in mirror_chunks]
        mirror_chunks += [far_low, far_high]
        mirror_chunks += [toggled(c, 1) for c in mirror_chunks[4:]]
        own_chunks = [low, high] + own + across + [toggled(c, 1) for c in across]
        weights = total_weights(partial)
        mirror = mirror_columns(slot, partner, mirror_chunks)
        mirrored = mirror_product(cp_list, mirror, cp_kernel)
        out = finish(
            last, slot, res_list, own_chunks, x, y, levels, shifts, res_kernel, basis, weights, mirrored
        )
        if last:
            return tuple(out)
        x, y, low, high, partial = out


def solution(mesh):
    return jax.shard_map(
        on_device,
        mesh=mesh,
        in_specs=(
            P(AXES, None),
            P(AXES, None),
            P(AXES),
            P(),
            P(AXES, None, None, None),
            P(AXES, None),
            P(AXES, None, None, None),
            P(AXES, None),
            P("wide", None),
            P(AXES, None),
        ),
        out_specs=(P(AXES, None), P(AXES, None)),
        check_vma=False,
    )
```

time: 226 us -> 217 us (0.960)
  blocking collectives: 0 us -> 39.6 us
  starting transfers between devices: 68 us -> 45.8 us
  local copies, waits for them, and re-layouts: 18.8 us -> 1.59 us
  Pallas kernels: 86.8 us -> 77.6 us
  waiting for transfers between devices: 47.5 us -> 50.5 us
    all_to_all x0 -> x2, blocking collectives: none -> 39.6 us  [total_weights(): lax.all_to_all(partial.reshape(size, part, vectors), AXES, 0, 0, tiled=True)]
    ppermute x28, waiting for transfers between devices: 31.2 us -> 50.5 us  [toggled(): lax.ppermute(array, AXES, [(i, i ^ mask) for i in range(lax.axis_size(AXE...]
    all_to_all x2 -> x0, starting transfers between devices: 18.6 us -> none  [total_weights(): lax.all_to_all(partial.reshape(size, part, vectors), AXES, 0, 0, tiled=True)]
    all_to_all x2 -> x0, waiting for transfers between devices: 16.3 us -> none  [total_weights(): lax.all_to_all(partial.reshape(size, part, vectors), AXES, 0, 0, tiled=True)]
    unnamed x62 -> x42, local copies, waits for them, and re-layouts: 15.9 us -> 0.1 us
    pallas_call x6 -> x8, Pallas kernels: 86.8 us -> 77.6 us  [the longest x2 33.1 us: finish(): pl.pallas_call(body, in_specs=[SMEM_SPEC] * 2 + [ANY_SPEC] * 10 + [VMEM_S...]
  transfers between devices with their start and end apart: 32 -> 30, of which waited for: 7 -> 8; matrix products, arithmetic and copies ran while one was open for 2% -> 1% of each run, Pallas kernels for 22% -> 20%
where the time goes in v2:
time: 217 us
  Pallas kernels  77.6 us (36%)
  waiting for transfers between devices  50.5 us (23%)
  starting transfers between devices  45.8 us (21%)
  blocking collectives  39.6 us (18%)
    ppermute x28, waiting for transfers between devices, toggled(): lax.ppermute(array, AXES, [(i, i ^ mask) for i in range(lax.axis_size(AXE...  50.5 us
    all_to_all x2, blocking collectives, total_weights(): lax.all_to_all(partial.reshape(size, part, vectors), AXES, 0, 0, tiled=True)  39.6 us
    ppermute x28, starting transfers between devices, toggled(): lax.ppermute(array, AXES, [(i, i ^ mask) for i in range(lax.axis_size(AXE...  36.8 us
    pallas_call x2, Pallas kernels, finish(): pl.pallas_call(body, in_specs=[SMEM_SPEC] * 2 + [ANY_SPEC] * 10 + [VMEM_S...  33.1 us
    pallas_call x2, Pallas kernels, mirror_columns(): pl.pallas_call(gather_body, in_specs=[SMEM_SPEC] * 2 + [ANY_SPEC] * 8, ou...  27 us
    pallas_call x2, Pallas kernels, mirror_product(): pl.pallas_call(product_body, in_specs=[SMEM_SPEC, VMEM_SPEC, ANY_SPEC], o...  11 us
    all_to_all x2, starting transfers between devices, total_weights(): lax.all_to_all(jnp.broadcast_to(own[None], (size, part, vectors)), AXES,...  8.97 us
    pallas_call x1, Pallas kernels, project(): pl.pallas_call(project_body, in_specs=[ANY_SPEC] * 3, out_specs=VMEM_SPEC...  4.84 us
  transfers between devices with their start and end apart: 30, of which 8 were waited for; matrix products, arithmetic and copies ran while one was open for 1% of the time, Pallas kernels for 20%

profile of v2, /device:TPU:1, one launch (start us, length us, event | category | flops | bytes accessed | tf_op | source)
XLA Modules:
  0.0 216.5 jit_solution(16430449658315540657)
XLA Ops:
  0.6 1.6 pack.1
  2.3 2.2 %collective-permute-start.4 = (bf16[2048,128]{1,0:T(8,128)(2,1)S(1)}, bf16[2048,128]{1,0:T(8,128)(2,1)S(1)}, u32[]{:S(2)}, u32[]{:S(2)}) collective-permute-start(bf16[2048,128]{1,0:T(8,128)(2,1)S(1)} %get-tuple-element.10.refs_3_), channel_id=1, source_target_pairs={{0,64},{1,65},{2,66},{3,67},{4,68},{5,69},{6,70},{7,71},{8,72},{9,... | collective-permute-start | bytes 1572872 | tf_op jit(solution)/shard_map/ppermute | solution.py:25
  4.5 1.9 collective-permute-start.2
  6.4 0.8 collective-permute-start.11
  7.2 8.6 %collective-permute-done.4.refs_1_ = bf16[2048,128]{1,0:T(8,128)(2,1)S(1)} collective-permute-done((bf16[2048,128]{1,0:T(8,128)(2,1)S(1)}, bf16[2048,128]{1,0:T(8,128)(2,1)S(1)}, u32[]{:S(2)}, u32[]{:S(2)}) %collective-permute-start.4) | collective-permute-done | bytes 524320 | tf_op jit(solution)/shard_map/ppermute | solution.py:25
  15.8 2.8 %collective-permute-start.10 = (bf16[2048,128]{1,0:T(8,128)(2,1)S(1)}, bf16[2048,128]{1,0:T(8,128)(2,1)S(1)}, u32[]{:S(2)}, u32[]{:S(2)}) collective-permute-start(bf16[2048,128]{1,0:T(8,128)(2,1)S(1)} %collective-permute-done.4.refs_1_), channel_id=1, source_target_pairs={{0,1},{1,0},{2,3},{3,2},{4,5},{5,4},{6,7},{7,6},{8,9},{9,8},{10,11... | collective-permute-start | bytes 1572872 | tf_op jit(solution)/shard_map/ppermute | solution.py:25
  18.6 2.9 %collective-permute-start.12 = (bf16[2048,128]{1,0:T(8,128)(2,1)S(1)}, bf16[2048,128]{1,0:T(8,128)(2,1)S(1)}, u32[]{:S(2)}, u32[]{:S(2)}) collective-permute-start(bf16[2048,128]{1,0:T(8,128)(2,1)S(1)} %collective-permute-done.2.refs_4_), channel_id=1, source_target_pairs={{0,1},{1,0},{2,3},{3,2},{4,5},{5,4},{6,7},{7,6},{8,9},{9,8},{10,11... | collective-permute-start | bytes 1572872 | tf_op jit(solution)/shard_map/ppermute | solution.py:25
  21.5 8.0 %collective-permute-done.11.refs_5_ = bf16[2048,128]{1,0:T(8,128)(2,1)S(1)} collective-permute-done((bf16[2048,128]{1,0:T(8,128)(2,1)S(1)}, bf16[2048,128]{1,0:T(8,128)(2,1)S(1)}, u32[]{:S(2)}, u32[]{:S(2)}) %collective-permute-start.11) | collective-permute-done | bytes 524320 | tf_op jit(solution)/shard_map/ppermute | solution.py:25
  29.5 1.8 collective-permute-start.13
  31.3 1.9 collective-permute-start.5
  33.2 0.4 collective-permute-start.9
  33.6 0.1 collective-permute-start
  33.7 0.4 collective-permute-start.1
  34.1 10.8 %collective-permute-done.3.refs_6_ = bf16[2048,128]{1,0:T(8,128)(2,1)} collective-permute-done((bf16[2048,128]{1,0:T(8,128)(2,1)S(1)}, bf16[2048,128]{1,0:T(8,128)(2,1)}, u32[]{:S(2)}, u32[]{:S(2)}) %collective-permute-start.3) | collective-permute-done | bytes 524320 | tf_op jit(solution)/shard_map/ppermute | solution.py:25
  44.9 0.9 collective-permute-start.6
  45.7 0.3 collective-permute-done.5.refs_7_
  46.0 0.9 collective-permute-start.7
  47.0 4.8 %project.1 = bf16[1024,128]{1,0:T(8,128)(2,1)} custom-call(f32[2048,128]{1,0:T(8,128)} %refs_10_.1, f32[2048,128]{1,0:T(8,128)} %refs_11_.1, bf16[2048,1024]{1,0:T(8,128)(2,1)} %refs_15_.3), custom_call_target="tpu_custom_call" | custom-call | tf_op jit(solution)/shard_map/project/pallas_call | solution.py:141
  51.8 20.1 %all_to_all.20 = bf16[128,8,128]{2,1,0:T(8,128)(2,1)S(1)} all-to-all(bf16[128,8,128]{2,1,0:T(8,128)(2,1)} %bitcast.13), channel_id=1, replica_groups=mesh['wide'=32,'narrow'=4] {'wide','narrow'}, dimensions={0} | all-to-all | bytes 524288 | tf_op jit(solution)/shard_map/all_to_all | solution.py:367
  72.1 0.8 broadcast_in_dim.4
  72.9 4.5 %all-to-all-start.1 = ((bf16[128,8,128]{2,1,0:T(8,128)(2,1)}), bf16[128,8,128]{2,1,0:T(8,128)(2,1)S(1)}, u32[]{:S(2)}, u32[]{:S(2)}) async-start(bf16[128,8,128]{2,1,0:T(8,128)(2,1)} %broadcast_in_dim.4), calls=%async_computation.1 | async-start | bytes 524288 | tf_op jit(solution)/shard_map/all_to_all | solution.py:369
  77.4 13.5 %mirror_columns.2.columns_ref = bf16[32,256,256]{2,1,0:T(8,128)(2,1)S(1)} custom-call(s32[1]{0:T(128)} %bitcast.slot_ref.refs_0_, s32[1,8192]{1,0:T(1,128)S(1)} %copy-done.4, bf16[2048,128]{1,0:T(8,128)(2,1)} %collective-permute-done.8.refs_0_, bf16[2048,128]{1,0:T(8,128)(2,1)} %copy-done.9, bf16[2048,128]{1,0:T(8,128)(2,1)} %collective-permute-done.9.refs_2_, ...), custom_call_target="tpu_custom_call" | custom-call | tf_op jit(solution)/shard_map/mirror_columns/pallas_call | solution.py:201
  91.0 5.5 %mirror_product.2.refs_17_ = f32[8,256,256]{2,1,0:T(8,128)S(1)} custom-call(s32[8,8]{1,0:T(8,128)S(1)} %copy-done.6, bf16[32,256,256]{2,1,0:T(8,128)(2,1)S(1)} %mirror_columns.2.columns_ref, bf16[8,8,256,256]{3,2,1,0:T(8,128)(2,1)} %kernel_hbm.3), custom_call_target="tpu_custom_call" | custom-call | tf_op jit(solution)/shard_map/mirror_product/pallas_call | solution.py:235
  96.6 18.7 %finish.1 = (f32[2048,128]{1,0:T(8,128)}, f32[2048,128]{1,0:T(8,128)}, bf16[2048,128]{1,0:T(8,128)(2,1)S(1)}, bf16[2048,128]{1,0:T(8,128)(2,1)S(1)}, bf16[1024,128]{1,0:T(8,128)(2,1)}) custom-call(s32[1]{0:T(128)} %bitcast.slot_ref.refs_0_, s32[8,8]{1,0:T(8,128)S(1)} %copy-done.7, bf16[2048,128]{1,0:T(8,128)(2,1)} %copy-done.2, bf16[2048,128]{1,0:T(8,128)(2,1)} %copy-done.3, ...), custom_call_target="tpu_custom_call" | custom-call | tf_op jit(solution)/shard_map/finish/pallas_call | solution.py:352
  115.3 1.4 collective-permute-start.18
  116.7 1.8 collective-permute-start.16
  118.5 0.3 collective-permute-start.22
  118.8 0.6 collective-permute-start.25
  119.4 8.3 %collective-permute-done.18.refs_1_ = bf16[2048,128]{1,0:T(8,128)(2,1)S(1)} collective-permute-done((bf16[2048,128]{1,0:T(8,128)(2,1)S(1)}, bf16[2048,128]{1,0:T(8,128)(2,1)S(1)}, u32[]{:S(2)}, u32[]{:S(2)}) %collective-permute-start.18) | collective-permute-done | bytes 524320 | tf_op jit(solution)/shard_map/ppermute | solution.py:25
  127.8 3.4 %collective-permute-start.24 = (bf16[2048,128]{1,0:T(8,128)(2,1)S(1)}, bf16[2048,128]{1,0:T(8,128)(2,1)S(1)}, u32[]{:S(2)}, u32[]{:S(2)}) collective-permute-start(bf16[2048,128]{1,0:T(8,128)(2,1)S(1)} %collective-permute-done.18.refs_1_), channel_id=1, source_target_pairs={{0,1},{1,0},{2,3},{3,2},{4,5},{5,4},{6,7},{7,6},{8,9},{9,8},{10,11... | collective-permute-start | bytes 1572872 | tf_op jit(solution)/shard_map/ppermute | solution.py:25
  131.2 2.2 %collective-permute-start.26 = (bf16[2048,128]{1,0:T(8,128)(2,1)S(1)}, bf16[2048,128]{1,0:T(8,128)(2,1)S(1)}, u32[]{:S(2)}, u32[]{:S(2)}) collective-permute-start(bf16[2048,128]{1,0:T(8,128)(2,1)S(1)} %collective-permute-done.16.refs_4_), channel_id=1, source_target_pairs={{0,1},{1,0},{2,3},{3,2},{4,5},{5,4},{6,7},{7,6},{8,9},{9,8},{10,11... | collective-permute-start | bytes 1572872 | tf_op jit(solution)/shard_map/ppermute | solution.py:25
  133.4 5.7 %collective-permute-done.22.refs_0_ = bf16[2048,128]{1,0:T(8,128)(2,1)S(1)} collective-permute-done((bf16[2048,128]{1,0:T(8,128)(2,1)S(1)}, bf16[2048,128]{1,0:T(8,128)(2,1)S(1)}, u32[]{:S(2)}, u32[]{:S(2)}) %collective-permute-start.22) | collective-permute-done | bytes 524320 | tf_op jit(solution)/shard_map/ppermute | solution.py:25
  139.1 1.8 collective-permute-start.23
  140.9 1.4 collective-permute-start.17
  142.3 1.8 collective-permute-start.19
  144.1 1.6 collective-permute-start.27
  145.7 0.3 collective-permute-start.14
  146.0 0.2 collective-permute-start.15
  146.2 8.3 %collective-permute-done.17.refs_6_ = bf16[2048,128]{1,0:T(8,128)(2,1)} collective-permute-done((bf16[2048,128]{1,0:T(8,128)(2,1)S(1)}, bf16[2048,128]{1,0:T(8,128)(2,1)}, u32[]{:S(2)}, u32[]{:S(2)}) %collective-permute-start.17) | collective-permute-done | bytes 524320 | tf_op jit(solution)/shard_map/ppermute | solution.py:25
  154.5 0.9 collective-permute-start.20
  155.4 0.4 collective-permute-done.19.refs_7_
  155.8 2.2 %collective-permute-start.21 = (bf16[2048,128]{1,0:T(8,128)(2,1)}, bf16[2048,128]{1,0:T(8,128)(2,1)}, u32[]{:S(2)}, u32[]{:S(2)}) collective-permute-start(bf16[2048,128]{1,0:T(8,128)(2,1)} %collective-permute-done.19.refs_7_), channel_id=1, source_target_pairs={{0,1},{1,0},{2,3},{3,2},{4,5},{5,4},{6,7},{7,6},{8,9},{9,8},{10,11... | collective-permute-start | bytes 1572872 | tf_op jit(solution)/shard_map/ppermute | solution.py:25
  158.0 19.4 %all_to_all.21 = bf16[128,8,128]{2,1,0:T(8,128)(2,1)S(1)} all-to-all(bf16[128,8,128]{2,1,0:T(8,128)(2,1)} %bitcast.14), channel_id=1, replica_groups=mesh['wide'=32,'narrow'=4] {'wide','narrow'}, dimensions={0} | all-to-all | bytes 524288 | tf_op jit(solution)/shard_map/all_to_all | solution.py:367
  177.5 0.7 broadcast_in_dim.5
  178.3 4.5 %all-to-all-start.3 = ((bf16[128,8,128]{2,1,0:T(8,128)(2,1)}), bf16[128,8,128]{2,1,0:T(8,128)(2,1)S(1)}, u32[]{:S(2)}, u32[]{:S(2)}) async-start(bf16[128,8,128]{2,1,0:T(8,128)(2,1)} %broadcast_in_dim.5), calls=%async_computation.3 | async-start | bytes 524288 | tf_op jit(solution)/shard_map/all_to_all | solution.py:369
  182.8 13.5 %mirror_columns.3.columns_ref = bf16[32,256,256]{2,1,0:T(8,128)(2,1)S(1)} custom-call(s32[1]{0:T(128)} %bitcast.slot_ref.refs_0_, s32[1,8192]{1,0:T(1,128)S(1)} %copy-done.4, bf16[2048,128]{1,0:T(8,128)(2,1)} %copy-done.14, bf16[2048,128]{1,0:T(8,128)(2,1)} %copy-done.12, bf16[2048,128]{1,0:T(8,128)(2,1)} %copy-done.20, bf16[2048,128]{1,0:T(8,128)(2,1)} %copy-done.17, ...), custom_call_target="tpu_custom_call" | custom-call | tf_op jit(solution)/shard_map/mirror_columns/pallas_call | solution.py:201
  196.4 5.5 %mirror_product.3.refs_17_ = f32[8,256,256]{2,1,0:T(8,128)S(1)} custom-call(s32[8,8]{1,0:T(8,128)S(1)} %copy-done.6, bf16[32,256,256]{2,1,0:T(8,128)(2,1)S(1)} %mirror_columns.3.columns_ref, bf16[8,8,256,256]{3,2,1,0:T(8,128)(2,1)} %kernel_hbm.3), custom_call_target="tpu_custom_call" | custom-call | tf_op jit(solution)/shard_map/mirror_product/pallas_call | solution.py:235
  201.9 14.4 %finish_last.1 = (f32[2048,128]{1,0:T(8,128)}, f32[2048,128]{1,0:T(8,128)}) custom-call(s32[1]{0:T(128)} %bitcast.slot_ref.refs_0_, s32[8,8]{1,0:T(8,128)S(1)} %copy-done.7, bf16[2048,128]{1,0:T(8,128)(2,1)} %copy-done, bf16[2048,128]{1,0:T(8,128)(2,1)} %copy-done.1, bf16[2048,128]{1,0:T(8,128)(2,1)} %collective-permute-done.14.refs_4_, ...), custom_call_target="tpu_custom_call" | custom-call | tf_op jit(solution)/shard_map/finish_last/pallas_call | solution.py:352
  (68 shorter events, 0.4 us)
Async XLA Ops:
  2.3 88.7 %copy-start.2 = (bf16[2048,128]{1,0:T(8,128)(2,1)}, bf16[2048,128]{1,0:T(8,128)(2,1)S(1)}, u32[]{:S(2)}) copy-start(bf16[2048,128]{1,0:T(8,128)(2,1)S(1)} %get-tuple-element.9.refs_2_) | copy-start | bytes 1572868
  2.3 88.6 %copy-start.3 = (bf16[2048,128]{1,0:T(8,128)(2,1)}, bf16[2048,128]{1,0:T(8,128)(2,1)S(1)}, u32[]{:S(2)}) copy-start(bf16[2048,128]{1,0:T(8,128)(2,1)S(1)} %get-tuple-element.10.refs_3_) | copy-start | bytes 1572868
  2.3 75.1 %copy-start.4 = (s32[1,8192]{1,0:T(1,128)S(1)}, s32[1,8192]{1,0:T(1,128)}, u32[]{:S(2)}) copy-start(s32[1,8192]{1,0:T(1,128)} %partner_ref.3) | copy-start | bytes 98308
  2.3 13.5 %collective-permute-start.4 = (bf16[2048,128]{1,0:T(8,128)(2,1)S(1)}, bf16[2048,128]{1,0:T(8,128)(2,1)S(1)}, u32[]{:S(2)}, u32[]{:S(2)}) collective-permute-start(bf16[2048,128]{1,0:T(8,128)(2,1)S(1)} %get-tuple-element.10.refs_3_), channel_id=1, source_target_pairs={{0,64},{1,65},{2,66},{3,67},{4,68},{5,69},{6,70},{7,71},{8,72},{9,... | collective-permute-start | bytes 1572872 | tf_op jit(solution)/shard_map/ppermute | solution.py:25
  4.5 14.1 %collective-permute-start.2 = (bf16[2048,128]{1,0:T(8,128)(2,1)S(1)}, bf16[2048,128]{1,0:T(8,128)(2,1)S(1)}, u32[]{:S(2)}, u32[]{:S(2)}) collective-permute-start(bf16[2048,128]{1,0:T(8,128)(2,1)S(1)} %get-tuple-element.9.refs_2_), channel_id=1, source_target_pairs={{0,66},{1,67},{2,64},{3,65},{4,70},{5,71},{6,68},{7,69},{8,74},{9,... | collective-permute-start | bytes 1572872 | tf_op jit(solution)/shard_map/ppermute | solution.py:25
  6.4 23.1 %collective-permute-start.11 = (bf16[2048,128]{1,0:T(8,128)(2,1)S(1)}, bf16[2048,128]{1,0:T(8,128)(2,1)S(1)}, u32[]{:S(2)}, u32[]{:S(2)}) collective-permute-start(bf16[2048,128]{1,0:T(8,128)(2,1)S(1)} %get-tuple-element.10.refs_3_), channel_id=1, source_target_pairs={{0,66},{1,67},{2,64},{3,65},{4,70},{5,71},{6,68},{7,69},{8,74},{9,... | collective-permute-start | bytes 1572872 | tf_op jit(solution)/shard_map/ppermute | solution.py:25
  7.2 24.1 %collective-permute-start.8 = (bf16[2048,128]{1,0:T(8,128)(2,1)S(1)}, bf16[2048,128]{1,0:T(8,128)(2,1)}, u32[]{:S(2)}, u32[]{:S(2)}) collective-permute-start(bf16[2048,128]{1,0:T(8,128)(2,1)S(1)} %get-tuple-element.9.refs_2_), channel_id=1, source_target_pairs={{0,64},{1,65},{2,66},{3,67},{4,68},{5,69},{6,70},{7,71},{8,72},{9,... | collective-permute-start | bytes 1572872 | tf_op jit(solution)/shard_map/ppermute | solution.py:25
  15.8 61.6 %copy-start.9 = (bf16[2048,128]{1,0:T(8,128)(2,1)}, bf16[2048,128]{1,0:T(8,128)(2,1)S(1)}, u32[]{:S(2)}) copy-start(bf16[2048,128]{1,0:T(8,128)(2,1)S(1)} %collective-permute-done.4.refs_1_) | copy-start | bytes 1572868
  15.8 17.4 %collective-permute-start.10 = (bf16[2048,128]{1,0:T(8,128)(2,1)S(1)}, bf16[2048,128]{1,0:T(8,128)(2,1)S(1)}, u32[]{:S(2)}, u32[]{:S(2)}) collective-permute-start(bf16[2048,128]{1,0:T(8,128)(2,1)S(1)} %collective-permute-done.4.refs_1_), channel_id=1, source_target_pairs={{0,1},{1,0},{2,3},{3,2},{4,5},{5,4},{6,7},{7,6},{8,9},{9,8},{10,11... | collective-permute-start | bytes 1572872 | tf_op jit(solution)/shard_map/ppermute | solution.py:25
  18.6 58.8 %copy-start.10 = (bf16[2048,128]{1,0:T(8,128)(2,1)}, bf16[2048,128]{1,0:T(8,128)(2,1)S(1)}, u32[]{:S(2)}) copy-start(bf16[2048,128]{1,0:T(8,128)(2,1)S(1)} %collective-permute-done.2.refs_4_) | copy-start | bytes 1572868
  18.6 15.0 %collective-permute-start.12 = (bf16[2048,128]{1,0:T(8,128)(2,1)S(1)}, bf16[2048,128]{1,0:T(8,128)(2,1)S(1)}, u32[]{:S(2)}, u32[]{:S(2)}) collective-permute-start(bf16[2048,128]{1,0:T(8,128)(2,1)S(1)} %collective-permute-done.2.refs_4_), channel_id=1, source_target_pairs={{0,1},{1,0},{2,3},{3,2},{4,5},{5,4},{6,7},{7,6},{8,9},{9,8},{10,11... | collective-permute-start | bytes 1572872 | tf_op jit(solution)/shard_map/ppermute | solution.py:25
  29.5 47.9 %copy-start.11 = (bf16[2048,128]{1,0:T(8,128)(2,1)}, bf16[2048,128]{1,0:T(8,128)(2,1)S(1)}, u32[]{:S(2)}) copy-start(bf16[2048,128]{1,0:T(8,128)(2,1)S(1)} %collective-permute-done.11.refs_5_) | copy-start | bytes 1572868
  29.5 4.2 %collective-permute-start.13 = (bf16[2048,128]{1,0:T(8,128)(2,1)S(1)}, bf16[2048,128]{1,0:T(8,128)(2,1)S(1)}, u32[]{:S(2)}, u32[]{:S(2)}) collective-permute-start(bf16[2048,128]{1,0:T(8,128)(2,1)S(1)} %collective-permute-done.11.refs_5_), channel_id=1, source_target_pairs={{0,1},{1,0},{2,3},{3,2},{4,5},{5,4},{6,7},{7,6},{8,9},{9,8},{10,11... | collective-permute-start | bytes 1572872 | tf_op jit(solution)/shard_map/ppermute | solution.py:25
  31.3 13.6 %collective-permute-start.3 = (bf16[2048,128]{1,0:T(8,128)(2,1)S(1)}, bf16[2048,128]{1,0:T(8,128)(2,1)}, u32[]{:S(2)}, u32[]{:S(2)}) collective-permute-start(bf16[2048,128]{1,0:T(8,128)(2,1)S(1)} %collective-permute-done.2.refs_4_), channel_id=1, source_target_pairs={{0,64},{1,65},{2,66},{3,67},{4,68},{5,69},{6,70},{7,71},{8,72},{9,... | collective-permute-start | bytes 1572872 | tf_op jit(solution)/shard_map/ppermute | solution.py:25
  31.3 14.7 %collective-permute-start.5 = (bf16[2048,128]{1,0:T(8,128)(2,1)S(1)}, bf16[2048,128]{1,0:T(8,128)(2,1)}, u32[]{:S(2)}, u32[]{:S(2)}) collective-permute-start(bf16[2048,128]{1,0:T(8,128)(2,1)S(1)} %collective-permute-done.4.refs_1_), channel_id=1, source_target_pairs={{0,66},{1,67},{2,64},{3,65},{4,70},{5,71},{6,68},{7,69},{8,74},{9,... | collective-permute-start | bytes 1572872 | tf_op jit(solution)/shard_map/ppermute | solution.py:25
  33.2 39.6 %copy-start.15 = (bf16[2048,128]{1,0:T(8,128)(2,1)}, bf16[2048,128]{1,0:T(8,128)(2,1)S(1)}, u32[]{:S(2)}) copy-start(bf16[2048,128]{1,0:T(8,128)(2,1)S(1)} %collective-permute-done.10.refs_3_) | copy-start | bytes 1572868
  33.2 44.1 %collective-permute-start.9 = (bf16[2048,128]{1,0:T(8,128)(2,1)}, bf16[2048,128]{1,0:T(8,128)(2,1)}, u32[]{:S(2)}, u32[]{:S(2)}) collective-permute-start(bf16[2048,128]{1,0:T(8,128)(2,1)} %collective-permute-done.8.refs_0_), channel_id=1, source_target_pairs={{0,1},{1,0},{2,3},{3,2},{4,5},{5,4},{6,7},{7,6},{8,9},{9,8},{10,11... | collective-permute-start | bytes 1572872 | tf_op jit(solution)/shard_map/ppermute | solution.py:25
  33.6 12.4 %copy-start.16 = (bf16[2048,128]{1,0:T(8,128)(2,1)}, bf16[2048,128]{1,0:T(8,128)(2,1)S(1)}, u32[]{:S(2)}) copy-start(bf16[2048,128]{1,0:T(8,128)(2,1)S(1)} %collective-permute-done.12.refs_6_) | copy-start | bytes 1572868
  33.6 62.9 %collective-permute-start = (bf16[2048,128]{1,0:T(8,128)(2,1)S(1)}, bf16[2048,128]{1,0:T(8,128)(2,1)}, u32[]{:S(2)}, u32[]{:S(2)}) collective-permute-start(bf16[2048,128]{1,0:T(8,128)(2,1)S(1)} %get-tuple-element.9.refs_2_), channel_id=1, source_target_pairs={{0,1},{1,0},{2,3},{3,2},{4,5},{5,4},{6,7},{7,6},{8,9},{9,8},{10,11... | collective-permute-start | bytes 1572872 | tf_op jit(solution)/shard_map/ppermute | solution.py:25
  33.7 12.3 %copy-start.18 = (bf16[2048,128]{1,0:T(8,128)(2,1)}, bf16[2048,128]{1,0:T(8,128)(2,1)S(1)}, u32[]{:S(2)}) copy-start(bf16[2048,128]{1,0:T(8,128)(2,1)S(1)} %collective-permute-done.13.refs_7_) | copy-start | bytes 1572868
  33.7 62.8 %collective-permute-start.1 = (bf16[2048,128]{1,0:T(8,128)(2,1)S(1)}, bf16[2048,128]{1,0:T(8,128)(2,1)}, u32[]{:S(2)}, u32[]{:S(2)}) collective-permute-start(bf16[2048,128]{1,0:T(8,128)(2,1)S(1)} %get-tuple-element.10.refs_3_), channel_id=1, source_target_pairs={{0,1},{1,0},{2,3},{3,2},{4,5},{5,4},{6,7},{7,6},{8,9},{9,8},{10,11... | collective-permute-start | bytes 1572872 | tf_op jit(solution)/shard_map/ppermute | solution.py:25
  44.9 51.6 %collective-permute-start.6 = (bf16[2048,128]{1,0:T(8,128)(2,1)}, bf16[2048,128]{1,0:T(8,128)(2,1)}, u32[]{:S(2)}, u32[]{:S(2)}) collective-permute-start(bf16[2048,128]{1,0:T(8,128)(2,1)} %collective-permute-done.3.refs_6_), channel_id=1, source_target_pairs={{0,1},{1,0},{2,3},{3,2},{4,5},{5,4},{6,7},{7,6},{8,9},{9,8},{10,11... | collective-permute-start | bytes 1572872 | tf_op jit(solution)/shard_map/ppermute | solution.py:25
  46.0 50.5 %collective-permute-start.7 = (bf16[2048,128]{1,0:T(8,128)(2,1)}, bf16[2048,128]{1,0:T(8,128)(2,1)}, u32[]{:S(2)}, u32[]{:S(2)}) collective-permute-start(bf16[2048,128]{1,0:T(8,128)(2,1)} %collective-permute-done.5.refs_7_), channel_id=1, source_target_pairs={{0,1},{1,0},{2,3},{3,2},{4,5},{5,4},{6,7},{7,6},{8,9},{9,8},{10,11... | collective-permute-start | bytes 1572872 | tf_op jit(solution)/shard_map/ppermute | solution.py:25
  72.9 23.6 %all-to-all-start.1 = ((bf16[128,8,128]{2,1,0:T(8,128)(2,1)}), bf16[128,8,128]{2,1,0:T(8,128)(2,1)S(1)}, u32[]{:S(2)}, u32[]{:S(2)}) async-start(bf16[128,8,128]{2,1,0:T(8,128)(2,1)} %broadcast_in_dim.4), calls=%async_computation.1 | async-start | bytes 524288 | tf_op jit(solution)/shard_map/all_to_all | solution.py:369
  77.4 13.5 %copy-start.6 = (s32[8,8]{1,0:T(8,128)S(1)}, s32[8,8]{1,0:T(8,128)}, u32[]{:S(2)}) copy-start(s32[8,8]{1,0:T(8,128)} %list_ref.3) | copy-start | bytes 772
  115.3 81.1 %copy-start = (bf16[2048,128]{1,0:T(8,128)(2,1)}, bf16[2048,128]{1,0:T(8,128)(2,1)S(1)}, u32[]{:S(2)}) copy-start(bf16[2048,128]{1,0:T(8,128)(2,1)S(1)} %get-tuple-element.11.refs_2_) | copy-start | bytes 1572868
  115.3 81.1 %copy-start.1 = (bf16[2048,128]{1,0:T(8,128)(2,1)}, bf16[2048,128]{1,0:T(8,128)(2,1)S(1)}, u32[]{:S(2)}) copy-start(bf16[2048,128]{1,0:T(8,128)(2,1)S(1)} %get-tuple-element.12.refs_3_) | copy-start | bytes 1572868
  115.3 12.5 %collective-permute-start.18 = (bf16[2048,128]{1,0:T(8,128)(2,1)S(1)}, bf16[2048,128]{1,0:T(8,128)(2,1)S(1)}, u32[]{:S(2)}, u32[]{:S(2)}) collective-permute-start(bf16[2048,128]{1,0:T(8,128)(2,1)S(1)} %get-tuple-element.12.refs_3_), channel_id=1, source_target_pairs={{0,64},{1,65},{2,66},{3,67},{4,68},{5,69},{6,70},{7,71},{8,72},{9,... | collective-permute-start | bytes 1572872 | tf_op jit(solution)/shard_map/ppermute | solution.py:25
  116.7 14.5 %collective-permute-start.16 = (bf16[2048,128]{1,0:T(8,128)(2,1)S(1)}, bf16[2048,128]{1,0:T(8,128)(2,1)S(1)}, u32[]{:S(2)}, u32[]{:S(2)}) collective-permute-start(bf16[2048,128]{1,0:T(8,128)(2,1)S(1)} %get-tuple-element.11.refs_2_), channel_id=1, source_target_pairs={{0,66},{1,67},{2,64},{3,65},{4,70},{5,71},{6,68},{7,69},{8,74},{9,... | collective-permute-start | bytes 1572872 | tf_op jit(solution)/shard_map/ppermute | solution.py:25
  118.5 20.6 %collective-permute-start.22 = (bf16[2048,128]{1,0:T(8,128)(2,1)S(1)}, bf16[2048,128]{1,0:T(8,128)(2,1)S(1)}, u32[]{:S(2)}, u32[]{:S(2)}) collective-permute-start(bf16[2048,128]{1,0:T(8,128)(2,1)S(1)} %get-tuple-element.11.refs_2_), channel_id=1, source_target_pairs={{0,64},{1,65},{2,66},{3,67},{4,68},{5,69},{6,70},{7,71},{8,72},{9,... | collective-permute-start | bytes 1572872 | tf_op jit(solution)/shard_map/ppermute | solution.py:25
  118.8 23.5 %collective-permute-start.25 = (bf16[2048,128]{1,0:T(8,128)(2,1)S(1)}, bf16[2048,128]{1,0:T(8,128)(2,1)}, u32[]{:S(2)}, u32[]{:S(2)}) collective-permute-start(bf16[2048,128]{1,0:T(8,128)(2,1)S(1)} %get-tuple-element.12.refs_3_), channel_id=1, source_target_pairs={{0,66},{1,67},{2,64},{3,65},{4,70},{5,71},{6,68},{7,69},{8,74},{9,... | collective-permute-start | bytes 1572872 | tf_op jit(solution)/shard_map/ppermute | solution.py:25
  127.8 55.0 %copy-start.12 = (bf16[2048,128]{1,0:T(8,128)(2,1)}, bf16[2048,128]{1,0:T(8,128)(2,1)S(1)}, u32[]{:S(2)}) copy-start(bf16[2048,128]{1,0:T(8,128)(2,1)S(1)} %collective-permute-done.18.refs_1_) | copy-start | bytes 1572868
  127.8 16.3 %collective-permute-start.24 = (bf16[2048,128]{1,0:T(8,128)(2,1)S(1)}, bf16[2048,128]{1,0:T(8,128)(2,1)S(1)}, u32[]{:S(2)}, u32[]{:S(2)}) collective-permute-start(bf16[2048,128]{1,0:T(8,128)(2,1)S(1)} %collective-permute-done.18.refs_1_), channel_id=1, source_target_pairs={{0,1},{1,0},{2,3},{3,2},{4,5},{5,4},{6,7},{7,6},{8,9},{9,8},{10,11... | collective-permute-start | bytes 1572872 | tf_op jit(solution)/shard_map/ppermute | solution.py:25
  131.2 51.6 %copy-start.13 = (bf16[2048,128]{1,0:T(8,128)(2,1)}, bf16[2048,128]{1,0:T(8,128)(2,1)S(1)}, u32[]{:S(2)}) copy-start(bf16[2048,128]{1,0:T(8,128)(2,1)S(1)} %collective-permute-done.16.refs_4_) | copy-start | bytes 1572868
  131.2 14.5 %collective-permute-start.26 = (bf16[2048,128]{1,0:T(8,128)(2,1)S(1)}, bf16[2048,128]{1,0:T(8,128)(2,1)S(1)}, u32[]{:S(2)}, u32[]{:S(2)}) collective-permute-start(bf16[2048,128]{1,0:T(8,128)(2,1)S(1)} %collective-permute-done.16.refs_4_), channel_id=1, source_target_pairs={{0,1},{1,0},{2,3},{3,2},{4,5},{5,4},{6,7},{7,6},{8,9},{9,8},{10,11... | collective-permute-start | bytes 1572872 | tf_op jit(solution)/shard_map/ppermute | solution.py:25
  139.1 43.7 %copy-start.14 = (bf16[2048,128]{1,0:T(8,128)(2,1)}, bf16[2048,128]{1,0:T(8,128)(2,1)S(1)}, u32[]{:S(2)}) copy-start(bf16[2048,128]{1,0:T(8,128)(2,1)S(1)} %collective-permute-done.22.refs_0_) | copy-start | bytes 1572868
  139.1 6.8 %collective-permute-start.23 = (bf16[2048,128]{1,0:T(8,128)(2,1)S(1)}, bf16[2048,128]{1,0:T(8,128)(2,1)S(1)}, u32[]{:S(2)}, u32[]{:S(2)}) collective-permute-start(bf16[2048,128]{1,0:T(8,128)(2,1)S(1)} %collective-permute-done.22.refs_0_), channel_id=1, source_target_pairs={{0,1},{1,0},{2,3},{3,2},{4,5},{5,4},{6,7},{7,6},{8,9},{9,8},{10,11... | collective-permute-start | bytes 1572872 | tf_op jit(solution)/shard_map/ppermute | solution.py:25
  140.9 13.6 %collective-permute-start.17 = (bf16[2048,128]{1,0:T(8,128)(2,1)S(1)}, bf16[2048,128]{1,0:T(8,128)(2,1)}, u32[]{:S(2)}, u32[]{:S(2)}) collective-permute-start(bf16[2048,128]{1,0:T(8,128)(2,1)S(1)} %collective-permute-done.16.refs_4_), channel_id=1, source_target_pairs={{0,64},{1,65},{2,66},{3,67},{4,68},{5,69},{6,70},{7,71},{8,72},{9,... | collective-permute-start | bytes 1572872 | tf_op jit(solution)/shard_map/ppermute | solution.py:25
  142.3 13.5 %collective-permute-start.19 = (bf16[2048,128]{1,0:T(8,128)(2,1)S(1)}, bf16[2048,128]{1,0:T(8,128)(2,1)}, u32[]{:S(2)}, u32[]{:S(2)}) collective-permute-start(bf16[2048,128]{1,0:T(8,128)(2,1)S(1)} %collective-permute-done.18.refs_1_), channel_id=1, source_target_pairs={{0,66},{1,67},{2,64},{3,65},{4,70},{5,71},{6,68},{7,69},{8,74},{9,... | collective-permute-start | bytes 1572872 | tf_op jit(solution)/shard_map/ppermute | solution.py:25
  144.1 34.2 %copy-start.17 = (bf16[2048,128]{1,0:T(8,128)(2,1)}, bf16[2048,128]{1,0:T(8,128)(2,1)S(1)}, u32[]{:S(2)}) copy-start(bf16[2048,128]{1,0:T(8,128)(2,1)S(1)} %collective-permute-done.24.refs_3_) | copy-start | bytes 1572868
  144.1 38.7 %collective-permute-start.27 = (bf16[2048,128]{1,0:T(8,128)(2,1)}, bf16[2048,128]{1,0:T(8,128)(2,1)}, u32[]{:S(2)}, u32[]{:S(2)}) collective-permute-start(bf16[2048,128]{1,0:T(8,128)(2,1)} %collective-permute-done.25.refs_5_), channel_id=1, source_target_pairs={{0,1},{1,0},{2,3},{3,2},{4,5},{5,4},{6,7},{7,6},{8,9},{9,8},{10,11... | collective-permute-start | bytes 1572872 | tf_op jit(solution)/shard_map/ppermute | solution.py:25
  145.7 12.3 %copy-start.19 = (bf16[2048,128]{1,0:T(8,128)(2,1)}, bf16[2048,128]{1,0:T(8,128)(2,1)S(1)}, u32[]{:S(2)}) copy-start(bf16[2048,128]{1,0:T(8,128)(2,1)S(1)} %collective-permute-done.26.refs_6_) | copy-start | bytes 1572868
  145.7 56.2 %collective-permute-start.14 = (bf16[2048,128]{1,0:T(8,128)(2,1)S(1)}, bf16[2048,128]{1,0:T(8,128)(2,1)}, u32[]{:S(2)}, u32[]{:S(2)}) collective-permute-start(bf16[2048,128]{1,0:T(8,128)(2,1)S(1)} %get-tuple-element.11.refs_2_), channel_id=1, source_target_pairs={{0,1},{1,0},{2,3},{3,2},{4,5},{5,4},{6,7},{7,6},{8,9},{9,8},{10,11... | collective-permute-start | bytes 1572872 | tf_op jit(solution)/shard_map/ppermute | solution.py:25
  146.0 12.0 %copy-start.20 = (bf16[2048,128]{1,0:T(8,128)(2,1)}, bf16[2048,128]{1,0:T(8,128)(2,1)S(1)}, u32[]{:S(2)}) copy-start(bf16[2048,128]{1,0:T(8,128)(2,1)S(1)} %collective-permute-done.23.refs_2_) | copy-start | bytes 1572868
  146.0 55.9 %collective-permute-start.15 = (bf16[2048,128]{1,0:T(8,128)(2,1)S(1)}, bf16[2048,128]{1,0:T(8,128)(2,1)}, u32[]{:S(2)}, u32[]{:S(2)}) collective-permute-start(bf16[2048,128]{1,0:T(8,128)(2,1)S(1)} %get-tuple-element.12.refs_3_), channel_id=1, source_target_pairs={{0,1},{1,0},{2,3},{3,2},{4,5},{5,4},{6,7},{7,6},{8,9},{9,8},{10,11... | collective-permute-start | bytes 1572872 | tf_op jit(solution)/shard_map/ppermute | solution.py:25
  154.5 47.4 %collective-permute-start.20 = (bf16[2048,128]{1,0:T(8,128)(2,1)}, bf16[2048,128]{1,0:T(8,128)(2,1)}, u32[]{:S(2)}, u32[]{:S(2)}) collective-permute-start(bf16[2048,128]{1,0:T(8,128)(2,1)} %collective-permute-done.17.refs_6_), channel_id=1, source_target_pairs={{0,1},{1,0},{2,3},{3,2},{4,5},{5,4},{6,7},{7,6},{8,9},{9,8},{10,11... | collective-permute-start | bytes 1572872 | tf_op jit(solution)/shard_map/ppermute | solution.py:25
  155.8 46.1 %collective-permute-start.21 = (bf16[2048,128]{1,0:T(8,128)(2,1)}, bf16[2048,128]{1,0:T(8,128)(2,1)}, u32[]{:S(2)}, u32[]{:S(2)}) collective-permute-start(bf16[2048,128]{1,0:T(8,128)(2,1)} %collective-permute-done.19.refs_7_), channel_id=1, source_target_pairs={{0,1},{1,0},{2,3},{3,2},{4,5},{5,4},{6,7},{7,6},{8,9},{9,8},{10,11... | collective-permute-start | bytes 1572872 | tf_op jit(solution)/shard_map/ppermute | solution.py:25
  178.3 23.6 %all-to-all-start.3 = ((bf16[128,8,128]{2,1,0:T(8,128)(2,1)}), bf16[128,8,128]{2,1,0:T(8,128)(2,1)S(1)}, u32[]{:S(2)}, u32[]{:S(2)}) async-start(bf16[128,8,128]{2,1,0:T(8,128)(2,1)} %broadcast_in_dim.5), calls=%async_computation.3 | async-start | bytes 524288 | tf_op jit(solution)/shard_map/all_to_all | solution.py:369
  (3 other events, 16.7 us)

commit v3 on v2

--- a/solution.py
+++ b/solution.py
@@ -108,7 +108,7 @@
 
 def store_projection(total, out_ref):
     for r in range(total.shape[1] // NV):
-        out_ref[r * NV : (r + 1) * NV, :] = total[:, r * NV : (r + 1) * NV].T.astype(BF16)
+        out_ref[r * NV : (r + 1) * NV, :] = total[:, r * NV : (r + 1) * NV].T
 
 
 def project_body(x_hbm, y_hbm, basis_hbm, out_ref, x, y, basis, total, sems):
@@ -142,7 +142,7 @@
         project_body,
         in_specs=[ANY_SPEC] * 3,
         out_specs=VMEM_SPEC,
-        out_shape=pltpu.HBM((rank, NV), BF16),
+        out_shape=pltpu.HBM((rank, NV), F32),
         scratch_shapes=[
             pltpu.VMEM((rows, NV), F32),
             pltpu.VMEM((rows, NV), F32),
@@ -249,16 +249,21 @@
 
 def finish_body(last, slot_ref, list_ref, *refs):
     chunks = refs[:8]
-    x_hbm, y_hbm, energy_ref, shift_ref, kernel_hbm, basis_hbm, weight_ref, mirror_ref = refs[8:16]
-    rest = refs[16:]
+    x_hbm, y_hbm, energy_ref, shift_ref, kernel_hbm, basis_hbm, kept_hbm, other_hbm, mirror_ref = refs[8:17]
+    rest = refs[17:]
     if last:
         next_x_hbm, next_y_hbm = rest[:2]
-        flat, columns, kernel, basis, x, y, chunk_sems, sems = rest[2:]
+        flat, columns, kernel, basis, x, y, weights, chunk_sems, sems, weight_sems = rest[2:]
     else:
         next_x_hbm, next_y_hbm, low_ref, high_ref, project_ref = rest[:5]
-        flat, columns, kernel, basis, x, y, chunk_sems, sems, scratch, total = rest[5:]
+        flat, columns, kernel, basis, x, y, weights, chunk_sems, sems, weight_sems, scratch, total = rest[5:]
     blocks = kernel.shape[0]
     copies = load_patch(slot_ref, chunks, flat, chunk_sems)
+    side = weights.shape[0] // 2
+    for k, half_hbm in enumerate((kept_hbm, other_hbm)):
+        place = pl.ds(pl.multiple_of(((slot_ref[0] ^ k) & 1) * side, side), side)
+        copies.append(pltpu.make_async_copy(half_hbm, weights.at[place], weight_sems.at[k]))
+        copies[-1].start()
 
     def load(b, t):
         if t == 0:
@@ -292,7 +297,7 @@
             load(b, t).wait()
         part = block_rows(b)
         mirrored = mirror_ref[b]
-        exchange = jnp.dot(basis[part, :], weight_ref[...], preferred_element_type=F32)
+        exchange = jnp.dot(basis[part, :], weights[...], preferred_element_type=F32)
         direct = list_product(kernel, columns, list_ref, b)
         row = energy_ref[b]
         levels = jnp.concatenate([column_of(row[:, 0:half]), column_of(row[:, half:])], axis=0)
@@ -338,12 +343,14 @@
         pltpu.VMEM(basis.shape, BF16),
         pltpu.VMEM((rows, NV), F32),
         pltpu.VMEM((rows, NV), F32),
+        pltpu.VMEM((rank, NV), BF16),
         pltpu.SemaphoreType.DMA((8,)),
         pltpu.SemaphoreType.DMA((4, blocks)),
+        pltpu.SemaphoreType.DMA((2,)),
     ]
     if not last:
         out_specs += [VMEM_SPEC] * 3
-        out_shape += [jax.ShapeDtypeStruct((rows, NV), BF16)] * 2 + [pltpu.HBM((rank, NV), BF16)]
+        out_shape += [jax.ShapeDtypeStruct((rows, NV), BF16)] * 2 + [pltpu.HBM((rank, NV), F32)]
         scratch += [pltpu.VMEM((2 * BLK, NV), F32), pltpu.VMEM((NV, rank), F32)]
 
     def body(*refs):
@@ -351,23 +358,37 @@
 
     return pl.pallas_call(
         body,
-        in_specs=[SMEM_SPEC] * 2 + [ANY_SPEC] * 10 + [VMEM_SPEC] * 2 + [ANY_SPEC] * 2 + [VMEM_SPEC] * 2,
+        in_specs=[SMEM_SPEC] * 2 + [ANY_SPEC] * 10 + [VMEM_SPEC] * 2 + [ANY_SPEC] * 4 + [VMEM_SPEC],
         out_specs=out_specs,
         out_shape=out_shape,
         scratch_shapes=scratch,
         compiler_params=pltpu.CompilerParams(vmem_limit_bytes=32 * MIB),
         name="finish_last" if last else "finish",
-    )(slot, indices, *in_hbm(*chunks, x, y), energy, shift, *in_hbm(kernel, basis), weights, mirrored)
-
-
-def total_weights(partial):
-    size = lax.axis_size(AXES)
+    )(slot, indices, *in_hbm(*chunks, x, y), energy, shift, *in_hbm(kernel, basis, *weights), mirrored)
+
+
+def half_of(array, index):
+    rows = array.shape[0] // 2
+    return lax.dynamic_slice_in_dim(array, index * rows, rows, 0)
+
+
+def total_weights(partial, near, far):
+    wide = lax.axis_size("wide")
+    plane = wide // 2
+    groups = [list(range(plane)), list(range(plane, wide))]
+    core = lax.axis_index("narrow") % 2
     rank, vectors = partial.shape
-    part = rank // size
-    pieces = lax.all_to_all(partial.reshape(size, part, vectors), AXES, 0, 0, tiled=True)
-    own = jnp.sum(pieces.astype(F32), axis=0).astype(BF16)
-    spread = lax.all_to_all(jnp.broadcast_to(own[None], (size, part, vectors)), AXES, 0, 0, tiled=True)
-    return spread.reshape(rank, vectors)
+    part = rank // (2 * plane)
+    mine = half_of(partial, core) + toggled(half_of(partial, 1 - core), 1)
+    pieces = lax.all_to_all(mine.reshape(plane, part, vectors), "wide", 0, 0, axis_index_groups=groups, tiled=True)
+    own = jnp.sum(pieces, axis=0)
+    others = [toggled(own, mask) for mask in (near, far, near ^ far)]
+    final = ((own + others[0]) + (others[1] + others[2])).astype(BF16)
+    spread = lax.all_to_all(
+        jnp.broadcast_to(final[None], (plane, part, vectors)), "wide", 0, 0, axis_index_groups=groups, tiled=True
+    )
+    kept = spread.reshape(rank // 2, vectors)
+    return kept, toggled(kept, 1)
 
 
 def on_device(x, y, energy, shift, res_kernel, res_list, cp_kernel, cp_list, partner, basis):
@@ -395,7 +416,7 @@
         mirror_chunks += [far_low, far_high]
         mirror_chunks += [toggled(c, 1) for c in mirror_chunks[4:]]
         own_chunks = [low, high] + own + across + [toggled(c, 1) for c in across]
-        weights = total_weights(partial)
+        weights = total_weights(partial, near, far)
         mirror = mirror_columns(slot, partner, mirror_chunks)
         mirrored = mirror_product(cp_list, mirror, cp_kernel)
         out = finish(

time: 217 us -> 205 us (0.945)
  waiting for transfers between devices: 50.5 us -> 34.7 us
  blocking collectives: 39.6 us -> 24 us
  starting transfers between devices: 45.8 us -> 57.8 us
  local copies, waits for them, and re-layouts: 1.59 us -> 4.96 us
  other arithmetic: 0.28 us -> 3.51 us
    ppermute x28 -> x38, waiting for transfers between devices: 50.5 us -> 26.7 us  [toggled(): lax.ppermute(array, AXES, [(i, i ^ mask) for i in range(lax.axis_size(AXE...]
    all_to_all x2, blocking collectives: 39.6 us -> 24 us  [total_weights(): lax.all_to_all(jnp.broadcast_to(final[None], (plane, part, vectors)), 'wi...]
    ppermute x28 -> x38, starting transfers between devices: 36.8 us -> 46.6 us  [toggled(): lax.ppermute(array, AXES, [(i, i ^ mask) for i in range(lax.axis_size(AXE...]
    all_to_all x2, waiting for transfers between devices: 0.01 us -> 8 us  [total_weights(): lax.all_to_all(mine.reshape(plane, part, vectors), 'wide', 0, 0, axis_ind...]
    add x0 -> x2, other arithmetic: none -> 3.44 us  [total_weights(): mine = half_of(partial, core) + toggled(half_of(partial, 1 - core), 1)]
    unnamed x42 -> x78, local copies, waits for them, and re-layouts: 0.1 us -> 2.77 us
  transfers between devices with their start and end apart: 30 -> 40, of which waited for: 8 -> 10; matrix products, arithmetic and copies ran while one was open for 1% -> 2% of each run, Pallas kernels for 20% -> 19%
where the time goes in v3:
time: 205 us; the launch traced here: 204 us
  Pallas kernels  77.8 us (38%)
  starting transfers between devices  57.8 us (28%)
  waiting for transfers between devices  34.7 us (17%)
  blocking collectives  24 us (12%)
  local copies, waits for them, and re-layouts  4.96 us (2%)
  other arithmetic  3.51 us (2%)
    ppermute x38, starting transfers between devices, toggled(): lax.ppermute(array, AXES, [(i, i ^ mask) for i in range(lax.axis_size(AXE...  46.6 us
    pallas_call x2, Pallas kernels, finish(): pl.pallas_call(body, in_specs=[SMEM_SPEC] * 2 + [ANY_SPEC] * 10 + [VMEM_S...  33.3 us
    pallas_call x2, Pallas kernels, mirror_columns(): pl.pallas_call(gather_body, in_specs=[SMEM_SPEC] * 2 + [ANY_SPEC] * 8, ou...  27 us
    ppermute x38, waiting for transfers between devices, toggled(): lax.ppermute(array, AXES, [(i, i ^ mask) for i in range(lax.axis_size(AXE...  26.7 us
    all_to_all x2, blocking collectives, total_weights(): lax.all_to_all(jnp.broadcast_to(final[None], (plane, part, vectors)), 'wi...  24 us
    all_to_all x2, starting transfers between devices, total_weights(): lax.all_to_all(mine.reshape(plane, part, vectors), 'wide', 0, 0, axis_ind...  11.1 us
    pallas_call x2, Pallas kernels, mirror_product(): pl.pallas_call(product_body, in_specs=[SMEM_SPEC, VMEM_SPEC, ANY_SPEC], o...  10.9 us
    all_to_all x2, waiting for transfers between devices, total_weights(): lax.all_to_all(mine.reshape(plane, part, vectors), 'wide', 0, 0, axis_ind...  8 us
  transfers between devices with their start and end apart: 40, of which 10 were waited for; matrix products, arithmetic and copies ran while one was open for 2% of the time, Pallas kernels for 19%

profile of v3, /device:TPU:1, one launch (start us, length us, event | category | flops | bytes accessed | tf_op | source)
XLA Modules:
  0.0 204.2 jit_solution(1227605228076079364)
XLA Ops:
  0.7 5.0 %project.1 = f32[1024,128]{1,0:T(8,128)} custom-call(f32[2048,128]{1,0:T(8,128)} %refs_10_.1, f32[2048,128]{1,0:T(8,128)} %refs_11_.1, bf16[2048,1024]{1,0:T(8,128)(2,1)} %refs_15_.3), custom_call_target="tpu_custom_call" | custom-call | tf_op jit(solution)/shard_map/project/pallas_call | solution.py:141
  5.7 1.0 constant_dynamic-slice_fusion.1
  6.7 1.5 collective-permute-start.8
  8.1 1.6 pack.1
  9.8 1.5 collective-permute-start.4
  11.3 1.9 collective-permute-start.2
  14.2 1.8 dynamic-slice_add_fusion.1
  15.9 7.6 %all-to-all-start = ((f32[16,32,128]{2,1,0:T(8,128)}), f32[16,32,128]{2,1,0:T(8,128)S(1)}, u32[]{:S(2)}, u32[]{:S(2)}) async-start(f32[16,32,128]{2,1,0:T(8,128)} %bitcast.3), calls=%async_computation | async-start | bytes 524288 | tf_op jit(solution)/shard_map/all_to_all | solution.py:383
  23.6 1.2 collective-permute-start.15
  24.8 6.1 %all-to-all-done = f32[16,32,128]{2,1,0:T(8,128)S(1)} async-done(((f32[16,32,128]{2,1,0:T(8,128)}), f32[16,32,128]{2,1,0:T(8,128)S(1)}, u32[]{:S(2)}, u32[]{:S(2)}) %all-to-all-start) | async-done | bytes 262176 | tf_op jit(solution)/shard_map/all_to_all | solution.py:383
  30.9 2.1 %collective-permute-start.10 = (f32[32,128]{1,0:T(8,128)S(1)}, f32[32,128]{1,0:T(8,128)S(1)}, u32[]{:S(2)}, u32[]{:S(2)}) collective-permute-start(f32[32,128]{1,0:T(8,128)S(1)} %reduce_sum.18), channel_id=1, source_target_pairs={{0,66},{1,67},{2,64},{3,65},{4,70},{5,71},{6,68},{7,69},{8,74},{9,... | collective-permute-start | bytes 49160 | tf_op jit(solution)/shard_map/ppermute | solution.py:25
  33.4 1.1 collective-permute-done.13.refs_0_
  34.6 1.4 collective-permute-start.9
  36.0 0.9 collective-permute-done.16.refs_5_
  36.9 1.5 collective-permute-start.17
  38.6 2.1 %collective-permute-start.5 = (bf16[2048,128]{1,0:T(8,128)(2,1)S(1)}, bf16[2048,128]{1,0:T(8,128)(2,1)S(1)}, u32[]{:S(2)}, u32[]{:S(2)}) collective-permute-start(bf16[2048,128]{1,0:T(8,128)(2,1)S(1)} %collective-permute-done.4.refs_1_), channel_id=1, source_target_pairs={{0,66},{1,67},{2,64},{3,65},{4,70},{5,71},{6,68},{7,69},{8,74},{9,... | collective-permute-start | bytes 1572872 | tf_op jit(solution)/shard_map/ppermute | solution.py:25
  40.7 1.8 collective-permute-start.18
  43.0 6.5 %collective-permute-done.3.refs_6_ = bf16[2048,128]{1,0:T(8,128)(2,1)S(1)} collective-permute-done((bf16[2048,128]{1,0:T(8,128)(2,1)S(1)}, bf16[2048,128]{1,0:T(8,128)(2,1)S(1)}, u32[]{:S(2)}, u32[]{:S(2)}) %collective-permute-start.3) | collective-permute-done | bytes 524320 | tf_op jit(solution)/shard_map/ppermute | solution.py:25
  49.5 3.4 %collective-permute-start.6 = (bf16[2048,128]{1,0:T(8,128)(2,1)S(1)}, bf16[2048,128]{1,0:T(8,128)(2,1)S(1)}, u32[]{:S(2)}, u32[]{:S(2)}) collective-permute-start(bf16[2048,128]{1,0:T(8,128)(2,1)S(1)} %collective-permute-done.3.refs_6_), channel_id=1, source_target_pairs={{0,1},{1,0},{2,3},{3,2},{4,5},{5,4},{6,7},{7,6},{8,9},{9,8},{10,11... | collective-permute-start | bytes 1572872 | tf_op jit(solution)/shard_map/ppermute | solution.py:25
  52.9 1.3 collective-permute-start.7
  54.3 14.3 %all_to_all.20 = bf16[16,32,128]{2,1,0:T(8,128)(2,1)S(1)} all-to-all(bf16[16,32,128]{2,1,0:T(8,128)(2,1)S(1)} %broadcast_in_dim.4), channel_id=1, replica_groups={{0,4,8,12,16,20,24,28,32,36,40,44,48,52,56,60},{64,68,72,76,80,84,88,92..., dimensions={0} | all-to-all | bytes 262144 | tf_op jit(solution)/shard_map/all_to_all | solution.py:387
  68.6 1.6 collective-permute-start.12
  70.3 13.5 %mirror_columns.2.columns_ref = bf16[32,256,256]{2,1,0:T(8,128)(2,1)S(1)} custom-call(s32[1]{0:T(128)} %bitcast.slot_ref.refs_0_, s32[1,8192]{1,0:T(1,128)S(1)} %copy-done.4, bf16[2048,128]{1,0:T(8,128)(2,1)} %copy-done.13, bf16[2048,128]{1,0:T(8,128)(2,1)} %copy-done.11, bf16[2048,128]{1,0:T(8,128)(2,1)} %copy-done.27, ...), custom_call_target="tpu_custom_call" | custom-call | tf_op jit(solution)/shard_map/mirror_columns/pallas_call | solution.py:201
  83.9 5.5 %mirror_product.2.refs_18_ = f32[8,256,256]{2,1,0:T(8,128)S(1)} custom-call(s32[8,8]{1,0:T(8,128)S(1)} %copy-done.6, bf16[32,256,256]{2,1,0:T(8,128)(2,1)S(1)} %mirror_columns.2.columns_ref, bf16[8,8,256,256]{3,2,1,0:T(8,128)(2,1)} %kernel_hbm.3), custom_call_target="tpu_custom_call" | custom-call | tf_op jit(solution)/shard_map/mirror_product/pallas_call | solution.py:235
  90.8 18.8 %finish.1 = (f32[2048,128]{1,0:T(8,128)}, f32[2048,128]{1,0:T(8,128)}, bf16[2048,128]{1,0:T(8,128)(2,1)S(1)}, bf16[2048,128]{1,0:T(8,128)(2,1)S(1)}, f32[1024,128]{1,0:T(8,128)}) custom-call(s32[1]{0:T(128)} %bitcast.slot_ref.refs_0_, s32[8,8]{1,0:T(8,128)S(1)} %copy-done.7, bf16[2048,128]{1,0:T(8,128)(2,1)} %copy-done.2, bf16[2048,128]{1,0:T(8,128)(2,1)} %copy-done.3, ...), custom_call_target="tpu_custom_call" | custom-call | tf_op jit(solution)/shard_map/finish/pallas_call | solution.py:359
  109.5 1.2 constant_dynamic-slice_fusion
  111.7 1.3 collective-permute-start.23
  113.0 1.9 collective-permute-start.21
  115.6 1.7 dynamic-slice_add_fusion
  117.3 3.5 %all-to-all-start.2 = ((f32[16,32,128]{2,1,0:T(8,128)}), f32[16,32,128]{2,1,0:T(8,128)S(1)}, u32[]{:S(2)}, u32[]{:S(2)}) async-start(f32[16,32,128]{2,1,0:T(8,128)} %bitcast.5), calls=%async_computation.2 | async-start | bytes 524288 | tf_op jit(solution)/shard_map/all_to_all | solution.py:383
  120.9 4.0 %collective-permute-done.32.refs_0_ = bf16[2048,128]{1,0:T(8,128)(2,1)S(1)} collective-permute-done((bf16[2048,128]{1,0:T(8,128)(2,1)S(1)}, bf16[2048,128]{1,0:T(8,128)(2,1)S(1)}, u32[]{:S(2)}, u32[]{:S(2)}) %collective-permute-start.32) | collective-permute-done | bytes 524320 | tf_op jit(solution)/shard_map/ppermute | solution.py:25
  124.9 1.5 collective-permute-start.33
  126.4 1.9 all-to-all-done.2
  128.6 7.6 %collective-permute-done.23.refs_1_ = bf16[2048,128]{1,0:T(8,128)(2,1)S(1)} collective-permute-done((bf16[2048,128]{1,0:T(8,128)(2,1)S(1)}, bf16[2048,128]{1,0:T(8,128)(2,1)S(1)}, u32[]{:S(2)}, u32[]{:S(2)}) %collective-permute-start.23) | collective-permute-done | bytes 524320 | tf_op jit(solution)/shard_map/ppermute | solution.py:25
  136.1 1.9 collective-permute-start.29
  138.2 1.5 collective-permute-start.34
  139.9 1.2 collective-permute-start.22
  141.2 1.0 collective-permute-done.30
  142.1 1.0 collective-permute-start.24
  143.1 2.7 %collective-permute-start.37 = (bf16[2048,128]{1,0:T(8,128)(2,1)S(1)}, bf16[2048,128]{1,0:T(8,128)(2,1)S(1)}, u32[]{:S(2)}, u32[]{:S(2)}) collective-permute-start(bf16[2048,128]{1,0:T(8,128)(2,1)S(1)} %collective-permute-done.35.refs_5_), channel_id=1, source_target_pairs={{0,1},{1,0},{2,3},{3,2},{4,5},{5,4},{6,7},{7,6},{8,9},{9,8},{10,11... | collective-permute-start | bytes 1572872 | tf_op jit(solution)/shard_map/ppermute | solution.py:25
  146.3 5.4 %collective-permute-done.22.refs_6_ = bf16[2048,128]{1,0:T(8,128)(2,1)S(1)} collective-permute-done((bf16[2048,128]{1,0:T(8,128)(2,1)S(1)}, bf16[2048,128]{1,0:T(8,128)(2,1)S(1)}, u32[]{:S(2)}, u32[]{:S(2)}) %collective-permute-start.22) | collective-permute-done | bytes 524320 | tf_op jit(solution)/shard_map/ppermute | solution.py:25
  151.7 2.6 %collective-permute-start.25 = (bf16[2048,128]{1,0:T(8,128)(2,1)S(1)}, bf16[2048,128]{1,0:T(8,128)(2,1)S(1)}, u32[]{:S(2)}, u32[]{:S(2)}) collective-permute-start(bf16[2048,128]{1,0:T(8,128)(2,1)S(1)} %collective-permute-done.22.refs_6_), channel_id=1, source_target_pairs={{0,1},{1,0},{2,3},{3,2},{4,5},{5,4},{6,7},{7,6},{8,9},{9,8},{10,11... | collective-permute-start | bytes 1572872 | tf_op jit(solution)/shard_map/ppermute | solution.py:25
  154.3 3.4 %collective-permute-start.26 = (bf16[2048,128]{1,0:T(8,128)(2,1)S(1)}, bf16[2048,128]{1,0:T(8,128)(2,1)S(1)}, u32[]{:S(2)}, u32[]{:S(2)}) collective-permute-start(bf16[2048,128]{1,0:T(8,128)(2,1)S(1)} %collective-permute-done.24.refs_7_), channel_id=1, source_target_pairs={{0,1},{1,0},{2,3},{3,2},{4,5},{5,4},{6,7},{7,6},{8,9},{9,8},{10,11... | collective-permute-start | bytes 1572872 | tf_op jit(solution)/shard_map/ppermute | solution.py:25
  157.7 9.7 %all_to_all.21 = bf16[16,32,128]{2,1,0:T(8,128)(2,1)S(1)} all-to-all(bf16[16,32,128]{2,1,0:T(8,128)(2,1)S(1)} %broadcast_in_dim.5), channel_id=1, replica_groups={{0,4,8,12,16,20,24,28,32,36,40,44,48,52,56,60},{64,68,72,76,80,84,88,92..., dimensions={0} | all-to-all | bytes 262144 | tf_op jit(solution)/shard_map/all_to_all | solution.py:387
  167.4 1.6 collective-permute-start.31
  169.1 13.5 %mirror_columns.3.columns_ref = bf16[32,256,256]{2,1,0:T(8,128)(2,1)S(1)} custom-call(s32[1]{0:T(128)} %bitcast.slot_ref.refs_0_, s32[1,8192]{1,0:T(1,128)S(1)} %copy-done.4, bf16[2048,128]{1,0:T(8,128)(2,1)} %copy-done.15, bf16[2048,128]{1,0:T(8,128)(2,1)} %copy-done.16, bf16[2048,128]{1,0:T(8,128)(2,1)} %collective-permute-done.33.refs_2_, ...), custom_call_target="tpu_custom_call" | custom-call | tf_op jit(solution)/shard_map/mirror_columns/pallas_call | solution.py:201
  182.6 5.5 %mirror_product.3.refs_18_ = f32[8,256,256]{2,1,0:T(8,128)S(1)} custom-call(s32[8,8]{1,0:T(8,128)S(1)} %copy-done.6, bf16[32,256,256]{2,1,0:T(8,128)(2,1)S(1)} %mirror_columns.3.columns_ref, bf16[8,8,256,256]{3,2,1,0:T(8,128)(2,1)} %kernel_hbm.3), custom_call_target="tpu_custom_call" | custom-call | tf_op jit(solution)/shard_map/mirror_product/pallas_call | solution.py:235
  189.5 14.5 %finish_last.1 = (f32[2048,128]{1,0:T(8,128)}, f32[2048,128]{1,0:T(8,128)}) custom-call(s32[1]{0:T(128)} %bitcast.slot_ref.refs_0_, s32[8,8]{1,0:T(8,128)S(1)} %copy-done.7, bf16[2048,128]{1,0:T(8,128)(2,1)} %copy-done, bf16[2048,128]{1,0:T(8,128)(2,1)} %copy-done.1, bf16[2048,128]{1,0:T(8,128)(2,1)} %copy-done.25, bf16[2048,128]{1,0:T(8,128)(2,1)} %copy-done.29, ...), custom_call_target="tpu_custom_call" | custom-call | tf_op jit(solution)/shard_map/finish_last/pallas_call | solution.py:359
  (130 shorter events, 7.8 us)
Async XLA Ops:
  0.6 69.6 %copy-start.4 = (s32[1,8192]{1,0:T(1,128)S(1)}, s32[1,8192]{1,0:T(1,128)}, u32[]{:S(2)}) copy-start(s32[1,8192]{1,0:T(1,128)} %partner_ref.3) | copy-start | bytes 98308
  6.7 7.5 %collective-permute-start.8 = (f32[512,128]{1,0:T(8,128)S(1)}, f32[512,128]{1,0:T(8,128)}, u32[]{:S(2)}, u32[]{:S(2)}) collective-permute-start(f32[512,128]{1,0:T(8,128)S(1)} %constant_dynamic-slice_fusion.1), channel_id=1, source_target_pairs={{0,1},{1,0},{2,3},{3,2},{4,5},{5,4},{6,7},{7,6},{8,9},{9,8},{10,11... | collective-permute-start | bytes 786440 | tf_op jit(solution)/shard_map/ppermute | solution.py:25
  9.8 74.0 %copy-start.2 = (bf16[2048,128]{1,0:T(8,128)(2,1)}, bf16[2048,128]{1,0:T(8,128)(2,1)S(1)}, u32[]{:S(2)}) copy-start(bf16[2048,128]{1,0:T(8,128)(2,1)S(1)} %get-tuple-element.9.refs_2_) | copy-start | bytes 1572868
  9.8 74.0 %copy-start.3 = (bf16[2048,128]{1,0:T(8,128)(2,1)}, bf16[2048,128]{1,0:T(8,128)(2,1)S(1)}, u32[]{:S(2)}) copy-start(bf16[2048,128]{1,0:T(8,128)(2,1)S(1)} %get-tuple-element.10.refs_3_) | copy-start | bytes 1572868
  9.8 13.8 %collective-permute-start.4 = (bf16[2048,128]{1,0:T(8,128)(2,1)S(1)}, bf16[2048,128]{1,0:T(8,128)(2,1)S(1)}, u32[]{:S(2)}, u32[]{:S(2)}) collective-permute-start(bf16[2048,128]{1,0:T(8,128)(2,1)S(1)} %get-tuple-element.10.refs_3_), channel_id=1, source_target_pairs={{0,64},{1,65},{2,66},{3,67},{4,68},{5,69},{6,70},{7,71},{8,72},{9,... | collective-permute-start | bytes 1572872 | tf_op jit(solution)/shard_map/ppermute | solution.py:25
  11.3 21.8 %collective-permute-start.2 = (bf16[2048,128]{1,0:T(8,128)(2,1)S(1)}, bf16[2048,128]{1,0:T(8,128)(2,1)S(1)}, u32[]{:S(2)}, u32[]{:S(2)}) collective-permute-start(bf16[2048,128]{1,0:T(8,128)(2,1)S(1)} %get-tuple-element.9.refs_2_), channel_id=1, source_target_pairs={{0,66},{1,67},{2,64},{3,65},{4,70},{5,71},{6,68},{7,69},{8,74},{9,... | collective-permute-start | bytes 1572872 | tf_op jit(solution)/shard_map/ppermute | solution.py:25
  13.2 21.4 %collective-permute-start.13 = (bf16[2048,128]{1,0:T(8,128)(2,1)S(1)}, bf16[2048,128]{1,0:T(8,128)(2,1)S(1)}, u32[]{:S(2)}, u32[]{:S(2)}) collective-permute-start(bf16[2048,128]{1,0:T(8,128)(2,1)S(1)} %get-tuple-element.9.refs_2_), channel_id=1, source_target_pairs={{0,64},{1,65},{2,66},{3,67},{4,68},{5,69},{6,70},{7,71},{8,72},{9,... | collective-permute-start | bytes 1572872 | tf_op jit(solution)/shard_map/ppermute | solution.py:25
  13.6 23.3 %collective-permute-start.16 = (bf16[2048,128]{1,0:T(8,128)(2,1)S(1)}, bf16[2048,128]{1,0:T(8,128)(2,1)S(1)}, u32[]{:S(2)}, u32[]{:S(2)}) collective-permute-start(bf16[2048,128]{1,0:T(8,128)(2,1)S(1)} %get-tuple-element.10.refs_3_), channel_id=1, source_target_pairs={{0,66},{1,67},{2,64},{3,65},{4,70},{5,71},{6,68},{7,69},{8,74},{9,... | collective-permute-start | bytes 1572872 | tf_op jit(solution)/shard_map/ppermute | solution.py:25
  15.9 15.0 %all-to-all-start = ((f32[16,32,128]{2,1,0:T(8,128)}), f32[16,32,128]{2,1,0:T(8,128)S(1)}, u32[]{:S(2)}, u32[]{:S(2)}) async-start(f32[16,32,128]{2,1,0:T(8,128)} %bitcast.3), calls=%async_computation | async-start | bytes 524288 | tf_op jit(solution)/shard_map/all_to_all | solution.py:383
  23.6 46.6 %copy-start.11 = (bf16[2048,128]{1,0:T(8,128)(2,1)}, bf16[2048,128]{1,0:T(8,128)(2,1)S(1)}, u32[]{:S(2)}) copy-start(bf16[2048,128]{1,0:T(8,128)(2,1)S(1)} %collective-permute-done.4.refs_1_) | copy-start | bytes 1572868
  23.6 17.1 %collective-permute-start.15 = (bf16[2048,128]{1,0:T(8,128)(2,1)S(1)}, bf16[2048,128]{1,0:T(8,128)(2,1)}, u32[]{:S(2)}, u32[]{:S(2)}) collective-permute-start(bf16[2048,128]{1,0:T(8,128)(2,1)S(1)} %collective-permute-done.4.refs_1_), channel_id=1, source_target_pairs={{0,1},{1,0},{2,3},{3,2},{4,5},{5,4},{6,7},{7,6},{8,9},{9,8},{10,11... | collective-permute-start | bytes 1572872 | tf_op jit(solution)/shard_map/ppermute | solution.py:25
  30.9 7.5 %collective-permute-start.10 = (f32[32,128]{1,0:T(8,128)S(1)}, f32[32,128]{1,0:T(8,128)S(1)}, u32[]{:S(2)}, u32[]{:S(2)}) collective-permute-start(f32[32,128]{1,0:T(8,128)S(1)} %reduce_sum.18), channel_id=1, source_target_pairs={{0,66},{1,67},{2,64},{3,65},{4,70},{5,71},{6,68},{7,69},{8,74},{9,... | collective-permute-start | bytes 49160 | tf_op jit(solution)/shard_map/ppermute | solution.py:25
  33.1 37.1 %copy-start.12 = (bf16[2048,128]{1,0:T(8,128)(2,1)}, bf16[2048,128]{1,0:T(8,128)(2,1)S(1)}, u32[]{:S(2)}) copy-start(bf16[2048,128]{1,0:T(8,128)(2,1)S(1)} %collective-permute-done.2.refs_4_) | copy-start | bytes 1572868
  33.1 5.5 %collective-permute-start.11 = (f32[32,128]{1,0:T(8,128)S(1)}, f32[32,128]{1,0:T(8,128)S(1)}, u32[]{:S(2)}, u32[]{:S(2)}) collective-permute-start(f32[32,128]{1,0:T(8,128)S(1)} %reduce_sum.18), channel_id=1, source_target_pairs={{0,2},{1,3},{2,0},{3,1},{4,6},{5,7},{6,4},{7,5},{8,10},{9,11},{10,... | collective-permute-start | bytes 49160 | tf_op jit(solution)/shard_map/ppermute | solution.py:25
  34.6 4.0 %collective-permute-start.9 = (f32[32,128]{1,0:T(8,128)S(1)}, f32[32,128]{1,0:T(8,128)S(1)}, u32[]{:S(2)}, u32[]{:S(2)}) collective-permute-start(f32[32,128]{1,0:T(8,128)S(1)} %reduce_sum.18), channel_id=1, source_target_pairs={{0,64},{1,65},{2,66},{3,67},{4,68},{5,69},{6,70},{7,71},{8,72},{9,... | collective-permute-start | bytes 49160 | tf_op jit(solution)/shard_map/ppermute | solution.py:25
  36.9 5.6 %collective-permute-start.17 = (bf16[2048,128]{1,0:T(8,128)(2,1)S(1)}, bf16[2048,128]{1,0:T(8,128)(2,1)S(1)}, u32[]{:S(2)}, u32[]{:S(2)}) collective-permute-start(bf16[2048,128]{1,0:T(8,128)(2,1)S(1)} %collective-permute-done.2.refs_4_), channel_id=1, source_target_pairs={{0,1},{1,0},{2,3},{3,2},{4,5},{5,4},{6,7},{7,6},{8,9},{9,8},{10,11... | collective-permute-start | bytes 1572872 | tf_op jit(solution)/shard_map/ppermute | solution.py:25
  38.4 4.2 %collective-permute-start.14 = (bf16[2048,128]{1,0:T(8,128)(2,1)S(1)}, bf16[2048,128]{1,0:T(8,128)(2,1)S(1)}, u32[]{:S(2)}, u32[]{:S(2)}) collective-permute-start(bf16[2048,128]{1,0:T(8,128)(2,1)S(1)} %collective-permute-done.13.refs_0_), channel_id=1, source_target_pairs={{0,1},{1,0},{2,3},{3,2},{4,5},{5,4},{6,7},{7,6},{8,9},{9,8},{10,11... | collective-permute-start | bytes 1572872 | tf_op jit(solution)/shard_map/ppermute | solution.py:25
  38.6 10.9 %collective-permute-start.3 = (bf16[2048,128]{1,0:T(8,128)(2,1)S(1)}, bf16[2048,128]{1,0:T(8,128)(2,1)S(1)}, u32[]{:S(2)}, u32[]{:S(2)}) collective-permute-start(bf16[2048,128]{1,0:T(8,128)(2,1)S(1)} %collective-permute-done.2.refs_4_), channel_id=1, source_target_pairs={{0,64},{1,65},{2,66},{3,67},{4,68},{5,69},{6,70},{7,71},{8,72},{9,... | collective-permute-start | bytes 1572872 | tf_op jit(solution)/shard_map/ppermute | solution.py:25
  38.6 14.3 %collective-permute-start.5 = (bf16[2048,128]{1,0:T(8,128)(2,1)S(1)}, bf16[2048,128]{1,0:T(8,128)(2,1)S(1)}, u32[]{:S(2)}, u32[]{:S(2)}) collective-permute-start(bf16[2048,128]{1,0:T(8,128)(2,1)S(1)} %collective-permute-done.4.refs_1_), channel_id=1, source_target_pairs={{0,66},{1,67},{2,64},{3,65},{4,70},{5,71},{6,68},{7,69},{8,74},{9,... | collective-permute-start | bytes 1572872 | tf_op jit(solution)/shard_map/ppermute | solution.py:25
  40.7 27.9 %collective-permute-start.18 = (bf16[2048,128]{1,0:T(8,128)(2,1)S(1)}, bf16[2048,128]{1,0:T(8,128)(2,1)S(1)}, u32[]{:S(2)}, u32[]{:S(2)}) collective-permute-start(bf16[2048,128]{1,0:T(8,128)(2,1)S(1)} %collective-permute-done.16.refs_5_), channel_id=1, source_target_pairs={{0,1},{1,0},{2,3},{3,2},{4,5},{5,4},{6,7},{7,6},{8,9},{9,8},{10,11... | collective-permute-start | bytes 1572872 | tf_op jit(solution)/shard_map/ppermute | solution.py:25
  42.5 46.8 %collective-permute-start = (bf16[2048,128]{1,0:T(8,128)(2,1)S(1)}, bf16[2048,128]{1,0:T(8,128)(2,1)S(1)}, u32[]{:S(2)}, u32[]{:S(2)}) collective-permute-start(bf16[2048,128]{1,0:T(8,128)(2,1)S(1)} %get-tuple-element.9.refs_2_), channel_id=1, source_target_pairs={{0,1},{1,0},{2,3},{3,2},{4,5},{5,4},{6,7},{7,6},{8,9},{9,8},{10,11... | collective-permute-start | bytes 1572872 | tf_op jit(solution)/shard_map/ppermute | solution.py:25
  42.6 46.8 %collective-permute-start.1 = (bf16[2048,128]{1,0:T(8,128)(2,1)S(1)}, bf16[2048,128]{1,0:T(8,128)(2,1)S(1)}, u32[]{:S(2)}, u32[]{:S(2)}) collective-permute-start(bf16[2048,128]{1,0:T(8,128)(2,1)S(1)} %get-tuple-element.10.refs_3_), channel_id=1, source_target_pairs={{0,1},{1,0},{2,3},{3,2},{4,5},{5,4},{6,7},{7,6},{8,9},{9,8},{10,11... | collective-permute-start | bytes 1572872 | tf_op jit(solution)/shard_map/ppermute | solution.py:25
  49.5 39.9 %collective-permute-start.6 = (bf16[2048,128]{1,0:T(8,128)(2,1)S(1)}, bf16[2048,128]{1,0:T(8,128)(2,1)S(1)}, u32[]{:S(2)}, u32[]{:S(2)}) collective-permute-start(bf16[2048,128]{1,0:T(8,128)(2,1)S(1)} %collective-permute-done.3.refs_6_), channel_id=1, source_target_pairs={{0,1},{1,0},{2,3},{3,2},{4,5},{5,4},{6,7},{7,6},{8,9},{9,8},{10,11... | collective-permute-start | bytes 1572872 | tf_op jit(solution)/shard_map/ppermute | solution.py:25
  52.9 36.5 %collective-permute-start.7 = (bf16[2048,128]{1,0:T(8,128)(2,1)S(1)}, bf16[2048,128]{1,0:T(8,128)(2,1)S(1)}, u32[]{:S(2)}, u32[]{:S(2)}) collective-permute-start(bf16[2048,128]{1,0:T(8,128)(2,1)S(1)} %collective-permute-done.5.refs_7_), channel_id=1, source_target_pairs={{0,1},{1,0},{2,3},{3,2},{4,5},{5,4},{6,7},{7,6},{8,9},{9,8},{10,11... | collective-permute-start | bytes 1572872 | tf_op jit(solution)/shard_map/ppermute | solution.py:25
  68.6 20.8 %collective-permute-start.12 = (bf16[512,128]{1,0:T(8,128)(2,1)S(1)}, bf16[512,128]{1,0:T(8,128)(2,1)S(1)}, u32[]{:S(2)}, u32[]{:S(2)}) collective-permute-start(bf16[512,128]{1,0:T(8,128)(2,1)S(1)} %bitcast.13), channel_id=1, source_target_pairs={{0,1},{1,0},{2,3},{3,2},{4,5},{5,4},{6,7},{7,6},{8,9},{9,8},{10,11... | collective-permute-start | bytes 393224 | tf_op jit(solution)/shard_map/ppermute | solution.py:25
  109.5 73.1 %copy-start = (bf16[2048,128]{1,0:T(8,128)(2,1)}, bf16[2048,128]{1,0:T(8,128)(2,1)S(1)}, u32[]{:S(2)}) copy-start(bf16[2048,128]{1,0:T(8,128)(2,1)S(1)} %get-tuple-element.11.refs_2_) | copy-start | bytes 1572868
  109.5 73.1 %copy-start.1 = (bf16[2048,128]{1,0:T(8,128)(2,1)}, bf16[2048,128]{1,0:T(8,128)(2,1)S(1)}, u32[]{:S(2)}) copy-start(bf16[2048,128]{1,0:T(8,128)(2,1)S(1)} %get-tuple-element.12.refs_3_) | copy-start | bytes 1572868
  110.7 4.9 %collective-permute-start.27 = (f32[512,128]{1,0:T(8,128)S(1)}, f32[512,128]{1,0:T(8,128)S(1)}, u32[]{:S(2)}, u32[]{:S(2)}) collective-permute-start(f32[512,128]{1,0:T(8,128)S(1)} %constant_dynamic-slice_fusion), channel_id=1, source_target_pairs={{0,1},{1,0},{2,3},{3,2},{4,5},{5,4},{6,7},{7,6},{8,9},{9,8},{10,11... | collective-permute-start | bytes 786440 | tf_op jit(solution)/shard_map/ppermute | solution.py:25
  111.5 13.4 %collective-permute-start.32 = (bf16[2048,128]{1,0:T(8,128)(2,1)S(1)}, bf16[2048,128]{1,0:T(8,128)(2,1)S(1)}, u32[]{:S(2)}, u32[]{:S(2)}) collective-permute-start(bf16[2048,128]{1,0:T(8,128)(2,1)S(1)} %get-tuple-element.11.refs_2_), channel_id=1, source_target_pairs={{0,64},{1,65},{2,66},{3,67},{4,68},{5,69},{6,70},{7,71},{8,72},{9,... | collective-permute-start | bytes 1572872 | tf_op jit(solution)/shard_map/ppermute | solution.py:25
  111.7 24.5 %collective-permute-start.23 = (bf16[2048,128]{1,0:T(8,128)(2,1)S(1)}, bf16[2048,128]{1,0:T(8,128)(2,1)S(1)}, u32[]{:S(2)}, u32[]{:S(2)}) collective-permute-start(bf16[2048,128]{1,0:T(8,128)(2,1)S(1)} %get-tuple-element.12.refs_3_), channel_id=1, source_target_pairs={{0,64},{1,65},{2,66},{3,67},{4,68},{5,69},{6,70},{7,71},{8,72},{9,... | collective-permute-start | bytes 1572872 | tf_op jit(solution)/shard_map/ppermute | solution.py:25
  113.0 25.1 %collective-permute-start.21 = (bf16[2048,128]{1,0:T(8,128)(2,1)S(1)}, bf16[2048,128]{1,0:T(8,128)(2,1)S(1)}, u32[]{:S(2)}, u32[]{:S(2)}) collective-permute-start(bf16[2048,128]{1,0:T(8,128)(2,1)S(1)} %get-tuple-element.11.refs_2_), channel_id=1, source_target_pairs={{0,66},{1,67},{2,64},{3,65},{4,70},{5,71},{6,68},{7,69},{8,74},{9,... | collective-permute-start | bytes 1572872 | tf_op jit(solution)/shard_map/ppermute | solution.py:25
  114.9 23.4 %collective-permute-start.35 = (bf16[2048,128]{1,0:T(8,128)(2,1)S(1)}, bf16[2048,128]{1,0:T(8,128)(2,1)S(1)}, u32[]{:S(2)}, u32[]{:S(2)}) collective-permute-start(bf16[2048,128]{1,0:T(8,128)(2,1)S(1)} %get-tuple-element.12.refs_3_), channel_id=1, source_target_pairs={{0,66},{1,67},{2,64},{3,65},{4,70},{5,71},{6,68},{7,69},{8,74},{9,... | collective-permute-start | bytes 1572872 | tf_op jit(solution)/shard_map/ppermute | solution.py:25
  117.3 10.9 %all-to-all-start.2 = ((f32[16,32,128]{2,1,0:T(8,128)}), f32[16,32,128]{2,1,0:T(8,128)S(1)}, u32[]{:S(2)}, u32[]{:S(2)}) async-start(f32[16,32,128]{2,1,0:T(8,128)} %bitcast.5), calls=%async_computation.2 | async-start | bytes 524288 | tf_op jit(solution)/shard_map/all_to_all | solution.py:383
  124.9 44.2 %copy-start.15 = (bf16[2048,128]{1,0:T(8,128)(2,1)}, bf16[2048,128]{1,0:T(8,128)(2,1)S(1)}, u32[]{:S(2)}) copy-start(bf16[2048,128]{1,0:T(8,128)(2,1)S(1)} %collective-permute-done.32.refs_0_) | copy-start | bytes 1572868
  124.9 18.2 %collective-permute-start.33 = (bf16[2048,128]{1,0:T(8,128)(2,1)S(1)}, bf16[2048,128]{1,0:T(8,128)(2,1)}, u32[]{:S(2)}, u32[]{:S(2)}) collective-permute-start(bf16[2048,128]{1,0:T(8,128)(2,1)S(1)} %collective-permute-done.32.refs_0_), channel_id=1, source_target_pairs={{0,1},{1,0},{2,3},{3,2},{4,5},{5,4},{6,7},{7,6},{8,9},{9,8},{10,11... | collective-permute-start | bytes 1572872 | tf_op jit(solution)/shard_map/ppermute | solution.py:25
  128.3 11.5 %collective-permute-start.28 = (f32[32,128]{1,0:T(8,128)S(1)}, f32[32,128]{1,0:T(8,128)S(1)}, u32[]{:S(2)}, u32[]{:S(2)}) collective-permute-start(f32[32,128]{1,0:T(8,128)S(1)} %reduce_sum.19), channel_id=1, source_target_pairs={{0,64},{1,65},{2,66},{3,67},{4,68},{5,69},{6,70},{7,71},{8,72},{9,... | collective-permute-start | bytes 49160 | tf_op jit(solution)/shard_map/ppermute | solution.py:25
  136.1 3.8 %collective-permute-start.29 = (f32[32,128]{1,0:T(8,128)S(1)}, f32[32,128]{1,0:T(8,128)S(1)}, u32[]{:S(2)}, u32[]{:S(2)}) collective-permute-start(f32[32,128]{1,0:T(8,128)S(1)} %reduce_sum.19), channel_id=1, source_target_pairs={{0,66},{1,67},{2,64},{3,65},{4,70},{5,71},{6,68},{7,69},{8,74},{9,... | collective-permute-start | bytes 49160 | tf_op jit(solution)/shard_map/ppermute | solution.py:25
  138.0 4.1 %collective-permute-start.30 = (f32[32,128]{1,0:T(8,128)S(1)}, f32[32,128]{1,0:T(8,128)S(1)}, u32[]{:S(2)}, u32[]{:S(2)}) collective-permute-start(f32[32,128]{1,0:T(8,128)S(1)} %reduce_sum.19), channel_id=1, source_target_pairs={{0,2},{1,3},{2,0},{3,1},{4,6},{5,7},{6,4},{7,5},{8,10},{9,11},{10,... | collective-permute-start | bytes 49160 | tf_op jit(solution)/shard_map/ppermute | solution.py:25
  138.2 7.5 %collective-permute-start.34 = (bf16[2048,128]{1,0:T(8,128)(2,1)S(1)}, bf16[2048,128]{1,0:T(8,128)(2,1)S(1)}, u32[]{:S(2)}, u32[]{:S(2)}) collective-permute-start(bf16[2048,128]{1,0:T(8,128)(2,1)S(1)} %collective-permute-done.23.refs_1_), channel_id=1, source_target_pairs={{0,1},{1,0},{2,3},{3,2},{4,5},{5,4},{6,7},{7,6},{8,9},{9,8},{10,11... | collective-permute-start | bytes 1572872 | tf_op jit(solution)/shard_map/ppermute | solution.py:25
  139.8 6.1 %collective-permute-start.36 = (bf16[2048,128]{1,0:T(8,128)(2,1)S(1)}, bf16[2048,128]{1,0:T(8,128)(2,1)S(1)}, u32[]{:S(2)}, u32[]{:S(2)}) collective-permute-start(bf16[2048,128]{1,0:T(8,128)(2,1)S(1)} %collective-permute-done.21.refs_4_), channel_id=1, source_target_pairs={{0,1},{1,0},{2,3},{3,2},{4,5},{5,4},{6,7},{7,6},{8,9},{9,8},{10,11... | collective-permute-start | bytes 1572872 | tf_op jit(solution)/shard_map/ppermute | solution.py:25
  139.9 11.8 %collective-permute-start.22 = (bf16[2048,128]{1,0:T(8,128)(2,1)S(1)}, bf16[2048,128]{1,0:T(8,128)(2,1)S(1)}, u32[]{:S(2)}, u32[]{:S(2)}) collective-permute-start(bf16[2048,128]{1,0:T(8,128)(2,1)S(1)} %collective-permute-done.21.refs_4_), channel_id=1, source_target_pairs={{0,64},{1,65},{2,66},{3,67},{4,68},{5,69},{6,70},{7,71},{8,72},{9,... | collective-permute-start | bytes 1572872 | tf_op jit(solution)/shard_map/ppermute | solution.py:25
  142.1 12.2 %collective-permute-start.24 = (bf16[2048,128]{1,0:T(8,128)(2,1)S(1)}, bf16[2048,128]{1,0:T(8,128)(2,1)S(1)}, u32[]{:S(2)}, u32[]{:S(2)}) collective-permute-start(bf16[2048,128]{1,0:T(8,128)(2,1)S(1)} %collective-permute-done.23.refs_1_), channel_id=1, source_target_pairs={{0,66},{1,67},{2,64},{3,65},{4,70},{5,71},{6,68},{7,69},{8,74},{9,... | collective-permute-start | bytes 1572872 | tf_op jit(solution)/shard_map/ppermute | solution.py:25
  143.1 24.3 %collective-permute-start.37 = (bf16[2048,128]{1,0:T(8,128)(2,1)S(1)}, bf16[2048,128]{1,0:T(8,128)(2,1)S(1)}, u32[]{:S(2)}, u32[]{:S(2)}) collective-permute-start(bf16[2048,128]{1,0:T(8,128)(2,1)S(1)} %collective-permute-done.35.refs_5_), channel_id=1, source_target_pairs={{0,1},{1,0},{2,3},{3,2},{4,5},{5,4},{6,7},{7,6},{8,9},{9,8},{10,11... | collective-permute-start | bytes 1572872 | tf_op jit(solution)/shard_map/ppermute | solution.py:25
  145.8 42.3 %collective-permute-start.19 = (bf16[2048,128]{1,0:T(8,128)(2,1)S(1)}, bf16[2048,128]{1,0:T(8,128)(2,1)S(1)}, u32[]{:S(2)}, u32[]{:S(2)}) collective-permute-start(bf16[2048,128]{1,0:T(8,128)(2,1)S(1)} %get-tuple-element.11.refs_2_), channel_id=1, source_target_pairs={{0,1},{1,0},{2,3},{3,2},{4,5},{5,4},{6,7},{7,6},{8,9},{9,8},{10,11... | collective-permute-start | bytes 1572872 | tf_op jit(solution)/shard_map/ppermute | solution.py:25
  145.9 42.3 %collective-permute-start.20 = (bf16[2048,128]{1,0:T(8,128)(2,1)S(1)}, bf16[2048,128]{1,0:T(8,128)(2,1)S(1)}, u32[]{:S(2)}, u32[]{:S(2)}) collective-permute-start(bf16[2048,128]{1,0:T(8,128)(2,1)S(1)} %get-tuple-element.12.refs_3_), channel_id=1, source_target_pairs={{0,1},{1,0},{2,3},{3,2},{4,5},{5,4},{6,7},{7,6},{8,9},{9,8},{10,11... | collective-permute-start | bytes 1572872 | tf_op jit(solution)/shard_map/ppermute | solution.py:25
  151.7 36.5 %collective-permute-start.25 = (bf16[2048,128]{1,0:T(8,128)(2,1)S(1)}, bf16[2048,128]{1,0:T(8,128)(2,1)S(1)}, u32[]{:S(2)}, u32[]{:S(2)}) collective-permute-start(bf16[2048,128]{1,0:T(8,128)(2,1)S(1)} %collective-permute-done.22.refs_6_), channel_id=1, source_target_pairs={{0,1},{1,0},{2,3},{3,2},{4,5},{5,4},{6,7},{7,6},{8,9},{9,8},{10,11... | collective-permute-start | bytes 1572872 | tf_op jit(solution)/shard_map/ppermute | solution.py:25
  154.3 33.9 %collective-permute-start.26 = (bf16[2048,128]{1,0:T(8,128)(2,1)S(1)}, bf16[2048,128]{1,0:T(8,128)(2,1)S(1)}, u32[]{:S(2)}, u32[]{:S(2)}) collective-permute-start(bf16[2048,128]{1,0:T(8,128)(2,1)S(1)} %collective-permute-done.24.refs_7_), channel_id=1, source_target_pairs={{0,1},{1,0},{2,3},{3,2},{4,5},{5,4},{6,7},{7,6},{8,9},{9,8},{10,11... | collective-permute-start | bytes 1572872 | tf_op jit(solution)/shard_map/ppermute | solution.py:25
  167.4 20.7 %collective-permute-start.31 = (bf16[512,128]{1,0:T(8,128)(2,1)S(1)}, bf16[512,128]{1,0:T(8,128)(2,1)S(1)}, u32[]{:S(2)}, u32[]{:S(2)}) collective-permute-start(bf16[512,128]{1,0:T(8,128)(2,1)S(1)} %bitcast.11), channel_id=1, source_target_pairs={{0,1},{1,0},{2,3},{3,2},{4,5},{5,4},{6,7},{7,6},{8,9},{9,8},{10,11... | collective-permute-start | bytes 393224 | tf_op jit(solution)/shard_map/ppermute | solution.py:25
  (31 other events, 468.6 us)

commit v4 on v2

v4 whole, which is shorter than its diff:
```python
import jax
import jax.numpy as jnp
from jax import lax
from jax.experimental import pallas as pl
from jax.experimental.pallas import tpu as pltpu
from jax.sharding import PartitionSpec as P


BLK = 256
NV = 128
NBLK = 8
APPS = 2
AXES = ("wide", "narrow")
BF16 = jnp.bfloat16
F32 = jnp.float32
MIB = 1 << 20


VMEM_SPEC = pl.BlockSpec(memory_space=pltpu.VMEM)
SMEM_SPEC = pl.BlockSpec(memory_space=pltpu.SMEM)
ANY_SPEC = pl.BlockSpec(memory_space=pl.ANY)


def toggled(array, mask):
    return lax.ppermute(array, AXES, [(i, i ^ mask) for i in range(lax.axis_size(AXES))])


def interleave(x, y, scratch):
    scratch[pl.ds(0, x.shape[0], stride=2), :] = x
    scratch[pl.ds(1, x.shape[0], stride=2), :] = y
    return scratch[...].astype(BF16)


def in_hbm(*arrays):
    return [pltpu.with_memory_space_constraint(a, pltpu.HBM) for a in arrays]


def block_rows(b, size=BLK):
    return pl.ds(pl.multiple_of(b * size, size), size)


def split_matrix():
    row = lax.broadcasted_iota(jnp.int32, (BLK, BLK), 0)
    col = lax.broadcasted_iota(jnp.int32, (BLK, BLK), 1)
    half = BLK // 2
    hit = (col == 2 * row) | (col == 2 * (row - half) + 1)
    return jnp.where(hit, 1.0, 0.0).astype(F32).astype(BF16)


def split_block(flat, base, block, out, select):
    half = BLK // 2
    pair = jnp.concatenate([flat[pl.ds(base, BLK), :], flat[pl.ds(base + BLK, BLK), :]], axis=1)
    parts = jnp.dot(select, pair, preferred_element_type=F32).astype(BF16)
    out[block, 0:half, 0:NV] = parts[0:half, 0:NV]
    out[block, half:BLK, 0:NV] = parts[0:half, NV:]
    out[block, 0:half, NV:] = parts[half:, 0:NV]
    out[block, half:BLK, NV:] = parts[half:, NV:]


def pack_body(x_hbm, y_hbm, low_ref, high_ref, x, y, scratch, sems):
    size = scratch.shape[0] // 2
    parts = x.shape[0] // size
    loads = []
    for p in range(parts):
        for t, (source, target) in enumerate(((x_hbm, x), (y_hbm, y))):
            rows = pl.ds(p * size, size)
            loads.append(pltpu.make_async_copy(source.at[rows], target.at[rows], sems.at[2 * p + t]))
            loads[-1].start()
    for p in range(parts):
        loads[2 * p].wait()
        loads[2 * p + 1].wait()
        rows = pl.ds(p * size, size)
        out, place = (low_ref, p) if p < parts // 2 else (high_ref, p - parts // 2)
        out[pl.ds(place * 2 * size, 2 * size), :] = interleave(x[rows, :], y[rows, :], scratch)


def pack(x, y):
    rows = x.shape[0]
    parts = 4
    return pl.pallas_call(
        pack_body,
        in_specs=[ANY_SPEC, ANY_SPEC],
        out_specs=[VMEM_SPEC, VMEM_SPEC],
        out_shape=[jax.ShapeDtypeStruct((rows, NV), BF16)] * 2,
        scratch_shapes=[
            pltpu.VMEM((rows, NV), F32),
            pltpu.VMEM((rows, NV), F32),
            pltpu.VMEM((2 * rows // parts, NV), F32),
            pltpu.SemaphoreType.DMA((2 * parts,)),
        ],
        compiler_params=pltpu.CompilerParams(vmem_limit_bytes=8 * MIB),
        name="pack",
    )(*in_hbm(x, y))


def project_body(x_hbm, y_hbm, basis_hbm, out_ref, x, y, basis, summed, sems):
    copies = []
    for t, (source, target) in enumerate(((x_hbm, x), (y_hbm, y), (basis_hbm, basis))):
        copies.append(pltpu.make_async_copy(source, target, sems.at[t]))
        copies[-1].start()
    copies[0].wait()
    copies[1].wait()
    rows = x.shape[0]
    for b in range(rows // BLK):
        part = pl.ds(b * BLK, BLK)
        summed[:, b * BLK : (b + 1) * BLK] = (x[part, :] + y[part, :]).T.astype(BF16)
    copies[2].wait()
    rank = basis.shape[1]
    wide = 2 * BLK
    for r in range(rank // wide):
        value = jnp.dot(summed[...], basis[:, r * wide : (r + 1) * wide], preferred_element_type=F32)
        for q in range(wide // NV):
            row = r * wide + q * NV
            out_ref[row : row + NV, :] = value[:, q * NV : (q + 1) * NV].T


def project(x, y, basis):
    rows, rank = basis.shape
    return pl.pallas_call(
        project_body,
        in_specs=[ANY_SPEC] * 3,
        out_specs=VMEM_SPEC,
        out_shape=pltpu.HBM((rank, NV), F32),
        scratch_shapes=[
            pltpu.VMEM((rows, NV), F32),
            pltpu.VMEM((rows, NV), F32),
            pltpu.VMEM((rows, rank), BF16),
            pltpu.VMEM((NV, rows), BF16),
            pltpu.SemaphoreType.DMA((3,)),
        ],
        compiler_params=pltpu.CompilerParams(vmem_limit_bytes=12 * MIB),
        name="project",
    )(*in_hbm(x, y, basis))


def list_product(kernel, columns, list_ref, b):
    left = jnp.concatenate([kernel[b, n] for n in range(NBLK)], axis=1)
    right = jnp.concatenate([columns[list_ref[b, n]] for n in range(NBLK)], axis=0)
    return jnp.dot(left, right, preferred_element_type=F32)


def load_patch(slot, chunks, flat, sems):
    rows = chunks[0].shape[0]
    copies = []
    for k, chunk in enumerate(chunks):
        start = pl.multiple_of((slot ^ (k // 2)) * 2 * rows + (k % 2) * rows, rows)
        copies.append(pltpu.make_async_copy(chunk, flat.at[pl.ds(start, rows)], sems.at[k]))
        copies[-1].start()
    return copies


def split_all(flat, first, out, select):
    def split(block, carry):
        split_block(flat, pl.multiple_of(block * 2 * BLK, 2 * BLK), first + block, out, select)
        return carry

    lax.fori_loop(0, flat.shape[0] // (2 * BLK), split, 0, unroll=8)


def own_body(slot_ref, *refs):
    chunks = refs[:4]
    out_ref, flat, sems = refs[4:]
    copies = load_patch(slot_ref[0] & 1, chunks, flat, sems)
    select = split_matrix()
    for copy in copies:
        copy.wait()
    split_all(flat, 0, out_ref, select)


def own_columns(slot, chunks):
    rows = chunks[0].shape[0]
    return pl.pallas_call(
        own_body,
        in_specs=[SMEM_SPEC] + [ANY_SPEC] * 4,
        out_specs=VMEM_SPEC,
        out_shape=pltpu.HBM((2 * rows // BLK, BLK, 2 * NV), BF16),
        scratch_shapes=[pltpu.VMEM((4 * rows, NV), BF16), pltpu.SemaphoreType.DMA((4,))],
        compiler_params=pltpu.CompilerParams(vmem_limit_bytes=8 * MIB),
        name="own_columns",
    )(slot, *in_hbm(*chunks))


def mirror_body(slot_ref, partner_ref, list_ref, *refs):
    chunks = refs[:8]
    kernel_hbm, out_ref, source, gathered, columns, kernel, sems, kernel_sems = refs[8:]
    copies = load_patch(slot_ref[0], chunks, source.reshape(2 * source.shape[0], NV), sems)
    blocks = kernel.shape[0]
    loads = [pltpu.make_async_copy(kernel_hbm.at[b], kernel.at[b], kernel_sems.at[b]) for b in range(blocks)]
    for load in loads:
        load.start()
    select = split_matrix()
    for copy in copies:
        copy.wait()
    unroll = 128

    def gather(step, carry):
        base = step * unroll
        for u in range(unroll):
            gathered[base + u] = source[partner_ref[0, base + u]]
        return carry

    lax.fori_loop(0, source.shape[0] // unroll, gather, 0)
    split_all(gathered.reshape(2 * gathered.shape[0], NV), 0, columns, select)
    for load in loads:
        load.wait()

    def product(b, carry):
        out_ref[b] = list_product(kernel, columns, list_ref, b)
        return carry

    lax.fori_loop(0, blocks, product, 0, unroll=2)


def mirror_product(slot, partner, indices, chunks, kernel):
    patch = partner.shape[1]
    blocks = kernel.shape[0]
    return pl.pallas_call(
        mirror_body,
        in_specs=[SMEM_SPEC] * 3 + [ANY_SPEC] * 9,
        out_specs=VMEM_SPEC,
        out_shape=jax.ShapeDtypeStruct((blocks, BLK, 2 * NV), F32),
        scratch_shapes=[
            pltpu.VMEM((patch, 2, NV), BF16),
            pltpu.VMEM((patch, 2, NV), BF16),
            pltpu.VMEM((patch // BLK, BLK, 2 * NV), BF16),
            pltpu.VMEM(kernel.shape, BF16),
            pltpu.SemaphoreType.DMA((8,)),
            pltpu.SemaphoreType.DMA((blocks,)),
        ],
        compiler_params=pltpu.CompilerParams(vmem_limit_bytes=24 * MIB),
        name="mirror_product",
    )(slot, partner, indices, *in_hbm(*chunks, kernel))


def column_of(row):
    return jnp.broadcast_to(row, (NV, NV)).T


def finish_body(last, slot_ref, list_ref, *refs):
    chunks = refs[:4]
    own_hbm, x_hbm, y_hbm, energy_ref, shift_ref, kernel_hbm, basis_hbm, weight_ref, mirror_ref = refs[4:13]
    rest = refs[13:]
    if last:
        next_x_hbm, next_y_hbm = rest[:2]
        rest = rest[2:]
    else:
        next_x_hbm, next_y_hbm, low_ref, high_ref = rest[:4]
        rest = rest[4:]
    flat, columns, kernel, basis, x, y, levels, scratch, chunk_sems, sems, save_sems = rest
    blocks = kernel.shape[0]
    core = slot_ref[0] & 1
    copies = load_patch(core, chunks, flat, chunk_sems)
    count = own_hbm.shape[0]
    own_first = (slot_ref[0] // 2) * count
    extra = [pltpu.make_async_copy(own_hbm, columns.at[pl.ds(own_first, count)], chunk_sems.at[4])]
    for copy in extra:
        copy.start()

    def load(b, t):
        if t == 0:
            return pltpu.make_async_copy(kernel_hbm.at[b], kernel.at[b], sems.at[0, b])
        source, target = ((basis_hbm, basis), (x_hbm, x), (y_hbm, y))[t - 1]
        part = block_rows(b)
        return pltpu.make_async_copy(source.at[part], target.at[part], sems.at[t, b])

    def save(b, t):
        source, target = ((x, next_x_hbm), (y, next_y_hbm))[t]
        part = block_rows(b)
        return pltpu.make_async_copy(source.at[part], target.at[part], save_sems.at[t, b])

    for b in range(blocks):
        for t in range(4):
            load(b, t).start()
    half = BLK // 2
    for b in range(blocks):
        row = energy_ref[b]
        levels[b * BLK : b * BLK + half, :] = column_of(row[:, 0:half])
        levels[b * BLK + half : (b + 1) * BLK, :] = column_of(row[:, half:])
    for copy in copies:
        copy.wait()
    split_all(flat, (1 - slot_ref[0] // 2) * count, columns, split_matrix())
    for copy in extra:
        copy.wait()
    for b in range(blocks):
        for t in range(4):
            load(b, t).wait()
    shifts = shift_ref[...]

    def step(b):
        part = block_rows(b)
        mirrored = mirror_ref[b]
        exchange = jnp.dot(basis[part, :], weight_ref[...], preferred_element_type=F32)
        direct = list_product(kernel, columns, list_ref, b)
        level = levels[part, :]
        next_x = x[part, :] + (direct[:, :NV] + mirrored[:, NV:] + exchange) / (level - shifts)
        next_y = y[part, :] + (direct[:, NV:] + mirrored[:, :NV] + exchange) / (level + shifts)
        x[part, :] = next_x
        y[part, :] = next_y
        for t in range(2):
            save(b, t).start()
        return (next_x, next_y)

    if last:
        lax.fori_loop(0, blocks, lambda b, carry: (step(b), carry)[1], 0, unroll=2)
    else:
        for place, out_ref in enumerate((low_ref, high_ref)):
            base = place * (blocks // 2)

            def pair(b, carry):
                next_x, next_y = step(base + b)
                out_ref[block_rows(b, 2 * BLK), :] = interleave(next_x, next_y, scratch.at[b % 2])
                return carry

            lax.fori_loop(0, blocks // 2, pair, 0, unroll=2)
    for b in range(blocks):
        for t in range(2):
            save(b, t).wait()


def finish(last, slot, indices, chunks, own, x, y, energy, shift, kernel, basis, weights, mirrored):
    rows, _ = basis.shape
    blocks = kernel.shape[0]
    patch = 4 * rows
    out_specs = [ANY_SPEC, ANY_SPEC]
    out_shape = [pltpu.HBM((rows, NV), F32)] * 2
    if not last:
        out_specs += [VMEM_SPEC] * 2
        out_shape += [jax.ShapeDtypeStruct((rows, NV), BF16)] * 2

    def body(*refs):
        finish_body(last, *refs)

    return pl.pallas_call(
        body,
        in_specs=[SMEM_SPEC] * 2 + [ANY_SPEC] * 7 + [VMEM_SPEC] * 2 + [ANY_SPEC] * 2 + [VMEM_SPEC] * 2,
        out_specs=out_specs,
        out_shape=out_shape,
        scratch_shapes=[
            pltpu.VMEM((patch, NV), BF16),
            pltpu.VMEM((patch // BLK, BLK, 2 * NV), BF16),
            pltpu.VMEM(kernel.shape, BF16),
            pltpu.VMEM(basis.shape, BF16),
            pltpu.VMEM((rows, NV), F32),
            pltpu.VMEM((rows, NV), F32),
            pltpu.VMEM((rows, NV), F32),
            pltpu.VMEM((2, 2 * BLK, NV), F32),
            pltpu.SemaphoreType.DMA((8,)),
            pltpu.SemaphoreType.DMA((4, blocks)),
            pltpu.SemaphoreType.DMA((2, blocks)),
        ],
        compiler_params=pltpu.CompilerParams(vmem_limit_bytes=32 * MIB),
        name="finish_last" if last else "finish",
    )(slot, indices, *in_hbm(*chunks, own, x, y), energy, shift, *in_hbm(kernel, basis), weights, mirrored)


def total_weights(partial):
    size = lax.axis_size(AXES)
    rank, vectors = partial.shape
    part = rank // size
    pieces = lax.all_to_all(partial.reshape(size, part, vectors), AXES, 0, 0, tiled=True)
    own = jnp.sum(pieces.astype(F32), axis=0).astype(BF16)
    spread = lax.all_to_all(jnp.broadcast_to(own[None], (size, part, vectors)), AXES, 0, 0, tiled=True)
    return spread.reshape(rank, vectors)


def on_device(x, y, energy, shift, res_kernel, res_list, cp_kernel, cp_list, partner, basis):
    size = lax.axis_size(AXES)
    narrow = lax.axis_size("narrow")
    near = size // 2
    far = near | (narrow // 2)
    slot = lax.axis_index("narrow").astype(jnp.int32).reshape(1)
    blocks = res_kernel.shape[0]
    levels = energy.reshape(blocks, 1, BLK)
    shifts = shift.reshape(1, NV)
    for app in range(APPS):
        last = app == APPS - 1
        if app == 0:
            low, high = pack(x, y)
        far_low = toggled(low, far)
        near_high = toggled(high, near)
        weights = total_weights(project(x, y, basis))
        far_high = toggled(high, far)
        near_low = toggled(low, near)
        own = [toggled(low, 1), toggled(high, 1)]
        across = [toggled(far_low, near), toggled(near_high, far)]
        near_swap = [toggled(near_low, 1), toggled(near_high, 1)]
        far_swap = [toggled(far_low, 1), toggled(far_high, 1)]
        mirror_chunks = [near_low, near_high] + near_swap + [far_low, far_high] + far_swap
        own_half = own_columns(slot, [low, high] + own)
        across += [toggled(c, 1) for c in across]
        mirrored = mirror_product(slot, partner, cp_list, mirror_chunks, cp_kernel)
        out = finish(last, slot, res_list, across, own_half, x, y, levels, shifts, res_kernel, basis, weights, mirrored)
        if last:
            return tuple(out)
        x, y, low, high = out


def solution(mesh):
    return jax.shard_map(
        on_device,
        mesh=mesh,
        in_specs=(
            P(AXES, None),
            P(AXES, None),
            P(AXES),
            P(),
            P(AXES, None, None, None),
            P(AXES, None),
            P(AXES, None, None, None),
            P(AXES, None),
            P("wide", None),
            P(AXES, None),
        ),
        out_specs=(P(AXES, None), P(AXES, None)),
        check_vma=False,
    )
```

time: 217 us -> 201 us (0.926)
  blocking collectives: 39.6 us -> 0 us
  starting transfers between devices: 45.8 us -> 62.5 us
  Pallas kernels: 77.6 us -> 80.6 us
  local copies, waits for them, and re-layouts: 1.59 us -> 3.89 us
    all_to_all x2 -> x0, blocking collectives: 39.6 us -> none  [total_weights(): lax.all_to_all(partial.reshape(size, part, vectors), AXES, 0, 0, tiled=True)]
    all_to_all x0 -> x2, waiting for transfers between devices: none -> 22.8 us  [total_weights(): lax.all_to_all(partial.reshape(size, part, vectors), AXES, 0, 0, tiled=True)]
    ppermute x28, waiting for transfers between devices: 50.5 us -> 29 us  [toggled(): lax.ppermute(array, AXES, [(i, i ^ mask) for i in range(lax.axis_size(AXE...]
    all_to_all x0 -> x2, starting transfers between devices: none -> 19.6 us  [total_weights(): lax.all_to_all(partial.reshape(size, part, vectors), AXES, 0, 0, tiled=True)]
    pallas_call x1 -> x2, Pallas kernels: 4.84 us -> 8.97 us  [project(): pl.pallas_call(project_body, in_specs=[ANY_SPEC] * 3, out_specs=VMEM_SPEC...]
    ppermute x28, starting transfers between devices: 36.8 us -> 33.6 us  [toggled(): lax.ppermute(array, AXES, [(i, i ^ mask) for i in range(lax.axis_size(AXE...]
    unnamed x42 -> x40, local copies, waits for them, and re-layouts: 0.1 us -> 2.41 us
  transfers between devices with their start and end apart: 30 -> 32, of which waited for: 8 -> 6; matrix products, arithmetic and copies ran while one was open for 1% -> 1% of each run, Pallas kernels for 20% -> 27%
where the time goes in v4:
time: 201 us; the launch traced here: 200 us
  Pallas kernels  80.6 us (40%)
  starting transfers between devices  62.5 us (31%)
  waiting for transfers between devices  51.9 us (26%)
  local copies, waits for them, and re-layouts  3.89 us (2%)
    pallas_call x2, Pallas kernels, mirror_product(): pl.pallas_call(mirror_body, in_specs=[SMEM_SPEC] * 3 + [ANY_SPEC] * 9, ou...  36.6 us
    ppermute x28, starting transfers between devices, toggled(): lax.ppermute(array, AXES, [(i, i ^ mask) for i in range(lax.axis_size(AXE...  33.6 us
    ppermute x28, waiting for transfers between devices, toggled(): lax.ppermute(array, AXES, [(i, i ^ mask) for i in range(lax.axis_size(AXE...  29 us
    pallas_call x2, Pallas kernels, finish(): pl.pallas_call(body, in_specs=[SMEM_SPEC] * 2 + [ANY_SPEC] * 7 + [VMEM_SP...  25.9 us
    all_to_all x2, waiting for transfers between devices, total_weights(): lax.all_to_all(partial.reshape(size, part, vectors), AXES, 0, 0, tiled=True)  22.8 us
    all_to_all x2, starting transfers between devices, total_weights(): lax.all_to_all(partial.reshape(size, part, vectors), AXES, 0, 0, tiled=True)  19.6 us
    all_to_all x2, starting transfers between devices, total_weights(): lax.all_to_all(jnp.broadcast_to(own[None], (size, part, vectors)), AXES,...  9.26 us
    pallas_call x2, Pallas kernels, project(): pl.pallas_call(project_body, in_specs=[ANY_SPEC] * 3, out_specs=VMEM_SPEC...  8.97 us
  transfers between devices with their start and end apart: 32, of which 6 were waited for; matrix products, arithmetic and copies ran while one was open for 1% of the time, Pallas kernels for 27%

profile of v4, /device:TPU:1, one launch (start us, length us, event | category | flops | bytes accessed | tf_op | source)
XLA Modules:
  0.0 200.4 jit_solution(9335417679665814175)
XLA Ops:
  0.6 1.6 pack.1
  2.3 2.2 %collective-permute-start.2 = (bf16[2048,128]{1,0:T(8,128)(2,1)S(1)}, bf16[2048,128]{1,0:T(8,128)(2,1)S(1)}, u32[]{:S(2)}, u32[]{:S(2)}) collective-permute-start(bf16[2048,128]{1,0:T(8,128)(2,1)S(1)} %get-tuple-element.9.refs_1_), channel_id=1, source_target_pairs={{0,64},{1,65},{2,66},{3,67},{4,68},{5,69},{6,70},{7,71},{8,72},{9,... | collective-permute-start | bytes 1572872 | tf_op jit(solution)/shard_map/ppermute | solution.py:25
  4.5 1.9 collective-permute-start
  6.4 0.8 collective-permute-start.11
  7.2 1.5 collective-permute-start.6
  8.7 7.1 %collective-permute-done.2.refs_1_ = bf16[2048,128]{1,0:T(8,128)(2,1)S(1)} collective-permute-done((bf16[2048,128]{1,0:T(8,128)(2,1)S(1)}, bf16[2048,128]{1,0:T(8,128)(2,1)S(1)}, u32[]{:S(2)}, u32[]{:S(2)}) %collective-permute-start.2) | collective-permute-done | bytes 524320 | tf_op jit(solution)/shard_map/ppermute | solution.py:25
  15.8 2.8 %collective-permute-start.7 = (bf16[2048,128]{1,0:T(8,128)(2,1)S(1)}, bf16[2048,128]{1,0:T(8,128)(2,1)}, u32[]{:S(2)}, u32[]{:S(2)}) collective-permute-start(bf16[2048,128]{1,0:T(8,128)(2,1)S(1)} %get-tuple-element.9.refs_1_), channel_id=1, source_target_pairs={{0,1},{1,0},{2,3},{3,2},{4,5},{5,4},{6,7},{7,6},{8,9},{9,8},{10,11... | collective-permute-start | bytes 1572872 | tf_op jit(solution)/shard_map/ppermute | solution.py:25
  18.6 2.9 %collective-permute-start.10 = (bf16[2048,128]{1,0:T(8,128)(2,1)S(1)}, bf16[2048,128]{1,0:T(8,128)(2,1)}, u32[]{:S(2)}, u32[]{:S(2)}) collective-permute-start(bf16[2048,128]{1,0:T(8,128)(2,1)S(1)} %collective-permute-done.2.refs_1_), channel_id=1, source_target_pairs={{0,1},{1,0},{2,3},{3,2},{4,5},{5,4},{6,7},{7,6},{8,9},{9,8},{10,11... | collective-permute-start | bytes 1572872 | tf_op jit(solution)/shard_map/ppermute | solution.py:25
  21.5 8.0 %collective-permute-done.11.refs_5_ = bf16[2048,128]{1,0:T(8,128)(2,1)S(1)} collective-permute-done((bf16[2048,128]{1,0:T(8,128)(2,1)S(1)}, bf16[2048,128]{1,0:T(8,128)(2,1)S(1)}, u32[]{:S(2)}, u32[]{:S(2)}) %collective-permute-start.11) | collective-permute-done | bytes 524320 | tf_op jit(solution)/shard_map/ppermute | solution.py:25
  29.5 2.0 collective-permute-start.3
  31.5 4.5 %project.2 = f32[1024,128]{1,0:T(8,128)} custom-call(f32[2048,128]{1,0:T(8,128)} %refs_7_.1, f32[2048,128]{1,0:T(8,128)} %refs_8_.4, bf16[2048,1024]{1,0:T(8,128)(2,1)} %refs_12_.3), custom_call_target="tpu_custom_call" | custom-call | tf_op jit(solution)/shard_map/project/pallas_call | solution.py:119
  36.0 10.7 %all-to-all-start = ((f32[128,8,128]{2,1,0:T(8,128)}), f32[128,8,128]{2,1,0:T(8,128)S(1)}, u32[]{:S(2)}, u32[]{:S(2)}) async-start(f32[128,8,128]{2,1,0:T(8,128)} %bitcast.13), calls=%async_computation | async-start | bytes 1048576 | tf_op jit(solution)/shard_map/all_to_all | solution.py:360
  46.7 1.1 collective-permute-start.12
  47.9 0.1 collective-permute-start.13
  48.0 0.4 collective-permute-start.9
  48.5 0.4 collective-permute-start.5
  48.9 11.4 %all-to-all-done = f32[128,8,128]{2,1,0:T(8,128)S(1)} async-done(((f32[128,8,128]{2,1,0:T(8,128)}), f32[128,8,128]{2,1,0:T(8,128)S(1)}, u32[]{:S(2)}, u32[]{:S(2)}) %all-to-all-start) | async-done | bytes 524320 | tf_op jit(solution)/shard_map/all_to_all | solution.py:360
  60.4 0.1 reduce_sum.18
  60.5 0.7 broadcast_in_dim.4
  61.2 4.6 %all-to-all-start.1 = ((bf16[128,8,128]{2,1,0:T(8,128)(2,1)}), bf16[128,8,128]{2,1,0:T(8,128)(2,1)S(1)}, u32[]{:S(2)}, u32[]{:S(2)}) async-start(bf16[128,8,128]{2,1,0:T(8,128)(2,1)} %broadcast_in_dim.4), calls=%async_computation.1 | async-start | bytes 524288 | tf_op jit(solution)/shard_map/all_to_all | solution.py:362
  65.9 3.8 %own_columns.2.refs_6_ = bf16[16,256,256]{2,1,0:T(8,128)(2,1)} custom-call(s32[1]{0:T(128)} %bitcast.slot_ref.refs_0_, bf16[2048,128]{1,0:T(8,128)(2,1)} %copy-done.2, bf16[2048,128]{1,0:T(8,128)(2,1)} %copy-done.3, bf16[2048,128]{1,0:T(8,128)(2,1)} %collective-permute-done.6.refs_2_, bf16[2048,128]{1,0:T(8,128)(2,1)} %collective-permute-done.7.refs_3_), custom_call_target="tpu_custom_call" | custom-call | tf_op jit(solution)/shard_map/own_columns/pallas_call | solution.py:172
  69.8 0.8 copy-done.17
  70.5 18.3 %mirror_product.2.refs_14_ = f32[8,256,256]{2,1,0:T(8,128)S(1)} custom-call(s32[1]{0:T(128)} %bitcast.slot_ref.refs_0_, s32[1,8192]{1,0:T(1,128)S(1)} %copy-done.4, s32[8,8]{1,0:T(8,128)S(1)} %copy-done.6, bf16[2048,128]{1,0:T(8,128)(2,1)} %copy-done.14, bf16[2048,128]{1,0:T(8,128)(2,1)} %copy-done.9, bf16[2048,128]{1,0:T(8,128)(2,1)} %collective-permute-done.9.refs_2_, ...), custom_call_target="tpu_custom_call" | custom-call | tf_op jit(solution)/shard_map/mirror_product/pallas_call | solution.py:217
  88.9 13.1 %finish.1 = (f32[2048,128]{1,0:T(8,128)}, f32[2048,128]{1,0:T(8,128)}, bf16[2048,128]{1,0:T(8,128)(2,1)S(1)}, bf16[2048,128]{1,0:T(8,128)(2,1)S(1)}) custom-call(s32[1]{0:T(128)} %bitcast.slot_ref.refs_0_, s32[8,8]{1,0:T(8,128)S(1)} %copy-done.7, bf16[2048,128]{1,0:T(8,128)(2,1)} %collective-permute-done.1.refs_2_, ...), custom_call_target="tpu_custom_call" | custom-call | tf_op jit(solution)/shard_map/finish/pallas_call | solution.py:333
  102.0 1.4 collective-permute-start.22
  103.5 2.6 %collective-permute-start.14 = (bf16[2048,128]{1,0:T(8,128)(2,1)S(1)}, bf16[2048,128]{1,0:T(8,128)(2,1)S(1)}, u32[]{:S(2)}, u32[]{:S(2)}) collective-permute-start(bf16[2048,128]{1,0:T(8,128)(2,1)S(1)} %get-tuple-element.10.refs_0_), channel_id=1, source_target_pairs={{0,66},{1,67},{2,64},{3,65},{4,70},{5,71},{6,68},{7,69},{8,74},{9,... | collective-permute-start | bytes 1572872 | tf_op jit(solution)/shard_map/ppermute | solution.py:25
  106.2 2.2 %collective-permute-start.20 = (bf16[2048,128]{1,0:T(8,128)(2,1)S(1)}, bf16[2048,128]{1,0:T(8,128)(2,1)}, u32[]{:S(2)}, u32[]{:S(2)}) collective-permute-start(bf16[2048,128]{1,0:T(8,128)(2,1)S(1)} %get-tuple-element.10.refs_0_), channel_id=1, source_target_pairs={{0,1},{1,0},{2,3},{3,2},{4,5},{5,4},{6,7},{7,6},{8,9},{9,8},{10,11... | collective-permute-start | bytes 1572872 | tf_op jit(solution)/shard_map/ppermute | solution.py:25
  108.4 6.1 %collective-permute-done.22.refs_0_ = bf16[2048,128]{1,0:T(8,128)(2,1)S(1)} collective-permute-done((bf16[2048,128]{1,0:T(8,128)(2,1)S(1)}, bf16[2048,128]{1,0:T(8,128)(2,1)S(1)}, u32[]{:S(2)}, u32[]{:S(2)}) %collective-permute-start.22) | collective-permute-done | bytes 524320 | tf_op jit(solution)/shard_map/ppermute | solution.py:25
  114.5 3.5 %collective-permute-start.21 = (bf16[2048,128]{1,0:T(8,128)(2,1)S(1)}, bf16[2048,128]{1,0:T(8,128)(2,1)}, u32[]{:S(2)}, u32[]{:S(2)}) collective-permute-start(bf16[2048,128]{1,0:T(8,128)(2,1)S(1)} %get-tuple-element.11.refs_1_), channel_id=1, source_target_pairs={{0,1},{1,0},{2,3},{3,2},{4,5},{5,4},{6,7},{7,6},{8,9},{9,8},{10,11... | collective-permute-start | bytes 1572872 | tf_op jit(solution)/shard_map/ppermute | solution.py:25
  117.9 7.8 %collective-permute-done.16.refs_1_ = bf16[2048,128]{1,0:T(8,128)(2,1)S(1)} collective-permute-done((bf16[2048,128]{1,0:T(8,128)(2,1)S(1)}, bf16[2048,128]{1,0:T(8,128)(2,1)S(1)}, u32[]{:S(2)}, u32[]{:S(2)}) %collective-permute-start.16) | collective-permute-done | bytes 524320 | tf_op jit(solution)/shard_map/ppermute | solution.py:25
  125.7 1.9 collective-permute-start.23
  127.7 1.4 collective-permute-start.15
  129.0 2.1 %collective-permute-start.17 = (bf16[2048,128]{1,0:T(8,128)(2,1)S(1)}, bf16[2048,128]{1,0:T(8,128)(2,1)}, u32[]{:S(2)}, u32[]{:S(2)}) collective-permute-start(bf16[2048,128]{1,0:T(8,128)(2,1)S(1)} %collective-permute-done.16.refs_1_), channel_id=1, source_target_pairs={{0,66},{1,67},{2,64},{3,65},{4,70},{5,71},{6,68},{7,69},{8,74},{9,... | collective-permute-start | bytes 1572872 | tf_op jit(solution)/shard_map/ppermute | solution.py:25
  131.2 4.5 %project.3 = f32[1024,128]{1,0:T(8,128)} custom-call(f32[2048,128]{1,0:T(8,128)} %get-tuple-element.12.x_hbm.refs_7_, f32[2048,128]{1,0:T(8,128)} %get-tuple-element.13.y_hbm.refs_8_, bf16[2048,1024]{1,0:T(8,128)(2,1)} %refs_12_.3), custom_call_target="tpu_custom_call" | custom-call | tf_op jit(solution)/shard_map/project/pallas_call | solution.py:119
  135.7 8.9 %all-to-all-start.2 = ((f32[128,8,128]{2,1,0:T(8,128)}), f32[128,8,128]{2,1,0:T(8,128)S(1)}, u32[]{:S(2)}, u32[]{:S(2)}) async-start(f32[128,8,128]{2,1,0:T(8,128)} %bitcast.14), calls=%async_computation.2 | async-start | bytes 1048576 | tf_op jit(solution)/shard_map/all_to_all | solution.py:360
  144.6 1.1 collective-permute-start.24
  145.8 0.1 collective-permute-start.26
  145.9 0.4 collective-permute-start.27
  146.4 0.4 collective-permute-start.19
  146.8 11.4 %all-to-all-done.2 = f32[128,8,128]{2,1,0:T(8,128)S(1)} async-done(((f32[128,8,128]{2,1,0:T(8,128)}), f32[128,8,128]{2,1,0:T(8,128)S(1)}, u32[]{:S(2)}, u32[]{:S(2)}) %all-to-all-start.2) | async-done | bytes 524320 | tf_op jit(solution)/shard_map/all_to_all | solution.py:360
  158.2 0.1 reduce_sum.19
  158.4 0.7 broadcast_in_dim.5
  159.1 4.6 %all-to-all-start.3 = ((bf16[128,8,128]{2,1,0:T(8,128)(2,1)}), bf16[128,8,128]{2,1,0:T(8,128)(2,1)S(1)}, u32[]{:S(2)}, u32[]{:S(2)}) async-start(bf16[128,8,128]{2,1,0:T(8,128)(2,1)} %broadcast_in_dim.5), calls=%async_computation.3 | async-start | bytes 524288 | tf_op jit(solution)/shard_map/all_to_all | solution.py:362
  163.7 3.8 %own_columns.3.refs_6_ = bf16[16,256,256]{2,1,0:T(8,128)(2,1)} custom-call(s32[1]{0:T(128)} %bitcast.slot_ref.refs_0_, bf16[2048,128]{1,0:T(8,128)(2,1)} %copy-done, bf16[2048,128]{1,0:T(8,128)(2,1)} %copy-done.1, bf16[2048,128]{1,0:T(8,128)(2,1)} %collective-permute-done.20.refs_2_, bf16[2048,128]{1,0:T(8,128)(2,1)} %collective-permute-done.21.refs_3_), custom_call_target="tpu_custom_call" | custom-call | tf_op jit(solution)/shard_map/own_columns/pallas_call | solution.py:172
  167.6 0.8 copy-done.19
  168.3 18.3 %mirror_product.3.refs_14_ = f32[8,256,256]{2,1,0:T(8,128)S(1)} custom-call(s32[1]{0:T(128)} %bitcast.slot_ref.refs_0_, s32[1,8192]{1,0:T(1,128)S(1)} %copy-done.4, s32[8,8]{1,0:T(8,128)S(1)} %copy-done.6, bf16[2048,128]{1,0:T(8,128)(2,1)} %copy-done.11, bf16[2048,128]{1,0:T(8,128)(2,1)} %copy-done.13, bf16[2048,128]{1,0:T(8,128)(2,1)} %collective-permute-done.23.refs_2_, ...), custom_call_target="tpu_custom_call" | custom-call | tf_op jit(solution)/shard_map/mirror_product/pallas_call | solution.py:217
  186.7 0.8 copy-done.18
  187.4 12.8 %finish_last.1 = (f32[2048,128]{1,0:T(8,128)}, f32[2048,128]{1,0:T(8,128)}) custom-call(s32[1]{0:T(128)} %bitcast.slot_ref.refs_0_, s32[8,8]{1,0:T(8,128)S(1)} %copy-done.7, bf16[2048,128]{1,0:T(8,128)(2,1)} %collective-permute-done.15.refs_2_, bf16[2048,128]{1,0:T(8,128)(2,1)} %collective-permute-done.17.refs_3_, bf16[2048,128]{1,0:T(8,128)(2,1)} %copy-done.18, ...), custom_call_target="tpu_custom_call" | custom-call | tf_op jit(solution)/shard_map/finish_last/pallas_call | solution.py:333
  (69 shorter events, 0.5 us)
Async XLA Ops:
  2.3 33.7 %copy-start.2 = (bf16[2048,128]{1,0:T(8,128)(2,1)}, bf16[2048,128]{1,0:T(8,128)(2,1)S(1)}, u32[]{:S(2)}) copy-start(bf16[2048,128]{1,0:T(8,128)(2,1)S(1)} %get-tuple-element.8.refs_0_) | copy-start | bytes 1572868
  2.3 33.7 %copy-start.3 = (bf16[2048,128]{1,0:T(8,128)(2,1)}, bf16[2048,128]{1,0:T(8,128)(2,1)S(1)}, u32[]{:S(2)}) copy-start(bf16[2048,128]{1,0:T(8,128)(2,1)S(1)} %get-tuple-element.9.refs_1_) | copy-start | bytes 1572868
  2.3 13.5 %collective-permute-start.2 = (bf16[2048,128]{1,0:T(8,128)(2,1)S(1)}, bf16[2048,128]{1,0:T(8,128)(2,1)S(1)}, u32[]{:S(2)}, u32[]{:S(2)}) collective-permute-start(bf16[2048,128]{1,0:T(8,128)(2,1)S(1)} %get-tuple-element.9.refs_1_), channel_id=1, source_target_pairs={{0,64},{1,65},{2,66},{3,67},{4,68},{5,69},{6,70},{7,71},{8,72},{9,... | collective-permute-start | bytes 1572872 | tf_op jit(solution)/shard_map/ppermute | solution.py:25
  4.5 14.1 %collective-permute-start = (bf16[2048,128]{1,0:T(8,128)(2,1)S(1)}, bf16[2048,128]{1,0:T(8,128)(2,1)S(1)}, u32[]{:S(2)}, u32[]{:S(2)}) collective-permute-start(bf16[2048,128]{1,0:T(8,128)(2,1)S(1)} %get-tuple-element.8.refs_0_), channel_id=1, source_target_pairs={{0,66},{1,67},{2,64},{3,65},{4,70},{5,71},{6,68},{7,69},{8,74},{9,... | collective-permute-start | bytes 1572872 | tf_op jit(solution)/shard_map/ppermute | solution.py:25
  6.4 23.1 %collective-permute-start.11 = (bf16[2048,128]{1,0:T(8,128)(2,1)S(1)}, bf16[2048,128]{1,0:T(8,128)(2,1)S(1)}, u32[]{:S(2)}, u32[]{:S(2)}) collective-permute-start(bf16[2048,128]{1,0:T(8,128)(2,1)S(1)} %get-tuple-element.9.refs_1_), channel_id=1, source_target_pairs={{0,66},{1,67},{2,64},{3,65},{4,70},{5,71},{6,68},{7,69},{8,74},{9,... | collective-permute-start | bytes 1572872 | tf_op jit(solution)/shard_map/ppermute | solution.py:25
  7.2 22.3 %collective-permute-start.8 = (bf16[2048,128]{1,0:T(8,128)(2,1)S(1)}, bf16[2048,128]{1,0:T(8,128)(2,1)S(1)}, u32[]{:S(2)}, u32[]{:S(2)}) collective-permute-start(bf16[2048,128]{1,0:T(8,128)(2,1)S(1)} %get-tuple-element.8.refs_0_), channel_id=1, source_target_pairs={{0,64},{1,65},{2,66},{3,67},{4,68},{5,69},{6,70},{7,71},{8,72},{9,... | collective-permute-start | bytes 1572872 | tf_op jit(solution)/shard_map/ppermute | solution.py:25
  7.2 39.6 %collective-permute-start.6 = (bf16[2048,128]{1,0:T(8,128)(2,1)S(1)}, bf16[2048,128]{1,0:T(8,128)(2,1)}, u32[]{:S(2)}, u32[]{:S(2)}) collective-permute-start(bf16[2048,128]{1,0:T(8,128)(2,1)S(1)} %get-tuple-element.8.refs_0_), channel_id=1, source_target_pairs={{0,1},{1,0},{2,3},{3,2},{4,5},{5,4},{6,7},{7,6},{8,9},{9,8},{10,11... | collective-permute-start | bytes 1572872 | tf_op jit(solution)/shard_map/ppermute | solution.py:25
  15.8 20.2 %copy-start.9 = (bf16[2048,128]{1,0:T(8,128)(2,1)}, bf16[2048,128]{1,0:T(8,128)(2,1)S(1)}, u32[]{:S(2)}) copy-start(bf16[2048,128]{1,0:T(8,128)(2,1)S(1)} %collective-permute-done.2.refs_1_) | copy-start | bytes 1572868
  15.8 32.1 %collective-permute-start.7 = (bf16[2048,128]{1,0:T(8,128)(2,1)S(1)}, bf16[2048,128]{1,0:T(8,128)(2,1)}, u32[]{:S(2)}, u32[]{:S(2)}) collective-permute-start(bf16[2048,128]{1,0:T(8,128)(2,1)S(1)} %get-tuple-element.9.refs_1_), channel_id=1, source_target_pairs={{0,1},{1,0},{2,3},{3,2},{4,5},{5,4},{6,7},{7,6},{8,9},{9,8},{10,11... | collective-permute-start | bytes 1572872 | tf_op jit(solution)/shard_map/ppermute | solution.py:25
  18.6 28.2 %copy-start.10 = (bf16[2048,128]{1,0:T(8,128)(2,1)}, bf16[2048,128]{1,0:T(8,128)(2,1)S(1)}, u32[]{:S(2)}) copy-start(bf16[2048,128]{1,0:T(8,128)(2,1)S(1)} %collective-permute-done.refs_4_) | copy-start | bytes 1572868
  18.6 29.4 %collective-permute-start.10 = (bf16[2048,128]{1,0:T(8,128)(2,1)S(1)}, bf16[2048,128]{1,0:T(8,128)(2,1)}, u32[]{:S(2)}, u32[]{:S(2)}) collective-permute-start(bf16[2048,128]{1,0:T(8,128)(2,1)S(1)} %collective-permute-done.2.refs_1_), channel_id=1, source_target_pairs={{0,1},{1,0},{2,3},{3,2},{4,5},{5,4},{6,7},{7,6},{8,9},{9,8},{10,11... | collective-permute-start | bytes 1572872 | tf_op jit(solution)/shard_map/ppermute | solution.py:25
  29.5 18.4 %copy-start.12 = (bf16[2048,128]{1,0:T(8,128)(2,1)}, bf16[2048,128]{1,0:T(8,128)(2,1)S(1)}, u32[]{:S(2)}) copy-start(bf16[2048,128]{1,0:T(8,128)(2,1)S(1)} %collective-permute-done.11.refs_5_) | copy-start | bytes 1572868
  29.5 18.9 %collective-permute-start.1 = (bf16[2048,128]{1,0:T(8,128)(2,1)S(1)}, bf16[2048,128]{1,0:T(8,128)(2,1)}, u32[]{:S(2)}, u32[]{:S(2)}) collective-permute-start(bf16[2048,128]{1,0:T(8,128)(2,1)S(1)} %collective-permute-done.refs_4_), channel_id=1, source_target_pairs={{0,64},{1,65},{2,66},{3,67},{4,68},{5,69},{6,70},{7,71},{8,72},{9,... | collective-permute-start | bytes 1572872 | tf_op jit(solution)/shard_map/ppermute | solution.py:25
  29.5 6.5 %copy-start.14 = (bf16[2048,128]{1,0:T(8,128)(2,1)}, bf16[2048,128]{1,0:T(8,128)(2,1)S(1)}, u32[]{:S(2)}) copy-start(bf16[2048,128]{1,0:T(8,128)(2,1)S(1)} %collective-permute-done.8.refs_0_) | copy-start | bytes 1572868
  29.5 19.0 %collective-permute-start.3 = (bf16[2048,128]{1,0:T(8,128)(2,1)S(1)}, bf16[2048,128]{1,0:T(8,128)(2,1)}, u32[]{:S(2)}, u32[]{:S(2)}) collective-permute-start(bf16[2048,128]{1,0:T(8,128)(2,1)S(1)} %collective-permute-done.2.refs_1_), channel_id=1, source_target_pairs={{0,66},{1,67},{2,64},{3,65},{4,70},{5,71},{6,68},{7,69},{8,74},{9,... | collective-permute-start | bytes 1572872 | tf_op jit(solution)/shard_map/ppermute | solution.py:25
  36.0 24.3 %all-to-all-start = ((f32[128,8,128]{2,1,0:T(8,128)}), f32[128,8,128]{2,1,0:T(8,128)S(1)}, u32[]{:S(2)}, u32[]{:S(2)}) async-start(f32[128,8,128]{2,1,0:T(8,128)} %bitcast.13), calls=%async_computation | async-start | bytes 1048576 | tf_op jit(solution)/shard_map/all_to_all | solution.py:360
  46.7 23.0 %collective-permute-start.12 = (bf16[2048,128]{1,0:T(8,128)(2,1)S(1)}, bf16[2048,128]{1,0:T(8,128)(2,1)S(1)}, u32[]{:S(2)}, u32[]{:S(2)}) collective-permute-start(bf16[2048,128]{1,0:T(8,128)(2,1)S(1)} %collective-permute-done.refs_4_), channel_id=1, source_target_pairs={{0,1},{1,0},{2,3},{3,2},{4,5},{5,4},{6,7},{7,6},{8,9},{9,8},{10,11... | collective-permute-start | bytes 1572872 | tf_op jit(solution)/shard_map/ppermute | solution.py:25
  47.9 21.9 %collective-permute-start.13 = (bf16[2048,128]{1,0:T(8,128)(2,1)S(1)}, bf16[2048,128]{1,0:T(8,128)(2,1)}, u32[]{:S(2)}, u32[]{:S(2)}) collective-permute-start(bf16[2048,128]{1,0:T(8,128)(2,1)S(1)} %collective-permute-done.11.refs_5_), channel_id=1, source_target_pairs={{0,1},{1,0},{2,3},{3,2},{4,5},{5,4},{6,7},{7,6},{8,9},{9,8},{10,11... | collective-permute-start | bytes 1572872 | tf_op jit(solution)/shard_map/ppermute | solution.py:25
  48.0 21.8 %collective-permute-start.9 = (bf16[2048,128]{1,0:T(8,128)(2,1)}, bf16[2048,128]{1,0:T(8,128)(2,1)}, u32[]{:S(2)}, u32[]{:S(2)}) collective-permute-start(bf16[2048,128]{1,0:T(8,128)(2,1)} %copy-done.14), channel_id=1, source_target_pairs={{0,1},{1,0},{2,3},{3,2},{4,5},{5,4},{6,7},{7,6},{8,9},{9,8},{10,11... | collective-permute-start | bytes 1572872 | tf_op jit(solution)/shard_map/ppermute | solution.py:25
  48.4 40.4 %collective-permute-start.4 = (bf16[2048,128]{1,0:T(8,128)(2,1)}, bf16[2048,128]{1,0:T(8,128)(2,1)}, u32[]{:S(2)}, u32[]{:S(2)}) collective-permute-start(bf16[2048,128]{1,0:T(8,128)(2,1)} %collective-permute-done.1.refs_2_), channel_id=1, source_target_pairs={{0,1},{1,0},{2,3},{3,2},{4,5},{5,4},{6,7},{7,6},{8,9},{9,8},{10,11... | collective-permute-start | bytes 1572872 | tf_op jit(solution)/shard_map/ppermute | solution.py:25
  48.5 40.3 %collective-permute-start.5 = (bf16[2048,128]{1,0:T(8,128)(2,1)}, bf16[2048,128]{1,0:T(8,128)(2,1)}, u32[]{:S(2)}, u32[]{:S(2)}) collective-permute-start(bf16[2048,128]{1,0:T(8,128)(2,1)} %collective-permute-done.3.refs_3_), channel_id=1, source_target_pairs={{0,1},{1,0},{2,3},{3,2},{4,5},{5,4},{6,7},{7,6},{8,9},{9,8},{10,11... | collective-permute-start | bytes 1572872 | tf_op jit(solution)/shard_map/ppermute | solution.py:25
  61.2 27.6 %all-to-all-start.1 = ((bf16[128,8,128]{2,1,0:T(8,128)(2,1)}), bf16[128,8,128]{2,1,0:T(8,128)(2,1)S(1)}, u32[]{:S(2)}, u32[]{:S(2)}) async-start(bf16[128,8,128]{2,1,0:T(8,128)(2,1)} %broadcast_in_dim.4), calls=%async_computation.1 | async-start | bytes 524288 | tf_op jit(solution)/shard_map/all_to_all | solution.py:362
  65.9 4.7 %copy-start.4 = (s32[1,8192]{1,0:T(1,128)S(1)}, s32[1,8192]{1,0:T(1,128)}, u32[]{:S(2)}) copy-start(s32[1,8192]{1,0:T(1,128)} %partner_ref.3) | copy-start | bytes 98308
  69.7 19.2 %copy-start.5 = (f32[2048]{0:T(1024)S(1)}, f32[2048]{0:T(1024)}, u32[]{:S(2)}) copy-start(f32[2048]{0:T(1024)} %param.12) | copy-start | bytes 24580
  69.7 19.2 %copy-start.7 = (s32[8,8]{1,0:T(8,128)S(1)}, s32[8,8]{1,0:T(8,128)}, u32[]{:S(2)}) copy-start(s32[8,8]{1,0:T(8,128)} %refs_1_.3) | copy-start | bytes 772
  69.7 19.2 %copy-start.8 = (f32[128]{0:T(128)S(1)}, f32[128]{0:T(128)}, u32[]{:S(2)}) copy-start(f32[128]{0:T(128)} %param.13) | copy-start | bytes 1540
  102.0 33.7 %copy-start = (bf16[2048,128]{1,0:T(8,128)(2,1)}, bf16[2048,128]{1,0:T(8,128)(2,1)S(1)}, u32[]{:S(2)}) copy-start(bf16[2048,128]{1,0:T(8,128)(2,1)S(1)} %get-tuple-element.10.refs_0_) | copy-start | bytes 1572868
  102.0 33.7 %copy-start.1 = (bf16[2048,128]{1,0:T(8,128)(2,1)}, bf16[2048,128]{1,0:T(8,128)(2,1)S(1)}, u32[]{:S(2)}) copy-start(bf16[2048,128]{1,0:T(8,128)(2,1)S(1)} %get-tuple-element.11.refs_1_) | copy-start | bytes 1572868
  102.0 12.5 %collective-permute-start.22 = (bf16[2048,128]{1,0:T(8,128)(2,1)S(1)}, bf16[2048,128]{1,0:T(8,128)(2,1)S(1)}, u32[]{:S(2)}, u32[]{:S(2)}) collective-permute-start(bf16[2048,128]{1,0:T(8,128)(2,1)S(1)} %get-tuple-element.10.refs_0_), channel_id=1, source_target_pairs={{0,64},{1,65},{2,66},{3,67},{4,68},{5,69},{6,70},{7,71},{8,72},{9,... | collective-permute-start | bytes 1572872 | tf_op jit(solution)/shard_map/ppermute | solution.py:25
  103.4 22.3 %collective-permute-start.16 = (bf16[2048,128]{1,0:T(8,128)(2,1)S(1)}, bf16[2048,128]{1,0:T(8,128)(2,1)S(1)}, u32[]{:S(2)}, u32[]{:S(2)}) collective-permute-start(bf16[2048,128]{1,0:T(8,128)(2,1)S(1)} %get-tuple-element.11.refs_1_), channel_id=1, source_target_pairs={{0,64},{1,65},{2,66},{3,67},{4,68},{5,69},{6,70},{7,71},{8,72},{9,... | collective-permute-start | bytes 1572872 | tf_op jit(solution)/shard_map/ppermute | solution.py:25
  103.5 24.1 %collective-permute-start.14 = (bf16[2048,128]{1,0:T(8,128)(2,1)S(1)}, bf16[2048,128]{1,0:T(8,128)(2,1)S(1)}, u32[]{:S(2)}, u32[]{:S(2)}) collective-permute-start(bf16[2048,128]{1,0:T(8,128)(2,1)S(1)} %get-tuple-element.10.refs_0_), channel_id=1, source_target_pairs={{0,66},{1,67},{2,64},{3,65},{4,70},{5,71},{6,68},{7,69},{8,74},{9,... | collective-permute-start | bytes 1572872 | tf_op jit(solution)/shard_map/ppermute | solution.py:25
  106.2 22.9 %collective-permute-start.25 = (bf16[2048,128]{1,0:T(8,128)(2,1)S(1)}, bf16[2048,128]{1,0:T(8,128)(2,1)S(1)}, u32[]{:S(2)}, u32[]{:S(2)}) collective-permute-start(bf16[2048,128]{1,0:T(8,128)(2,1)S(1)} %get-tuple-element.11.refs_1_), channel_id=1, source_target_pairs={{0,66},{1,67},{2,64},{3,65},{4,70},{5,71},{6,68},{7,69},{8,74},{9,... | collective-permute-start | bytes 1572872 | tf_op jit(solution)/shard_map/ppermute | solution.py:25
  106.2 38.4 %collective-permute-start.20 = (bf16[2048,128]{1,0:T(8,128)(2,1)S(1)}, bf16[2048,128]{1,0:T(8,128)(2,1)}, u32[]{:S(2)}, u32[]{:S(2)}) collective-permute-start(bf16[2048,128]{1,0:T(8,128)(2,1)S(1)} %get-tuple-element.10.refs_0_), channel_id=1, source_target_pairs={{0,1},{1,0},{2,3},{3,2},{4,5},{5,4},{6,7},{7,6},{8,9},{9,8},{10,11... | collective-permute-start | bytes 1572872 | tf_op jit(solution)/shard_map/ppermute | solution.py:25
  114.5 21.2 %copy-start.11 = (bf16[2048,128]{1,0:T(8,128)(2,1)}, bf16[2048,128]{1,0:T(8,128)(2,1)S(1)}, u32[]{:S(2)}) copy-start(bf16[2048,128]{1,0:T(8,128)(2,1)S(1)} %collective-permute-done.22.refs_0_) | copy-start | bytes 1572868
  114.5 31.3 %collective-permute-start.21 = (bf16[2048,128]{1,0:T(8,128)(2,1)S(1)}, bf16[2048,128]{1,0:T(8,128)(2,1)}, u32[]{:S(2)}, u32[]{:S(2)}) collective-permute-start(bf16[2048,128]{1,0:T(8,128)(2,1)S(1)} %get-tuple-element.11.refs_1_), channel_id=1, source_target_pairs={{0,1},{1,0},{2,3},{3,2},{4,5},{5,4},{6,7},{7,6},{8,9},{9,8},{10,11... | collective-permute-start | bytes 1572872 | tf_op jit(solution)/shard_map/ppermute | solution.py:25
  125.7 18.9 %copy-start.13 = (bf16[2048,128]{1,0:T(8,128)(2,1)}, bf16[2048,128]{1,0:T(8,128)(2,1)S(1)}, u32[]{:S(2)}) copy-start(bf16[2048,128]{1,0:T(8,128)(2,1)S(1)} %collective-permute-done.16.refs_1_) | copy-start | bytes 1572868
  125.7 20.1 %collective-permute-start.23 = (bf16[2048,128]{1,0:T(8,128)(2,1)S(1)}, bf16[2048,128]{1,0:T(8,128)(2,1)}, u32[]{:S(2)}, u32[]{:S(2)}) collective-permute-start(bf16[2048,128]{1,0:T(8,128)(2,1)S(1)} %collective-permute-done.22.refs_0_), channel_id=1, source_target_pairs={{0,1},{1,0},{2,3},{3,2},{4,5},{5,4},{6,7},{7,6},{8,9},{9,8},{10,11... | collective-permute-start | bytes 1572872 | tf_op jit(solution)/shard_map/ppermute | solution.py:25
  127.7 18.1 %copy-start.15 = (bf16[2048,128]{1,0:T(8,128)(2,1)}, bf16[2048,128]{1,0:T(8,128)(2,1)S(1)}, u32[]{:S(2)}) copy-start(bf16[2048,128]{1,0:T(8,128)(2,1)S(1)} %collective-permute-done.14.refs_4_) | copy-start | bytes 1572868
  127.7 18.6 %collective-permute-start.15 = (bf16[2048,128]{1,0:T(8,128)(2,1)S(1)}, bf16[2048,128]{1,0:T(8,128)(2,1)}, u32[]{:S(2)}, u32[]{:S(2)}) collective-permute-start(bf16[2048,128]{1,0:T(8,128)(2,1)S(1)} %collective-permute-done.14.refs_4_), channel_id=1, source_target_pairs={{0,64},{1,65},{2,66},{3,67},{4,68},{5,69},{6,70},{7,71},{8,72},{9,... | collective-permute-start | bytes 1572872 | tf_op jit(solution)/shard_map/ppermute | solution.py:25
  129.0 6.7 %copy-start.16 = (bf16[2048,128]{1,0:T(8,128)(2,1)}, bf16[2048,128]{1,0:T(8,128)(2,1)S(1)}, u32[]{:S(2)}) copy-start(bf16[2048,128]{1,0:T(8,128)(2,1)S(1)} %collective-permute-done.25.refs_5_) | copy-start | bytes 1572868
  129.0 17.4 %collective-permute-start.17 = (bf16[2048,128]{1,0:T(8,128)(2,1)S(1)}, bf16[2048,128]{1,0:T(8,128)(2,1)}, u32[]{:S(2)}, u32[]{:S(2)}) collective-permute-start(bf16[2048,128]{1,0:T(8,128)(2,1)S(1)} %collective-permute-done.16.refs_1_), channel_id=1, source_target_pairs={{0,66},{1,67},{2,64},{3,65},{4,70},{5,71},{6,68},{7,69},{8,74},{9,... | collective-permute-start | bytes 1572872 | tf_op jit(solution)/shard_map/ppermute | solution.py:25
  135.7 22.5 %all-to-all-start.2 = ((f32[128,8,128]{2,1,0:T(8,128)}), f32[128,8,128]{2,1,0:T(8,128)S(1)}, u32[]{:S(2)}, u32[]{:S(2)}) async-start(f32[128,8,128]{2,1,0:T(8,128)} %bitcast.14), calls=%async_computation.2 | async-start | bytes 1048576 | tf_op jit(solution)/shard_map/all_to_all | solution.py:360
  144.6 22.9 %collective-permute-start.24 = (bf16[2048,128]{1,0:T(8,128)(2,1)S(1)}, bf16[2048,128]{1,0:T(8,128)(2,1)S(1)}, u32[]{:S(2)}, u32[]{:S(2)}) collective-permute-start(bf16[2048,128]{1,0:T(8,128)(2,1)S(1)} %collective-permute-done.16.refs_1_), channel_id=1, source_target_pairs={{0,1},{1,0},{2,3},{3,2},{4,5},{5,4},{6,7},{7,6},{8,9},{9,8},{10,11... | collective-permute-start | bytes 1572872 | tf_op jit(solution)/shard_map/ppermute | solution.py:25
  145.8 21.8 %collective-permute-start.26 = (bf16[2048,128]{1,0:T(8,128)(2,1)S(1)}, bf16[2048,128]{1,0:T(8,128)(2,1)}, u32[]{:S(2)}, u32[]{:S(2)}) collective-permute-start(bf16[2048,128]{1,0:T(8,128)(2,1)S(1)} %collective-permute-done.14.refs_4_), channel_id=1, source_target_pairs={{0,1},{1,0},{2,3},{3,2},{4,5},{5,4},{6,7},{7,6},{8,9},{9,8},{10,11... | collective-permute-start | bytes 1572872 | tf_op jit(solution)/shard_map/ppermute | solution.py:25
  145.9 22.5 %collective-permute-start.27 = (bf16[2048,128]{1,0:T(8,128)(2,1)}, bf16[2048,128]{1,0:T(8,128)(2,1)}, u32[]{:S(2)}, u32[]{:S(2)}) collective-permute-start(bf16[2048,128]{1,0:T(8,128)(2,1)} %copy-done.16), channel_id=1, source_target_pairs={{0,1},{1,0},{2,3},{3,2},{4,5},{5,4},{6,7},{7,6},{8,9},{9,8},{10,11... | collective-permute-start | bytes 1572872 | tf_op jit(solution)/shard_map/ppermute | solution.py:25
  146.3 40.4 %collective-permute-start.18 = (bf16[2048,128]{1,0:T(8,128)(2,1)}, bf16[2048,128]{1,0:T(8,128)(2,1)S(1)}, u32[]{:S(2)}, u32[]{:S(2)}) collective-permute-start(bf16[2048,128]{1,0:T(8,128)(2,1)} %collective-permute-done.15.refs_2_), channel_id=1, source_target_pairs={{0,1},{1,0},{2,3},{3,2},{4,5},{5,4},{6,7},{7,6},{8,9},{9,8},{10,11... | collective-permute-start | bytes 1572872 | tf_op jit(solution)/shard_map/ppermute | solution.py:25
  146.4 40.3 %collective-permute-start.19 = (bf16[2048,128]{1,0:T(8,128)(2,1)}, bf16[2048,128]{1,0:T(8,128)(2,1)}, u32[]{:S(2)}, u32[]{:S(2)}) collective-permute-start(bf16[2048,128]{1,0:T(8,128)(2,1)} %collective-permute-done.17.refs_3_), channel_id=1, source_target_pairs={{0,1},{1,0},{2,3},{3,2},{4,5},{5,4},{6,7},{7,6},{8,9},{9,8},{10,11... | collective-permute-start | bytes 1572872 | tf_op jit(solution)/shard_map/ppermute | solution.py:25
  159.1 27.5 %all-to-all-start.3 = ((bf16[128,8,128]{2,1,0:T(8,128)(2,1)}), bf16[128,8,128]{2,1,0:T(8,128)(2,1)S(1)}, u32[]{:S(2)}, u32[]{:S(2)}) async-start(bf16[128,8,128]{2,1,0:T(8,128)(2,1)} %broadcast_in_dim.5), calls=%async_computation.3 | async-start | bytes 524288 | tf_op jit(solution)/shard_map/all_to_all | solution.py:362
  (4 other events, 7.0 us)

commit v5 on v4

--- a/solution.py
+++ b/solution.py
@@ -93,6 +93,20 @@
     )(*in_hbm(x, y))
 
 
+def store_projection(summed, basis, out_ref):
+    rank = basis.shape[1]
+    wide = 2 * BLK
+    for r in range(rank // wide):
+        value = jnp.dot(summed[...], basis[:, r * wide : (r + 1) * wide], preferred_element_type=F32)
+        for q in range(wide // NV):
+            row = r * wide + q * NV
+            out_ref[row : row + NV, :] = value[:, q * NV : (q + 1) * NV].T
+
+
+def add_vectors(x, y):
+    return (x + y).T.astype(BF16)
+
+
 def project_body(x_hbm, y_hbm, basis_hbm, out_ref, x, y, basis, summed, sems):
     copies = []
     for t, (source, target) in enumerate(((x_hbm, x), (y_hbm, y), (basis_hbm, basis))):
@@ -103,15 +117,9 @@
     rows = x.shape[0]
     for b in range(rows // BLK):
         part = pl.ds(b * BLK, BLK)
-        summed[:, b * BLK : (b + 1) * BLK] = (x[part, :] + y[part, :]).T.astype(BF16)
+        summed[:, b * BLK : (b + 1) * BLK] = add_vectors(x[part, :], y[part, :])
     copies[2].wait()
-    rank = basis.shape[1]
-    wide = 2 * BLK
-    for r in range(rank // wide):
-        value = jnp.dot(summed[...], basis[:, r * wide : (r + 1) * wide], preferred_element_type=F32)
-        for q in range(wide // NV):
-            row = r * wide + q * NV
-            out_ref[row : row + NV, :] = value[:, q * NV : (q + 1) * NV].T
+    store_projection(summed, basis, out_ref)
 
 
 def project(x, y, basis):
@@ -154,7 +162,7 @@
         split_block(flat, pl.multiple_of(block * 2 * BLK, 2 * BLK), first + block, out, select)
         return carry
 
-    lax.fori_loop(0, flat.shape[0] // (2 * BLK), split, 0, unroll=8)
+    lax.fori_loop(0, flat.shape[0] // (2 * BLK), split, 0, unroll=16)
 
 
 def own_body(slot_ref, *refs):
@@ -177,7 +185,7 @@
         scratch_shapes=[pltpu.VMEM((4 * rows, NV), BF16), pltpu.SemaphoreType.DMA((4,))],
         compiler_params=pltpu.CompilerParams(vmem_limit_bytes=8 * MIB),
         name="own_columns",
-    )(slot, *in_hbm(*chunks))
+    )(slot, *chunks)
 
 
 def mirror_body(slot_ref, partner_ref, list_ref, *refs):
@@ -186,11 +194,11 @@
     copies = load_patch(slot_ref[0], chunks, source.reshape(2 * source.shape[0], NV), sems)
     blocks = kernel.shape[0]
     loads = [pltpu.make_async_copy(kernel_hbm.at[b], kernel.at[b], kernel_sems.at[b]) for b in range(blocks)]
-    for load in loads:
-        load.start()
     select = split_matrix()
     for copy in copies:
         copy.wait()
+    for load in loads:
+        load.start()
     unroll = 128
 
     def gather(step, carry):
@@ -208,7 +216,7 @@
         out_ref[b] = list_product(kernel, columns, list_ref, b)
         return carry
 
-    lax.fori_loop(0, blocks, product, 0, unroll=2)
+    lax.fori_loop(0, blocks, product, 0, unroll=4)
 
 
 def mirror_product(slot, partner, indices, chunks, kernel):
@@ -244,9 +252,9 @@
         next_x_hbm, next_y_hbm = rest[:2]
         rest = rest[2:]
     else:
-        next_x_hbm, next_y_hbm, low_ref, high_ref = rest[:4]
-        rest = rest[4:]
-    flat, columns, kernel, basis, x, y, levels, scratch, chunk_sems, sems, save_sems = rest
+        next_x_hbm, next_y_hbm, low_ref, high_ref, project_ref = rest[:5]
+        rest = rest[5:]
+    flat, columns, kernel, basis, x, y, levels, scratch, summed, chunk_sems, sems, save_sems = rest
     blocks = kernel.shape[0]
     core = slot_ref[0] & 1
     copies = load_patch(core, chunks, flat, chunk_sems)
@@ -268,9 +276,6 @@
         part = block_rows(b)
         return pltpu.make_async_copy(source.at[part], target.at[part], save_sems.at[t, b])
 
-    for b in range(blocks):
-        for t in range(4):
-            load(b, t).start()
     half = BLK // 2
     for b in range(blocks):
         row = energy_ref[b]
@@ -278,16 +283,17 @@
         levels[b * BLK + half : (b + 1) * BLK, :] = column_of(row[:, half:])
     for copy in copies:
         copy.wait()
+    for b in range(blocks):
+        for t in range(4):
+            load(b, t).start()
     split_all(flat, (1 - slot_ref[0] // 2) * count, columns, split_matrix())
     for copy in extra:
         copy.wait()
+    shifts = shift_ref[...]
     for b in range(blocks):
         for t in range(4):
             load(b, t).wait()
-    shifts = shift_ref[...]
-
-    def step(b):
-        part = block_rows(b)
+        part = pl.ds(b * BLK, BLK)
         mirrored = mirror_ref[b]
         exchange = jnp.dot(basis[part, :], weight_ref[...], preferred_element_type=F32)
         direct = list_product(kernel, columns, list_ref, b)
@@ -298,34 +304,26 @@
         y[part, :] = next_y
         for t in range(2):
             save(b, t).start()
-        return (next_x, next_y)
-
-    if last:
-        lax.fori_loop(0, blocks, lambda b, carry: (step(b), carry)[1], 0, unroll=2)
-    else:
-        for place, out_ref in enumerate((low_ref, high_ref)):
-            base = place * (blocks // 2)
-
-            def pair(b, carry):
-                next_x, next_y = step(base + b)
-                out_ref[block_rows(b, 2 * BLK), :] = interleave(next_x, next_y, scratch.at[b % 2])
-                return carry
-
-            lax.fori_loop(0, blocks // 2, pair, 0, unroll=2)
+        if not last:
+            out_ref, place = (low_ref, b) if b < blocks // 2 else (high_ref, b - blocks // 2)
+            out_ref[pl.ds(place * 2 * BLK, 2 * BLK), :] = interleave(next_x, next_y, scratch.at[b % 2])
+            summed[:, b * BLK : (b + 1) * BLK] = add_vectors(next_x, next_y)
+    if not last:
+        store_projection(summed, basis, project_ref)
     for b in range(blocks):
         for t in range(2):
             save(b, t).wait()
 
 
 def finish(last, slot, indices, chunks, own, x, y, energy, shift, kernel, basis, weights, mirrored):
-    rows, _ = basis.shape
+    rows, rank = basis.shape
     blocks = kernel.shape[0]
     patch = 4 * rows
     out_specs = [ANY_SPEC, ANY_SPEC]
     out_shape = [pltpu.HBM((rows, NV), F32)] * 2
     if not last:
-        out_specs += [VMEM_SPEC] * 2
-        out_shape += [jax.ShapeDtypeStruct((rows, NV), BF16)] * 2
+        out_specs += [VMEM_SPEC] * 3
+        out_shape += [jax.ShapeDtypeStruct((rows, NV), BF16)] * 2 + [pltpu.HBM((rank, NV), F32)]
 
     def body(*refs):
         finish_body(last, *refs)
@@ -344,6 +342,7 @@
             pltpu.VMEM((rows, NV), F32),
             pltpu.VMEM((rows, NV), F32),
             pltpu.VMEM((2, 2 * BLK, NV), F32),
+            pltpu.VMEM((NV, rows), BF16),
             pltpu.SemaphoreType.DMA((8,)),
             pltpu.SemaphoreType.DMA((4, blocks)),
             pltpu.SemaphoreType.DMA((2, blocks)),
@@ -376,9 +375,10 @@
         last = app == APPS - 1
         if app == 0:
             low, high = pack(x, y)
+            partial = project(x, y, basis)
         far_low = toggled(low, far)
         near_high = toggled(high, near)
-        weights = total_weights(project(x, y, basis))
+        weights = total_weights(partial)
         far_high = toggled(high, far)
         near_low = toggled(low, near)
         own = [toggled(low, 1), toggled(high, 1)]
@@ -392,7 +392,7 @@
         out = finish(last, slot, res_list, across, own_half, x, y, levels, shifts, res_kernel, basis, weights, mirrored)
         if last:
             return tuple(out)
-        x, y, low, high = out
+        x, y, low, high, partial = out
 
 
 def solution(mesh):

time: 201 us -> 189 us (0.940)
  Pallas kernels: 80.6 us -> 68.6 us
  starting transfers between devices: 62.5 us -> 70.7 us
  waiting for transfers between devices: 51.9 us -> 45.3 us
    ppermute x28, starting transfers between devices: 33.6 us -> 40.4 us  [toggled(): lax.ppermute(array, AXES, [(i, i ^ mask) for i in range(lax.axis_size(AXE...]
    all_to_all x2, waiting for transfers between devices: 22.8 us -> 16.4 us  [total_weights(): lax.all_to_all(partial.reshape(size, part, vectors), AXES, 0, 0, tiled=True)]
    pallas_call x2, Pallas kernels: 36.6 us -> 31.2 us  [mirror_product(): pl.pallas_call(mirror_body, in_specs=[SMEM_SPEC] * 3 + [ANY_SPEC] * 9, ou...]
    pallas_call x2 -> x1, Pallas kernels: 8.97 us -> 4.48 us  [project(): pl.pallas_call(project_body, in_specs=[ANY_SPEC] * 3, out_specs=VMEM_SPEC...]
    pallas_call x2, Pallas kernels: 7.58 us -> 4.67 us  [own_columns(): pl.pallas_call(own_body, in_specs=[SMEM_SPEC] + [ANY_SPEC] * 4, out_specs...]
  transfers between devices with their start and end apart: 32 -> 32, of which waited for: 6 -> 7; matrix products, arithmetic and copies ran while one was open for 1% -> 1% of each run, Pallas kernels for 27% -> 21%
where the time goes in v5:
time: 189 us; the launch traced here: 188 us
  starting transfers between devices  70.7 us (37%)
  Pallas kernels  68.6 us (36%)
  waiting for transfers between devices  45.3 us (24%)
  local copies, waits for them, and re-layouts  2.31 us (1%)
    ppermute x28, starting transfers between devices, toggled(): lax.ppermute(array, AXES, [(i, i ^ mask) for i in range(lax.axis_size(AXE...  40.4 us
    pallas_call x2, Pallas kernels, mirror_product(): pl.pallas_call(mirror_body, in_specs=[SMEM_SPEC] * 3 + [ANY_SPEC] * 9, ou...  31.2 us
    ppermute x28, waiting for transfers between devices, toggled(): lax.ppermute(array, AXES, [(i, i ^ mask) for i in range(lax.axis_size(AXE...  28.9 us
    pallas_call x2, Pallas kernels, finish(): pl.pallas_call(body, in_specs=[SMEM_SPEC] * 2 + [ANY_SPEC] * 7 + [VMEM_SP...  26.6 us
    all_to_all x2, starting transfers between devices, total_weights(): lax.all_to_all(partial.reshape(size, part, vectors), AXES, 0, 0, tiled=True)  19.6 us
    all_to_all x2, waiting for transfers between devices, total_weights(): lax.all_to_all(partial.reshape(size, part, vectors), AXES, 0, 0, tiled=True)  16.4 us
    all_to_all x2, starting transfers between devices, total_weights(): lax.all_to_all(jnp.broadcast_to(own[None], (size, part, vectors)), AXES,...  10.7 us
    pallas_call x2, Pallas kernels, own_columns(): pl.pallas_call(own_body, in_specs=[SMEM_SPEC] + [ANY_SPEC] * 4, out_specs...  4.67 us
  transfers between devices with their start and end apart: 32, of which 7 were waited for; matrix products, arithmetic and copies ran while one was open for 1% of the time, Pallas kernels for 21%

profile of v5, /device:TPU:1, one launch (start us, length us, event | category | flops | bytes accessed | tf_op | source)
XLA Modules:
  0.0 188.3 jit_solution(13293192545610032127)
XLA Ops:
  0.6 1.6 pack.1
  2.3 2.2 %collective-permute-start.2 = (bf16[2048,128]{1,0:T(8,128)(2,1)S(1)}, bf16[2048,128]{1,0:T(8,128)(2,1)S(1)}, u32[]{:S(2)}, u32[]{:S(2)}) collective-permute-start(bf16[2048,128]{1,0:T(8,128)(2,1)S(1)} %get-tuple-element.10.refs_1_), channel_id=1, source_target_pairs={{0,64},{1,65},{2,66},{3,67},{4,68},{5,69},{6,70},{7,71},{8,72},{9,... | collective-permute-start | bytes 1572872 | tf_op jit(solution)/shard_map/ppermute | solution.py:25
  4.5 1.9 %collective-permute-start = (bf16[2048,128]{1,0:T(8,128)(2,1)S(1)}, bf16[2048,128]{1,0:T(8,128)(2,1)}, u32[]{:S(2)}, u32[]{:S(2)}) collective-permute-start(bf16[2048,128]{1,0:T(8,128)(2,1)S(1)} %get-tuple-element.9.refs_0_), channel_id=1, source_target_pairs={{0,66},{1,67},{2,64},{3,65},{4,70},{5,71},{6,68},{7,69},{8,74},{9,... | collective-permute-start | bytes 1572872 | tf_op jit(solution)/shard_map/ppermute | solution.py:25
  6.4 0.8 collective-permute-start.11
  7.2 1.5 collective-permute-start.6
  8.7 7.2 %collective-permute-done.2.refs_1_ = bf16[2048,128]{1,0:T(8,128)(2,1)S(1)} collective-permute-done((bf16[2048,128]{1,0:T(8,128)(2,1)S(1)}, bf16[2048,128]{1,0:T(8,128)(2,1)S(1)}, u32[]{:S(2)}, u32[]{:S(2)}) %collective-permute-start.2) | collective-permute-done | bytes 524320 | tf_op jit(solution)/shard_map/ppermute | solution.py:25
  15.9 2.7 %collective-permute-start.7 = (bf16[2048,128]{1,0:T(8,128)(2,1)S(1)}, bf16[2048,128]{1,0:T(8,128)(2,1)S(1)}, u32[]{:S(2)}, u32[]{:S(2)}) collective-permute-start(bf16[2048,128]{1,0:T(8,128)(2,1)S(1)} %get-tuple-element.10.refs_1_), channel_id=1, source_target_pairs={{0,1},{1,0},{2,3},{3,2},{4,5},{5,4},{6,7},{7,6},{8,9},{9,8},{10,11... | collective-permute-start | bytes 1572872 | tf_op jit(solution)/shard_map/ppermute | solution.py:25
  18.5 3.0 %collective-permute-start.10 = (bf16[2048,128]{1,0:T(8,128)(2,1)S(1)}, bf16[2048,128]{1,0:T(8,128)(2,1)}, u32[]{:S(2)}, u32[]{:S(2)}) collective-permute-start(bf16[2048,128]{1,0:T(8,128)(2,1)S(1)} %collective-permute-done.2.refs_1_), channel_id=1, source_target_pairs={{0,1},{1,0},{2,3},{3,2},{4,5},{5,4},{6,7},{7,6},{8,9},{9,8},{10,11... | collective-permute-start | bytes 1572872 | tf_op jit(solution)/shard_map/ppermute | solution.py:25
  21.5 7.9 %collective-permute-done.11.refs_5_ = bf16[2048,128]{1,0:T(8,128)(2,1)S(1)} collective-permute-done((bf16[2048,128]{1,0:T(8,128)(2,1)S(1)}, bf16[2048,128]{1,0:T(8,128)(2,1)S(1)}, u32[]{:S(2)}, u32[]{:S(2)}) %collective-permute-start.11) | collective-permute-done | bytes 524320 | tf_op jit(solution)/shard_map/ppermute | solution.py:25
  29.5 2.0 %collective-permute-start.3 = (bf16[2048,128]{1,0:T(8,128)(2,1)S(1)}, bf16[2048,128]{1,0:T(8,128)(2,1)}, u32[]{:S(2)}, u32[]{:S(2)}) collective-permute-start(bf16[2048,128]{1,0:T(8,128)(2,1)S(1)} %collective-permute-done.2.refs_1_), channel_id=1, source_target_pairs={{0,66},{1,67},{2,64},{3,65},{4,70},{5,71},{6,68},{7,69},{8,74},{9,... | collective-permute-start | bytes 1572872 | tf_op jit(solution)/shard_map/ppermute | solution.py:25
  31.4 4.5 %project.1 = f32[1024,128]{1,0:T(8,128)} custom-call(f32[2048,128]{1,0:T(8,128)} %refs_7_.1, f32[2048,128]{1,0:T(8,128)} %refs_8_.4, bf16[2048,1024]{1,0:T(8,128)(2,1)} %refs_12_.3), custom_call_target="tpu_custom_call" | custom-call | tf_op jit(solution)/shard_map/project/pallas_call | solution.py:127
  35.9 10.7 %all-to-all-start = ((f32[128,8,128]{2,1,0:T(8,128)}), f32[128,8,128]{2,1,0:T(8,128)S(1)}, u32[]{:S(2)}, u32[]{:S(2)}) async-start(f32[128,8,128]{2,1,0:T(8,128)} %bitcast.13), calls=%async_computation | async-start | bytes 1048576 | tf_op jit(solution)/shard_map/all_to_all | solution.py:359
  46.7 1.1 collective-permute-start.12
  47.8 0.1 collective-permute-start.13
  47.9 0.4 collective-permute-start.9
  48.5 0.4 collective-permute-start.5
  48.9 11.4 %all-to-all-done = f32[128,8,128]{2,1,0:T(8,128)S(1)} async-done(((f32[128,8,128]{2,1,0:T(8,128)}), f32[128,8,128]{2,1,0:T(8,128)S(1)}, u32[]{:S(2)}, u32[]{:S(2)}) %all-to-all-start) | async-done | bytes 524320 | tf_op jit(solution)/shard_map/all_to_all | solution.py:359
  60.3 0.1 reduce_sum.18
  60.4 0.7 broadcast_in_dim.4
  61.2 4.6 %all-to-all-start.1 = ((bf16[128,8,128]{2,1,0:T(8,128)(2,1)}), bf16[128,8,128]{2,1,0:T(8,128)(2,1)S(1)}, u32[]{:S(2)}, u32[]{:S(2)}) async-start(bf16[128,8,128]{2,1,0:T(8,128)(2,1)} %broadcast_in_dim.4), calls=%async_computation.1 | async-start | bytes 524288 | tf_op jit(solution)/shard_map/all_to_all | solution.py:361
  65.9 2.3 %own_columns.2.refs_6_ = bf16[16,256,256]{2,1,0:T(8,128)(2,1)} custom-call(s32[1]{0:T(128)} %bitcast.slot_ref.refs_0_, bf16[2048,128]{1,0:T(8,128)(2,1)S(1)} %get-tuple-element.9.refs_0_, bf16[2048,128]{1,0:T(8,128)(2,1)S(1)} %get-tuple-element.10.refs_1_, bf16[2048,128]{1,0:T(8,128)(2,1)S(1)} %collective-permute-done.6.refs_2_, ...), custom_call_target="tpu_custom_call" | custom-call | tf_op jit(solution)/shard_map/own_columns/pallas_call | solution.py:180
  68.3 15.6 %mirror_product.2.refs_14_ = f32[8,256,256]{2,1,0:T(8,128)S(1)} custom-call(s32[1]{0:T(128)} %bitcast.slot_ref.refs_0_, s32[1,8192]{1,0:T(1,128)S(1)} %copy-done, s32[8,8]{1,0:T(8,128)S(1)} %copy-done.2, bf16[2048,128]{1,0:T(8,128)(2,1)} %collective-permute-done.8.refs_0_, bf16[2048,128]{1,0:T(8,128)(2,1)} %copy-done.5, ...), custom_call_target="tpu_custom_call" | custom-call | tf_op jit(solution)/shard_map/mirror_product/pallas_call | solution.py:225
  83.9 0.8 copy-done.8
  84.7 14.2 %finish.1 = (f32[2048,128]{1,0:T(8,128)}, f32[2048,128]{1,0:T(8,128)}, bf16[2048,128]{1,0:T(8,128)(2,1)S(1)}, bf16[2048,128]{1,0:T(8,128)(2,1)S(1)}, f32[1024,128]{1,0:T(8,128)}) custom-call(s32[1]{0:T(128)} %bitcast.slot_ref.refs_0_, s32[8,8]{1,0:T(8,128)S(1)} %copy-done.3, bf16[2048,128]{1,0:T(8,128)(2,1)} %collective-permute-done.1.refs_2_, ...), custom_call_target="tpu_custom_call" | custom-call | tf_op jit(solution)/shard_map/finish/pallas_call | solution.py:331
  98.9 1.4 collective-permute-start.22
  100.3 0.1 collective-permute-start.16
  100.4 2.6 %collective-permute-start.14 = (bf16[2048,128]{1,0:T(8,128)(2,1)S(1)}, bf16[2048,128]{1,0:T(8,128)(2,1)}, u32[]{:S(2)}, u32[]{:S(2)}) collective-permute-start(bf16[2048,128]{1,0:T(8,128)(2,1)S(1)} %get-tuple-element.11.refs_0_), channel_id=1, source_target_pairs={{0,66},{1,67},{2,64},{3,65},{4,70},{5,71},{6,68},{7,69},{8,74},{9,... | collective-permute-start | bytes 1572872 | tf_op jit(solution)/shard_map/ppermute | solution.py:25
  103.1 2.4 %collective-permute-start.20 = (bf16[2048,128]{1,0:T(8,128)(2,1)S(1)}, bf16[2048,128]{1,0:T(8,128)(2,1)S(1)}, u32[]{:S(2)}, u32[]{:S(2)}) collective-permute-start(bf16[2048,128]{1,0:T(8,128)(2,1)S(1)} %get-tuple-element.11.refs_0_), channel_id=1, source_target_pairs={{0,1},{1,0},{2,3},{3,2},{4,5},{5,4},{6,7},{7,6},{8,9},{9,8},{10,11... | collective-permute-start | bytes 1572872 | tf_op jit(solution)/shard_map/ppermute | solution.py:25
  105.5 5.8 %collective-permute-done.22.refs_0_ = bf16[2048,128]{1,0:T(8,128)(2,1)S(1)} collective-permute-done((bf16[2048,128]{1,0:T(8,128)(2,1)S(1)}, bf16[2048,128]{1,0:T(8,128)(2,1)S(1)}, u32[]{:S(2)}, u32[]{:S(2)}) %collective-permute-start.22) | collective-permute-done | bytes 524320 | tf_op jit(solution)/shard_map/ppermute | solution.py:25
  111.3 3.7 %collective-permute-start.21 = (bf16[2048,128]{1,0:T(8,128)(2,1)S(1)}, bf16[2048,128]{1,0:T(8,128)(2,1)S(1)}, u32[]{:S(2)}, u32[]{:S(2)}) collective-permute-start(bf16[2048,128]{1,0:T(8,128)(2,1)S(1)} %get-tuple-element.12.refs_1_), channel_id=1, source_target_pairs={{0,1},{1,0},{2,3},{3,2},{4,5},{5,4},{6,7},{7,6},{8,9},{9,8},{10,11... | collective-permute-start | bytes 1572872 | tf_op jit(solution)/shard_map/ppermute | solution.py:25
  115.0 7.5 %collective-permute-done.16.refs_1_ = bf16[2048,128]{1,0:T(8,128)(2,1)} collective-permute-done((bf16[2048,128]{1,0:T(8,128)(2,1)S(1)}, bf16[2048,128]{1,0:T(8,128)(2,1)}, u32[]{:S(2)}, u32[]{:S(2)}) %collective-permute-start.16) | collective-permute-done | bytes 524320 | tf_op jit(solution)/shard_map/ppermute | solution.py:25
  122.6 2.1 %collective-permute-start.23 = (bf16[2048,128]{1,0:T(8,128)(2,1)S(1)}, bf16[2048,128]{1,0:T(8,128)(2,1)}, u32[]{:S(2)}, u32[]{:S(2)}) collective-permute-start(bf16[2048,128]{1,0:T(8,128)(2,1)S(1)} %collective-permute-done.22.refs_0_), channel_id=1, source_target_pairs={{0,1},{1,0},{2,3},{3,2},{4,5},{5,4},{6,7},{7,6},{8,9},{9,8},{10,11... | collective-permute-start | bytes 1572872 | tf_op jit(solution)/shard_map/ppermute | solution.py:25
  124.7 1.4 collective-permute-start.15
  126.0 2.2 %collective-permute-start.17 = (bf16[2048,128]{1,0:T(8,128)(2,1)}, bf16[2048,128]{1,0:T(8,128)(2,1)}, u32[]{:S(2)}, u32[]{:S(2)}) collective-permute-start(bf16[2048,128]{1,0:T(8,128)(2,1)} %collective-permute-done.16.refs_1_), channel_id=1, source_target_pairs={{0,66},{1,67},{2,64},{3,65},{4,70},{5,71},{6,68},{7,69},{8,74},{9,... | collective-permute-start | bytes 1572872 | tf_op jit(solution)/shard_map/ppermute | solution.py:25
  128.2 8.9 %all-to-all-start.2 = ((f32[128,8,128]{2,1,0:T(8,128)}), f32[128,8,128]{2,1,0:T(8,128)S(1)}, u32[]{:S(2)}, u32[]{:S(2)}) async-start(f32[128,8,128]{2,1,0:T(8,128)} %bitcast.14), calls=%async_computation.2 | async-start | bytes 1048576 | tf_op jit(solution)/shard_map/all_to_all | solution.py:359
  137.1 1.1 collective-permute-start.24
  138.2 0.1 collective-permute-start.26
  138.3 0.4 collective-permute-start.27
  138.7 0.6 collective-permute-start.18
  139.3 0.4 collective-permute-done.17.refs_3_
  139.7 6.0 %collective-permute-start.19 = (bf16[2048,128]{1,0:T(8,128)(2,1)}, bf16[2048,128]{1,0:T(8,128)(2,1)}, u32[]{:S(2)}, u32[]{:S(2)}) collective-permute-start(bf16[2048,128]{1,0:T(8,128)(2,1)} %collective-permute-done.17.refs_3_), channel_id=1, source_target_pairs={{0,1},{1,0},{2,3},{3,2},{4,5},{5,4},{6,7},{7,6},{8,9},{9,8},{10,11... | collective-permute-start | bytes 1572872 | tf_op jit(solution)/shard_map/ppermute | solution.py:25
  145.7 5.0 %all-to-all-done.2 = f32[128,8,128]{2,1,0:T(8,128)S(1)} async-done(((f32[128,8,128]{2,1,0:T(8,128)}), f32[128,8,128]{2,1,0:T(8,128)S(1)}, u32[]{:S(2)}, u32[]{:S(2)}) %all-to-all-start.2) | async-done | bytes 524320 | tf_op jit(solution)/shard_map/all_to_all | solution.py:359
  150.7 0.1 reduce_sum.19
  150.8 0.7 broadcast_in_dim.5
  151.6 6.1 %all-to-all-start.3 = ((bf16[128,8,128]{2,1,0:T(8,128)(2,1)}), bf16[128,8,128]{2,1,0:T(8,128)(2,1)S(1)}, u32[]{:S(2)}, u32[]{:S(2)}) async-start(bf16[128,8,128]{2,1,0:T(8,128)(2,1)} %broadcast_in_dim.5), calls=%async_computation.3 | async-start | bytes 524288 | tf_op jit(solution)/shard_map/all_to_all | solution.py:361
  157.7 2.3 %own_columns.3.refs_6_ = bf16[16,256,256]{2,1,0:T(8,128)(2,1)} custom-call(s32[1]{0:T(128)} %bitcast.slot_ref.refs_0_, bf16[2048,128]{1,0:T(8,128)(2,1)S(1)} %get-tuple-element.11.refs_0_, bf16[2048,128]{1,0:T(8,128)(2,1)S(1)} %get-tuple-element.12.refs_1_, bf16[2048,128]{1,0:T(8,128)(2,1)S(1)} %collective-permute-done.20.refs_2_, ...), custom_call_target="tpu_custom_call" | custom-call | tf_op jit(solution)/shard_map/own_columns/pallas_call | solution.py:180
  160.1 15.6 %mirror_product.3.refs_14_ = f32[8,256,256]{2,1,0:T(8,128)S(1)} custom-call(s32[1]{0:T(128)} %bitcast.slot_ref.refs_0_, s32[1,8192]{1,0:T(1,128)S(1)} %copy-done, s32[8,8]{1,0:T(8,128)S(1)} %copy-done.2, bf16[2048,128]{1,0:T(8,128)(2,1)} %copy-done.7, bf16[2048,128]{1,0:T(8,128)(2,1)} %collective-permute-done.16.refs_1_, ...), custom_call_target="tpu_custom_call" | custom-call | tf_op jit(solution)/shard_map/mirror_product/pallas_call | solution.py:225
  175.7 12.5 %finish_last.1 = (f32[2048,128]{1,0:T(8,128)}, f32[2048,128]{1,0:T(8,128)}) custom-call(s32[1]{0:T(128)} %bitcast.slot_ref.refs_0_, s32[8,8]{1,0:T(8,128)S(1)} %copy-done.3, bf16[2048,128]{1,0:T(8,128)(2,1)} %collective-permute-done.15.refs_2_, bf16[2048,128]{1,0:T(8,128)(2,1)} %collective-permute-done.17.refs_3_, ...), custom_call_target="tpu_custom_call" | custom-call | tf_op jit(solution)/shard_map/finish_last/pallas_call | solution.py:331
  (46 shorter events, 0.3 us)
Async XLA Ops:
  2.3 13.6 %collective-permute-start.2 = (bf16[2048,128]{1,0:T(8,128)(2,1)S(1)}, bf16[2048,128]{1,0:T(8,128)(2,1)S(1)}, u32[]{:S(2)}, u32[]{:S(2)}) collective-permute-start(bf16[2048,128]{1,0:T(8,128)(2,1)S(1)} %get-tuple-element.10.refs_1_), channel_id=1, source_target_pairs={{0,64},{1,65},{2,66},{3,67},{4,68},{5,69},{6,70},{7,71},{8,72},{9,... | collective-permute-start | bytes 1572872 | tf_op jit(solution)/shard_map/ppermute | solution.py:25
  4.5 14.1 %collective-permute-start = (bf16[2048,128]{1,0:T(8,128)(2,1)S(1)}, bf16[2048,128]{1,0:T(8,128)(2,1)}, u32[]{:S(2)}, u32[]{:S(2)}) collective-permute-start(bf16[2048,128]{1,0:T(8,128)(2,1)S(1)} %get-tuple-element.9.refs_0_), channel_id=1, source_target_pairs={{0,66},{1,67},{2,64},{3,65},{4,70},{5,71},{6,68},{7,69},{8,74},{9,... | collective-permute-start | bytes 1572872 | tf_op jit(solution)/shard_map/ppermute | solution.py:25
  6.4 23.1 %collective-permute-start.11 = (bf16[2048,128]{1,0:T(8,128)(2,1)S(1)}, bf16[2048,128]{1,0:T(8,128)(2,1)S(1)}, u32[]{:S(2)}, u32[]{:S(2)}) collective-permute-start(bf16[2048,128]{1,0:T(8,128)(2,1)S(1)} %get-tuple-element.10.refs_1_), channel_id=1, source_target_pairs={{0,66},{1,67},{2,64},{3,65},{4,70},{5,71},{6,68},{7,69},{8,74},{9,... | collective-permute-start | bytes 1572872 | tf_op jit(solution)/shard_map/ppermute | solution.py:25
  7.1 22.3 %collective-permute-start.8 = (bf16[2048,128]{1,0:T(8,128)(2,1)S(1)}, bf16[2048,128]{1,0:T(8,128)(2,1)}, u32[]{:S(2)}, u32[]{:S(2)}) collective-permute-start(bf16[2048,128]{1,0:T(8,128)(2,1)S(1)} %get-tuple-element.9.refs_0_), channel_id=1, source_target_pairs={{0,64},{1,65},{2,66},{3,67},{4,68},{5,69},{6,70},{7,71},{8,72},{9,... | collective-permute-start | bytes 1572872 | tf_op jit(solution)/shard_map/ppermute | solution.py:25
  7.2 39.5 %collective-permute-start.6 = (bf16[2048,128]{1,0:T(8,128)(2,1)S(1)}, bf16[2048,128]{1,0:T(8,128)(2,1)S(1)}, u32[]{:S(2)}, u32[]{:S(2)}) collective-permute-start(bf16[2048,128]{1,0:T(8,128)(2,1)S(1)} %get-tuple-element.9.refs_0_), channel_id=1, source_target_pairs={{0,1},{1,0},{2,3},{3,2},{4,5},{5,4},{6,7},{7,6},{8,9},{9,8},{10,11... | collective-permute-start | bytes 1572872 | tf_op jit(solution)/shard_map/ppermute | solution.py:25
  15.9 20.1 %copy-start.5 = (bf16[2048,128]{1,0:T(8,128)(2,1)}, bf16[2048,128]{1,0:T(8,128)(2,1)S(1)}, u32[]{:S(2)}) copy-start(bf16[2048,128]{1,0:T(8,128)(2,1)S(1)} %collective-permute-done.2.refs_1_) | copy-start | bytes 1572868
  15.9 32.0 %collective-permute-start.7 = (bf16[2048,128]{1,0:T(8,128)(2,1)S(1)}, bf16[2048,128]{1,0:T(8,128)(2,1)S(1)}, u32[]{:S(2)}, u32[]{:S(2)}) collective-permute-start(bf16[2048,128]{1,0:T(8,128)(2,1)S(1)} %get-tuple-element.10.refs_1_), channel_id=1, source_target_pairs={{0,1},{1,0},{2,3},{3,2},{4,5},{5,4},{6,7},{7,6},{8,9},{9,8},{10,11... | collective-permute-start | bytes 1572872 | tf_op jit(solution)/shard_map/ppermute | solution.py:25
  18.5 29.4 %collective-permute-start.10 = (bf16[2048,128]{1,0:T(8,128)(2,1)S(1)}, bf16[2048,128]{1,0:T(8,128)(2,1)}, u32[]{:S(2)}, u32[]{:S(2)}) collective-permute-start(bf16[2048,128]{1,0:T(8,128)(2,1)S(1)} %collective-permute-done.2.refs_1_), channel_id=1, source_target_pairs={{0,1},{1,0},{2,3},{3,2},{4,5},{5,4},{6,7},{7,6},{8,9},{9,8},{10,11... | collective-permute-start | bytes 1572872 | tf_op jit(solution)/shard_map/ppermute | solution.py:25
  29.4 6.5 %copy-start.6 = (bf16[2048,128]{1,0:T(8,128)(2,1)}, bf16[2048,128]{1,0:T(8,128)(2,1)S(1)}, u32[]{:S(2)}) copy-start(bf16[2048,128]{1,0:T(8,128)(2,1)S(1)} %collective-permute-done.11.refs_5_) | copy-start | bytes 1572868
  29.4 18.9 %collective-permute-start.1 = (bf16[2048,128]{1,0:T(8,128)(2,1)}, bf16[2048,128]{1,0:T(8,128)(2,1)}, u32[]{:S(2)}, u32[]{:S(2)}) collective-permute-start(bf16[2048,128]{1,0:T(8,128)(2,1)} %collective-permute-done.refs_4_), channel_id=1, source_target_pairs={{0,64},{1,65},{2,66},{3,67},{4,68},{5,69},{6,70},{7,71},{8,72},{9,... | collective-permute-start | bytes 1572872 | tf_op jit(solution)/shard_map/ppermute | solution.py:25
  29.5 19.0 %collective-permute-start.3 = (bf16[2048,128]{1,0:T(8,128)(2,1)S(1)}, bf16[2048,128]{1,0:T(8,128)(2,1)}, u32[]{:S(2)}, u32[]{:S(2)}) collective-permute-start(bf16[2048,128]{1,0:T(8,128)(2,1)S(1)} %collective-permute-done.2.refs_1_), channel_id=1, source_target_pairs={{0,66},{1,67},{2,64},{3,65},{4,70},{5,71},{6,68},{7,69},{8,74},{9,... | collective-permute-start | bytes 1572872 | tf_op jit(solution)/shard_map/ppermute | solution.py:25
  35.9 24.4 %all-to-all-start = ((f32[128,8,128]{2,1,0:T(8,128)}), f32[128,8,128]{2,1,0:T(8,128)S(1)}, u32[]{:S(2)}, u32[]{:S(2)}) async-start(f32[128,8,128]{2,1,0:T(8,128)} %bitcast.13), calls=%async_computation | async-start | bytes 1048576 | tf_op jit(solution)/shard_map/all_to_all | solution.py:359
  46.7 21.5 %collective-permute-start.12 = (bf16[2048,128]{1,0:T(8,128)(2,1)}, bf16[2048,128]{1,0:T(8,128)(2,1)}, u32[]{:S(2)}, u32[]{:S(2)}) collective-permute-start(bf16[2048,128]{1,0:T(8,128)(2,1)} %collective-permute-done.refs_4_), channel_id=1, source_target_pairs={{0,1},{1,0},{2,3},{3,2},{4,5},{5,4},{6,7},{7,6},{8,9},{9,8},{10,11... | collective-permute-start | bytes 1572872 | tf_op jit(solution)/shard_map/ppermute | solution.py:25
  47.8 20.4 %collective-permute-start.13 = (bf16[2048,128]{1,0:T(8,128)(2,1)}, bf16[2048,128]{1,0:T(8,128)(2,1)}, u32[]{:S(2)}, u32[]{:S(2)}) collective-permute-start(bf16[2048,128]{1,0:T(8,128)(2,1)} %copy-done.6), channel_id=1, source_target_pairs={{0,1},{1,0},{2,3},{3,2},{4,5},{5,4},{6,7},{7,6},{8,9},{9,8},{10,11... | collective-permute-start | bytes 1572872 | tf_op jit(solution)/shard_map/ppermute | solution.py:25
  47.9 20.3 %collective-permute-start.9 = (bf16[2048,128]{1,0:T(8,128)(2,1)}, bf16[2048,128]{1,0:T(8,128)(2,1)}, u32[]{:S(2)}, u32[]{:S(2)}) collective-permute-start(bf16[2048,128]{1,0:T(8,128)(2,1)} %collective-permute-done.8.refs_0_), channel_id=1, source_target_pairs={{0,1},{1,0},{2,3},{3,2},{4,5},{5,4},{6,7},{7,6},{8,9},{9,8},{10,11... | collective-permute-start | bytes 1572872 | tf_op jit(solution)/shard_map/ppermute | solution.py:25
  48.4 35.5 %collective-permute-start.4 = (bf16[2048,128]{1,0:T(8,128)(2,1)}, bf16[2048,128]{1,0:T(8,128)(2,1)}, u32[]{:S(2)}, u32[]{:S(2)}) collective-permute-start(bf16[2048,128]{1,0:T(8,128)(2,1)} %collective-permute-done.1.refs_2_), channel_id=1, source_target_pairs={{0,1},{1,0},{2,3},{3,2},{4,5},{5,4},{6,7},{7,6},{8,9},{9,8},{10,11... | collective-permute-start | bytes 1572872 | tf_op jit(solution)/shard_map/ppermute | solution.py:25
  48.5 35.4 %collective-permute-start.5 = (bf16[2048,128]{1,0:T(8,128)(2,1)}, bf16[2048,128]{1,0:T(8,128)(2,1)S(1)}, u32[]{:S(2)}, u32[]{:S(2)}) collective-permute-start(bf16[2048,128]{1,0:T(8,128)(2,1)} %collective-permute-done.3.refs_3_), channel_id=1, source_target_pairs={{0,1},{1,0},{2,3},{3,2},{4,5},{5,4},{6,7},{7,6},{8,9},{9,8},{10,11... | collective-permute-start | bytes 1572872 | tf_op jit(solution)/shard_map/ppermute | solution.py:25
  61.2 22.7 %all-to-all-start.1 = ((bf16[128,8,128]{2,1,0:T(8,128)(2,1)}), bf16[128,8,128]{2,1,0:T(8,128)(2,1)S(1)}, u32[]{:S(2)}, u32[]{:S(2)}) async-start(bf16[128,8,128]{2,1,0:T(8,128)(2,1)} %broadcast_in_dim.4), calls=%async_computation.1 | async-start | bytes 524288 | tf_op jit(solution)/shard_map/all_to_all | solution.py:361
  65.8 2.4 %copy-start = (s32[1,8192]{1,0:T(1,128)S(1)}, s32[1,8192]{1,0:T(1,128)}, u32[]{:S(2)}) copy-start(s32[1,8192]{1,0:T(1,128)} %partner_ref.3) | copy-start | bytes 98308
  65.8 2.4 %copy-start.2 = (s32[8,8]{1,0:T(8,128)S(1)}, s32[8,8]{1,0:T(8,128)}, u32[]{:S(2)}) copy-start(s32[8,8]{1,0:T(8,128)} %list_ref.3) | copy-start | bytes 772
  68.2 16.5 %copy-start.1 = (f32[2048]{0:T(1024)S(1)}, f32[2048]{0:T(1024)}, u32[]{:S(2)}) copy-start(f32[2048]{0:T(1024)} %param.12) | copy-start | bytes 24580
  68.2 16.5 %copy-start.3 = (s32[8,8]{1,0:T(8,128)S(1)}, s32[8,8]{1,0:T(8,128)}, u32[]{:S(2)}) copy-start(s32[8,8]{1,0:T(8,128)} %refs_1_.3) | copy-start | bytes 772
  68.2 16.5 %copy-start.4 = (f32[128]{0:T(128)S(1)}, f32[128]{0:T(128)}, u32[]{:S(2)}) copy-start(f32[128]{0:T(128)} %param.13) | copy-start | bytes 1540
  83.9 0.8 copy-start.8
  98.9 12.4 %collective-permute-start.22 = (bf16[2048,128]{1,0:T(8,128)(2,1)S(1)}, bf16[2048,128]{1,0:T(8,128)(2,1)S(1)}, u32[]{:S(2)}, u32[]{:S(2)}) collective-permute-start(bf16[2048,128]{1,0:T(8,128)(2,1)S(1)} %get-tuple-element.11.refs_0_), channel_id=1, source_target_pairs={{0,64},{1,65},{2,66},{3,67},{4,68},{5,69},{6,70},{7,71},{8,72},{9,... | collective-permute-start | bytes 1572872 | tf_op jit(solution)/shard_map/ppermute | solution.py:25
  100.3 22.2 %collective-permute-start.16 = (bf16[2048,128]{1,0:T(8,128)(2,1)S(1)}, bf16[2048,128]{1,0:T(8,128)(2,1)}, u32[]{:S(2)}, u32[]{:S(2)}) collective-permute-start(bf16[2048,128]{1,0:T(8,128)(2,1)S(1)} %get-tuple-element.12.refs_1_), channel_id=1, source_target_pairs={{0,64},{1,65},{2,66},{3,67},{4,68},{5,69},{6,70},{7,71},{8,72},{9,... | collective-permute-start | bytes 1572872 | tf_op jit(solution)/shard_map/ppermute | solution.py:25
  100.4 24.2 %collective-permute-start.14 = (bf16[2048,128]{1,0:T(8,128)(2,1)S(1)}, bf16[2048,128]{1,0:T(8,128)(2,1)}, u32[]{:S(2)}, u32[]{:S(2)}) collective-permute-start(bf16[2048,128]{1,0:T(8,128)(2,1)S(1)} %get-tuple-element.11.refs_0_), channel_id=1, source_target_pairs={{0,66},{1,67},{2,64},{3,65},{4,70},{5,71},{6,68},{7,69},{8,74},{9,... | collective-permute-start | bytes 1572872 | tf_op jit(solution)/shard_map/ppermute | solution.py:25
  103.1 22.9 %collective-permute-start.25 = (bf16[2048,128]{1,0:T(8,128)(2,1)S(1)}, bf16[2048,128]{1,0:T(8,128)(2,1)}, u32[]{:S(2)}, u32[]{:S(2)}) collective-permute-start(bf16[2048,128]{1,0:T(8,128)(2,1)S(1)} %get-tuple-element.12.refs_1_), channel_id=1, source_target_pairs={{0,66},{1,67},{2,64},{3,65},{4,70},{5,71},{6,68},{7,69},{8,74},{9,... | collective-permute-start | bytes 1572872 | tf_op jit(solution)/shard_map/ppermute | solution.py:25
  103.1 33.9 %collective-permute-start.20 = (bf16[2048,128]{1,0:T(8,128)(2,1)S(1)}, bf16[2048,128]{1,0:T(8,128)(2,1)S(1)}, u32[]{:S(2)}, u32[]{:S(2)}) collective-permute-start(bf16[2048,128]{1,0:T(8,128)(2,1)S(1)} %get-tuple-element.11.refs_0_), channel_id=1, source_target_pairs={{0,1},{1,0},{2,3},{3,2},{4,5},{5,4},{6,7},{7,6},{8,9},{9,8},{10,11... | collective-permute-start | bytes 1572872 | tf_op jit(solution)/shard_map/ppermute | solution.py:25
  111.3 48.7 %copy-start.7 = (bf16[2048,128]{1,0:T(8,128)(2,1)}, bf16[2048,128]{1,0:T(8,128)(2,1)S(1)}, u32[]{:S(2)}) copy-start(bf16[2048,128]{1,0:T(8,128)(2,1)S(1)} %collective-permute-done.22.refs_0_) | copy-start | bytes 1572868
  111.3 26.9 %collective-permute-start.21 = (bf16[2048,128]{1,0:T(8,128)(2,1)S(1)}, bf16[2048,128]{1,0:T(8,128)(2,1)S(1)}, u32[]{:S(2)}, u32[]{:S(2)}) collective-permute-start(bf16[2048,128]{1,0:T(8,128)(2,1)S(1)} %get-tuple-element.12.refs_1_), channel_id=1, source_target_pairs={{0,1},{1,0},{2,3},{3,2},{4,5},{5,4},{6,7},{7,6},{8,9},{9,8},{10,11... | collective-permute-start | bytes 1572872 | tf_op jit(solution)/shard_map/ppermute | solution.py:25
  122.6 15.8 %collective-permute-start.23 = (bf16[2048,128]{1,0:T(8,128)(2,1)S(1)}, bf16[2048,128]{1,0:T(8,128)(2,1)}, u32[]{:S(2)}, u32[]{:S(2)}) collective-permute-start(bf16[2048,128]{1,0:T(8,128)(2,1)S(1)} %collective-permute-done.22.refs_0_), channel_id=1, source_target_pairs={{0,1},{1,0},{2,3},{3,2},{4,5},{5,4},{6,7},{7,6},{8,9},{9,8},{10,11... | collective-permute-start | bytes 1572872 | tf_op jit(solution)/shard_map/ppermute | solution.py:25
  124.7 14.1 %collective-permute-start.15 = (bf16[2048,128]{1,0:T(8,128)(2,1)}, bf16[2048,128]{1,0:T(8,128)(2,1)}, u32[]{:S(2)}, u32[]{:S(2)}) collective-permute-start(bf16[2048,128]{1,0:T(8,128)(2,1)} %collective-permute-done.14.refs_4_), channel_id=1, source_target_pairs={{0,64},{1,65},{2,66},{3,67},{4,68},{5,69},{6,70},{7,71},{8,72},{9,... | collective-permute-start | bytes 1572872 | tf_op jit(solution)/shard_map/ppermute | solution.py:25
  126.0 13.7 %collective-permute-start.17 = (bf16[2048,128]{1,0:T(8,128)(2,1)}, bf16[2048,128]{1,0:T(8,128)(2,1)}, u32[]{:S(2)}, u32[]{:S(2)}) collective-permute-start(bf16[2048,128]{1,0:T(8,128)(2,1)} %collective-permute-done.16.refs_1_), channel_id=1, source_target_pairs={{0,66},{1,67},{2,64},{3,65},{4,70},{5,71},{6,68},{7,69},{8,74},{9,... | collective-permute-start | bytes 1572872 | tf_op jit(solution)/shard_map/ppermute | solution.py:25
  128.2 22.5 %all-to-all-start.2 = ((f32[128,8,128]{2,1,0:T(8,128)}), f32[128,8,128]{2,1,0:T(8,128)S(1)}, u32[]{:S(2)}, u32[]{:S(2)}) async-start(f32[128,8,128]{2,1,0:T(8,128)} %bitcast.14), calls=%async_computation.2 | async-start | bytes 1048576 | tf_op jit(solution)/shard_map/all_to_all | solution.py:359
  137.1 23.0 %collective-permute-start.24 = (bf16[2048,128]{1,0:T(8,128)(2,1)}, bf16[2048,128]{1,0:T(8,128)(2,1)}, u32[]{:S(2)}, u32[]{:S(2)}) collective-permute-start(bf16[2048,128]{1,0:T(8,128)(2,1)} %collective-permute-done.16.refs_1_), channel_id=1, source_target_pairs={{0,1},{1,0},{2,3},{3,2},{4,5},{5,4},{6,7},{7,6},{8,9},{9,8},{10,11... | collective-permute-start | bytes 1572872 | tf_op jit(solution)/shard_map/ppermute | solution.py:25
  138.2 21.8 %collective-permute-start.26 = (bf16[2048,128]{1,0:T(8,128)(2,1)}, bf16[2048,128]{1,0:T(8,128)(2,1)}, u32[]{:S(2)}, u32[]{:S(2)}) collective-permute-start(bf16[2048,128]{1,0:T(8,128)(2,1)} %collective-permute-done.14.refs_4_), channel_id=1, source_target_pairs={{0,1},{1,0},{2,3},{3,2},{4,5},{5,4},{6,7},{7,6},{8,9},{9,8},{10,11... | collective-permute-start | bytes 1572872 | tf_op jit(solution)/shard_map/ppermute | solution.py:25
  138.3 21.7 %collective-permute-start.27 = (bf16[2048,128]{1,0:T(8,128)(2,1)}, bf16[2048,128]{1,0:T(8,128)(2,1)}, u32[]{:S(2)}, u32[]{:S(2)}) collective-permute-start(bf16[2048,128]{1,0:T(8,128)(2,1)} %collective-permute-done.25.refs_5_), channel_id=1, source_target_pairs={{0,1},{1,0},{2,3},{3,2},{4,5},{5,4},{6,7},{7,6},{8,9},{9,8},{10,11... | collective-permute-start | bytes 1572872 | tf_op jit(solution)/shard_map/ppermute | solution.py:25
  138.7 36.9 %collective-permute-start.18 = (bf16[2048,128]{1,0:T(8,128)(2,1)}, bf16[2048,128]{1,0:T(8,128)(2,1)}, u32[]{:S(2)}, u32[]{:S(2)}) collective-permute-start(bf16[2048,128]{1,0:T(8,128)(2,1)} %collective-permute-done.15.refs_2_), channel_id=1, source_target_pairs={{0,1},{1,0},{2,3},{3,2},{4,5},{5,4},{6,7},{7,6},{8,9},{9,8},{10,11... | collective-permute-start | bytes 1572872 | tf_op jit(solution)/shard_map/ppermute | solution.py:25
  139.7 36.0 %collective-permute-start.19 = (bf16[2048,128]{1,0:T(8,128)(2,1)}, bf16[2048,128]{1,0:T(8,128)(2,1)}, u32[]{:S(2)}, u32[]{:S(2)}) collective-permute-start(bf16[2048,128]{1,0:T(8,128)(2,1)} %collective-permute-done.17.refs_3_), channel_id=1, source_target_pairs={{0,1},{1,0},{2,3},{3,2},{4,5},{5,4},{6,7},{7,6},{8,9},{9,8},{10,11... | collective-permute-start | bytes 1572872 | tf_op jit(solution)/shard_map/ppermute | solution.py:25
  151.6 24.1 %all-to-all-start.3 = ((bf16[128,8,128]{2,1,0:T(8,128)(2,1)}), bf16[128,8,128]{2,1,0:T(8,128)(2,1)S(1)}, u32[]{:S(2)}, u32[]{:S(2)}) async-start(bf16[128,8,128]{2,1,0:T(8,128)(2,1)} %broadcast_in_dim.5), calls=%async_computation.3 | async-start | bytes 524288 | tf_op jit(solution)/shard_map/all_to_all | solution.py:361

commit v6 on v5

--- a/solution.py
+++ b/solution.py
@@ -162,7 +162,8 @@
         split_block(flat, pl.multiple_of(block * 2 * BLK, 2 * BLK), first + block, out, select)
         return carry
 
-    lax.fori_loop(0, flat.shape[0] // (2 * BLK), split, 0, unroll=16)
+    count = flat.shape[0] // (2 * BLK)
+    lax.fori_loop(0, count, split, 0, unroll=min(count, 16))
 
 
 def own_body(slot_ref, *refs):
@@ -185,6 +186,29 @@
         scratch_shapes=[pltpu.VMEM((4 * rows, NV), BF16), pltpu.SemaphoreType.DMA((4,))],
         compiler_params=pltpu.CompilerParams(vmem_limit_bytes=8 * MIB),
         name="own_columns",
+    )(slot, *chunks)
+
+
+def far_body(slot_ref, *refs):
+    chunks = refs[:2]
+    out_ref, flat, sems = refs[2:]
+    copies = load_patch(slot_ref[0] & 0, chunks, flat, sems)
+    select = split_matrix()
+    for copy in copies:
+        copy.wait()
+    split_all(flat, 0, out_ref, select)
+
+
+def far_columns(slot, chunks):
+    half = chunks[0].shape[0]
+    return pl.pallas_call(
+        far_body,
+        in_specs=[SMEM_SPEC, ANY_SPEC, ANY_SPEC],
+        out_specs=VMEM_SPEC,
+        out_shape=pltpu.HBM((half // BLK, BLK, 2 * NV), BF16),
+        scratch_shapes=[pltpu.VMEM((2 * half, NV), BF16), pltpu.SemaphoreType.DMA((2,))],
+        compiler_params=pltpu.CompilerParams(vmem_limit_bytes=8 * MIB),
+        name="far_columns",
     )(slot, *chunks)
 
 
@@ -245,9 +269,9 @@
 
 
 def finish_body(last, slot_ref, list_ref, *refs):
-    chunks = refs[:4]
-    own_hbm, x_hbm, y_hbm, energy_ref, shift_ref, kernel_hbm, basis_hbm, weight_ref, mirror_ref = refs[4:13]
-    rest = refs[13:]
+    chunks = refs[:2]
+    own_hbm, far_hbm, x_hbm, y_hbm, energy_ref, shift_ref, kernel_hbm, basis_hbm, weight_ref, mirror_ref = refs[2:12]
+    rest = refs[12:]
     if last:
         next_x_hbm, next_y_hbm = rest[:2]
         rest = rest[2:]
@@ -256,11 +280,15 @@
         rest = rest[5:]
     flat, columns, kernel, basis, x, y, levels, scratch, summed, chunk_sems, sems, save_sems = rest
     blocks = kernel.shape[0]
-    core = slot_ref[0] & 1
-    copies = load_patch(core, chunks, flat, chunk_sems)
+    copies = load_patch(slot_ref[0] & 0, chunks, flat, chunk_sems)
     count = own_hbm.shape[0]
     own_first = (slot_ref[0] // 2) * count
-    extra = [pltpu.make_async_copy(own_hbm, columns.at[pl.ds(own_first, count)], chunk_sems.at[4])]
+    far_count = far_hbm.shape[0]
+    far_first = (slot_ref[0] ^ 2) * far_count
+    extra = [
+        pltpu.make_async_copy(own_hbm, columns.at[pl.ds(own_first, count)], chunk_sems.at[4]),
+        pltpu.make_async_copy(far_hbm, columns.at[pl.ds(far_first, far_count)], chunk_sems.at[5]),
+    ]
     for copy in extra:
         copy.start()
 
@@ -286,7 +314,7 @@
     for b in range(blocks):
         for t in range(4):
             load(b, t).start()
-    split_all(flat, (1 - slot_ref[0] // 2) * count, columns, split_matrix())
+    split_all(flat, (slot_ref[0] ^ 3) * far_count, columns, split_matrix())
     for copy in extra:
         copy.wait()
     shifts = shift_ref[...]
@@ -315,7 +343,7 @@
             save(b, t).wait()
 
 
-def finish(last, slot, indices, chunks, own, x, y, energy, shift, kernel, basis, weights, mirrored):
+def finish(last, slot, indices, chunks, own, far, x, y, energy, shift, kernel, basis, weights, mirrored):
     rows, rank = basis.shape
     blocks = kernel.shape[0]
     patch = 4 * rows
@@ -330,11 +358,11 @@
 
     return pl.pallas_call(
         body,
-        in_specs=[SMEM_SPEC] * 2 + [ANY_SPEC] * 7 + [VMEM_SPEC] * 2 + [ANY_SPEC] * 2 + [VMEM_SPEC] * 2,
+        in_specs=[SMEM_SPEC] * 2 + [ANY_SPEC] * 6 + [VMEM_SPEC] * 2 + [ANY_SPEC] * 2 + [VMEM_SPEC] * 2,
         out_specs=out_specs,
         out_shape=out_shape,
         scratch_shapes=[
-            pltpu.VMEM((patch, NV), BF16),
+            pltpu.VMEM((patch // 2, NV), BF16),
             pltpu.VMEM((patch // BLK, BLK, 2 * NV), BF16),
             pltpu.VMEM(kernel.shape, BF16),
             pltpu.VMEM(basis.shape, BF16),
@@ -349,7 +377,7 @@
         ],
         compiler_params=pltpu.CompilerParams(vmem_limit_bytes=32 * MIB),
         name="finish_last" if last else "finish",
-    )(slot, indices, *in_hbm(*chunks, own, x, y), energy, shift, *in_hbm(kernel, basis), weights, mirrored)
+    )(slot, indices, *in_hbm(*chunks, own, far, x, y), energy, shift, *in_hbm(kernel, basis), weights, mirrored)
 
 
 def total_weights(partial):
@@ -387,9 +415,25 @@
         far_swap = [toggled(far_low, 1), toggled(far_high, 1)]
         mirror_chunks = [near_low, near_high] + near_swap + [far_low, far_high] + far_swap
         own_half = own_columns(slot, [low, high] + own)
-        across += [toggled(c, 1) for c in across]
+        swapped = [toggled(c, 1) for c in across]
+        far_half = far_columns(slot, across)
         mirrored = mirror_product(slot, partner, cp_list, mirror_chunks, cp_kernel)
-        out = finish(last, slot, res_list, across, own_half, x, y, levels, shifts, res_kernel, basis, weights, mirrored)
+        out = finish(
+            last,
+            slot,
+            res_list,
+            swapped,
+            own_half,
+            far_half,
+            x,
+            y,
+            levels,
+            shifts,
+            res_kernel,
+            basis,
+            weights,
+            mirrored,
+        )
         if last:
             return tuple(out)
         x, y, low, high, partial = out

time: 189 us -> 193 us (1.021)
  Pallas kernels: 68.6 us -> 72.3 us
    pallas_call x2 -> x4, Pallas kernels: 26.6 us -> 30.3 us  [the longest x2 26.1 us: finish(): pl.pallas_call(body, in_specs=[SMEM_SPEC] * 2 + [ANY_SPEC] * 6 + [VMEM_SP...]
  transfers between devices with their start and end apart: 32 -> 32, of which waited for: 7 -> 7; matrix products, arithmetic and copies ran while one was open for 1% -> 1% of each run, Pallas kernels for 21% -> 23%
where the time goes in v6:
time: 193 us; the launch traced here: 192 us
  Pallas kernels  72.3 us (37%)
  starting transfers between devices  70.7 us (37%)
  waiting for transfers between devices  45.5 us (24%)
    ppermute x28, starting transfers between devices, toggled(): lax.ppermute(array, AXES, [(i, i ^ mask) for i in range(lax.axis_size(AXE...  39.8 us
    pallas_call x2, Pallas kernels, mirror_product(): pl.pallas_call(mirror_body, in_specs=[SMEM_SPEC] * 3 + [ANY_SPEC] * 9, ou...  31.1 us
    ppermute x28, waiting for transfers between devices, toggled(): lax.ppermute(array, AXES, [(i, i ^ mask) for i in range(lax.axis_size(AXE...  29.3 us
    pallas_call x2, Pallas kernels, finish(): pl.pallas_call(body, in_specs=[SMEM_SPEC] * 2 + [ANY_SPEC] * 6 + [VMEM_SP...  26.1 us
    all_to_all x2, starting transfers between devices, total_weights(): lax.all_to_all(partial.reshape(size, part, vectors), AXES, 0, 0, tiled=True)  20.3 us
    all_to_all x2, waiting for transfers between devices, total_weights(): lax.all_to_all(partial.reshape(size, part, vectors), AXES, 0, 0, tiled=True)  16.2 us
    all_to_all x2, starting transfers between devices, total_weights(): lax.all_to_all(jnp.broadcast_to(own[None], (size, part, vectors)), AXES,...  10.5 us
    pallas_call x2, Pallas kernels, own_columns(): pl.pallas_call(own_body, in_specs=[SMEM_SPEC] + [ANY_SPEC] * 4, out_specs...  4.69 us
  transfers between devices with their start and end apart: 32, of which 7 were waited for; matrix products, arithmetic and copies ran while one was open for 1% of the time, Pallas kernels for 23%

profile of v6, /device:TPU:1, one launch (start us, length us, event | category | flops | bytes accessed | tf_op | source)
XLA Modules:
  0.0 192.4 jit_solution(14362435388323629676)
XLA Ops:
  0.6 1.6 pack.1
  2.3 2.2 %collective-permute-start.3 = (bf16[2048,128]{1,0:T(8,128)(2,1)S(1)}, bf16[2048,128]{1,0:T(8,128)(2,1)}, u32[]{:S(2)}, u32[]{:S(2)}) collective-permute-start(bf16[2048,128]{1,0:T(8,128)(2,1)S(1)} %get-tuple-element.10.refs_1_), channel_id=1, source_target_pairs={{0,64},{1,65},{2,66},{3,67},{4,68},{5,69},{6,70},{7,71},{8,72},{9,... | collective-permute-start | bytes 1572872 | tf_op jit(solution)/shard_map/ppermute | solution.py:25
  4.5 1.9 collective-permute-start
  6.4 0.8 collective-permute-start.11
  7.2 1.5 collective-permute-start.6
  8.7 7.2 %collective-permute-done.3.refs_1_ = bf16[2048,128]{1,0:T(8,128)(2,1)} collective-permute-done((bf16[2048,128]{1,0:T(8,128)(2,1)S(1)}, bf16[2048,128]{1,0:T(8,128)(2,1)}, u32[]{:S(2)}, u32[]{:S(2)}) %collective-permute-start.3) | collective-permute-done | bytes 524320 | tf_op jit(solution)/shard_map/ppermute | solution.py:25
  15.9 2.8 %collective-permute-start.7 = (bf16[2048,128]{1,0:T(8,128)(2,1)S(1)}, bf16[2048,128]{1,0:T(8,128)(2,1)S(1)}, u32[]{:S(2)}, u32[]{:S(2)}) collective-permute-start(bf16[2048,128]{1,0:T(8,128)(2,1)S(1)} %get-tuple-element.10.refs_1_), channel_id=1, source_target_pairs={{0,1},{1,0},{2,3},{3,2},{4,5},{5,4},{6,7},{7,6},{8,9},{9,8},{10,11... | collective-permute-start | bytes 1572872 | tf_op jit(solution)/shard_map/ppermute | solution.py:25
  18.6 2.9 %collective-permute-start.10 = (bf16[2048,128]{1,0:T(8,128)(2,1)}, bf16[2048,128]{1,0:T(8,128)(2,1)}, u32[]{:S(2)}, u32[]{:S(2)}) collective-permute-start(bf16[2048,128]{1,0:T(8,128)(2,1)} %collective-permute-done.3.refs_1_), channel_id=1, source_target_pairs={{0,1},{1,0},{2,3},{3,2},{4,5},{5,4},{6,7},{7,6},{8,9},{9,8},{10,11... | collective-permute-start | bytes 1572872 | tf_op jit(solution)/shard_map/ppermute | solution.py:25
  21.5 8.0 %collective-permute-done.11.refs_5_ = bf16[2048,128]{1,0:T(8,128)(2,1)} collective-permute-done((bf16[2048,128]{1,0:T(8,128)(2,1)S(1)}, bf16[2048,128]{1,0:T(8,128)(2,1)}, u32[]{:S(2)}, u32[]{:S(2)}) %collective-permute-start.11) | collective-permute-done | bytes 524320 | tf_op jit(solution)/shard_map/ppermute | solution.py:25
  29.6 1.9 collective-permute-start.4
  31.5 4.5 %project.1 = f32[1024,128]{1,0:T(8,128)} custom-call(f32[2048,128]{1,0:T(8,128)} %refs_6_.1, f32[2048,128]{1,0:T(8,128)} %refs_7_.1, bf16[2048,1024]{1,0:T(8,128)(2,1)} %refs_11_.3), custom_call_target="tpu_custom_call" | custom-call | tf_op jit(solution)/shard_map/project/pallas_call | solution.py:127
  36.0 11.3 %all-to-all-start = ((f32[128,8,128]{2,1,0:T(8,128)}), f32[128,8,128]{2,1,0:T(8,128)}, u32[]{:S(2)}, u32[]{:S(2)}) async-start(f32[128,8,128]{2,1,0:T(8,128)} %bitcast.13), calls=%async_computation | async-start | bytes 1048576 | tf_op jit(solution)/shard_map/all_to_all | solution.py:387
  47.2 1.2 collective-permute-start.12
  48.5 0.1 collective-permute-start.13
  48.6 0.4 collective-permute-start.9
  49.0 0.1 collective-permute-start.2
  49.1 0.4 collective-permute-start.5
  49.5 11.0 %all-to-all-done = f32[128,8,128]{2,1,0:T(8,128)} async-done(((f32[128,8,128]{2,1,0:T(8,128)}), f32[128,8,128]{2,1,0:T(8,128)}, u32[]{:S(2)}, u32[]{:S(2)}) %all-to-all-start) | async-done | bytes 524320 | tf_op jit(solution)/shard_map/all_to_all | solution.py:387
  60.5 1.2 reduce_sum.18
  61.7 0.7 broadcast_in_dim.4
  62.4 4.6 %all-to-all-start.1 = ((bf16[128,8,128]{2,1,0:T(8,128)(2,1)}), bf16[128,8,128]{2,1,0:T(8,128)(2,1)S(1)}, u32[]{:S(2)}, u32[]{:S(2)}) async-start(bf16[128,8,128]{2,1,0:T(8,128)(2,1)} %broadcast_in_dim.4), calls=%async_computation.1 | async-start | bytes 524288 | tf_op jit(solution)/shard_map/all_to_all | solution.py:389
  67.1 2.3 %own_columns.2.refs_4_ = bf16[16,256,256]{2,1,0:T(8,128)(2,1)} custom-call(s32[1]{0:T(128)} %bitcast.slot_ref.refs_0_, bf16[2048,128]{1,0:T(8,128)(2,1)S(1)} %get-tuple-element.9.refs_0_, bf16[2048,128]{1,0:T(8,128)(2,1)S(1)} %get-tuple-element.10.refs_1_, bf16[2048,128]{1,0:T(8,128)(2,1)S(1)} %collective-permute-done.6.refs_2_, ...), custom_call_target="tpu_custom_call" | custom-call | tf_op jit(solution)/shard_map/own_columns/pallas_call | solution.py:181
  69.4 1.6 far_columns.2.refs_5_
  71.1 15.6 %mirror_product.2.refs_13_ = f32[8,256,256]{2,1,0:T(8,128)S(1)} custom-call(s32[1]{0:T(128)} %bitcast.slot_ref.refs_0_, s32[1,8192]{1,0:T(1,128)S(1)} %copy-done, s32[8,8]{1,0:T(8,128)S(1)} %copy-done.2, bf16[2048,128]{1,0:T(8,128)(2,1)} %collective-permute-done.8.refs_0_, bf16[2048,128]{1,0:T(8,128)(2,1)} %collective-permute-done.3.refs_1_, ...), custom_call_target="tpu_custom_call" | custom-call | tf_op jit(solution)/shard_map/mirror_product/pallas_call | solution.py:249
  86.8 13.9 %finish.1 = (f32[2048,128]{1,0:T(8,128)}, f32[2048,128]{1,0:T(8,128)}, bf16[2048,128]{1,0:T(8,128)(2,1)S(1)}, bf16[2048,128]{1,0:T(8,128)(2,1)S(1)}, f32[1024,128]{1,0:T(8,128)}) custom-call(s32[1]{0:T(128)} %bitcast.slot_ref.refs_0_, s32[8,8]{1,0:T(8,128)S(1)} %copy-done.3, bf16[2048,128]{1,0:T(8,128)(2,1)} %collective-permute-done.2.refs_2_, ...), custom_call_target="tpu_custom_call" | custom-call | tf_op jit(solution)/shard_map/finish/pallas_call | solution.py:359
  100.6 1.4 collective-permute-start.22
  102.2 2.6 %collective-permute-start.14 = (bf16[2048,128]{1,0:T(8,128)(2,1)S(1)}, bf16[2048,128]{1,0:T(8,128)(2,1)}, u32[]{:S(2)}, u32[]{:S(2)}) collective-permute-start(bf16[2048,128]{1,0:T(8,128)(2,1)S(1)} %get-tuple-element.11.refs_0_), channel_id=1, source_target_pairs={{0,66},{1,67},{2,64},{3,65},{4,70},{5,71},{6,68},{7,69},{8,74},{9,... | collective-permute-start | bytes 1572872 | tf_op jit(solution)/shard_map/ppermute | solution.py:25
  104.9 2.3 %collective-permute-start.20 = (bf16[2048,128]{1,0:T(8,128)(2,1)S(1)}, bf16[2048,128]{1,0:T(8,128)(2,1)S(1)}, u32[]{:S(2)}, u32[]{:S(2)}) collective-permute-start(bf16[2048,128]{1,0:T(8,128)(2,1)S(1)} %get-tuple-element.11.refs_0_), channel_id=1, source_target_pairs={{0,1},{1,0},{2,3},{3,2},{4,5},{5,4},{6,7},{7,6},{8,9},{9,8},{10,11... | collective-permute-start | bytes 1572872 | tf_op jit(solution)/shard_map/ppermute | solution.py:25
  107.2 5.9 %collective-permute-done.22.refs_0_ = bf16[2048,128]{1,0:T(8,128)(2,1)S(1)} collective-permute-done((bf16[2048,128]{1,0:T(8,128)(2,1)S(1)}, bf16[2048,128]{1,0:T(8,128)(2,1)S(1)}, u32[]{:S(2)}, u32[]{:S(2)}) %collective-permute-start.22) | collective-permute-done | bytes 524320 | tf_op jit(solution)/shard_map/ppermute | solution.py:25
  113.1 3.7 %collective-permute-start.21 = (bf16[2048,128]{1,0:T(8,128)(2,1)S(1)}, bf16[2048,128]{1,0:T(8,128)(2,1)S(1)}, u32[]{:S(2)}, u32[]{:S(2)}) collective-permute-start(bf16[2048,128]{1,0:T(8,128)(2,1)S(1)} %get-tuple-element.12.refs_1_), channel_id=1, source_target_pairs={{0,1},{1,0},{2,3},{3,2},{4,5},{5,4},{6,7},{7,6},{8,9},{9,8},{10,11... | collective-permute-start | bytes 1572872 | tf_op jit(solution)/shard_map/ppermute | solution.py:25
  116.7 7.6 %collective-permute-done.17.refs_1_ = bf16[2048,128]{1,0:T(8,128)(2,1)} collective-permute-done((bf16[2048,128]{1,0:T(8,128)(2,1)S(1)}, bf16[2048,128]{1,0:T(8,128)(2,1)}, u32[]{:S(2)}, u32[]{:S(2)}) %collective-permute-start.17) | collective-permute-done | bytes 524320 | tf_op jit(solution)/shard_map/ppermute | solution.py:25
  124.3 2.1 %collective-permute-start.23 = (bf16[2048,128]{1,0:T(8,128)(2,1)S(1)}, bf16[2048,128]{1,0:T(8,128)(2,1)}, u32[]{:S(2)}, u32[]{:S(2)}) collective-permute-start(bf16[2048,128]{1,0:T(8,128)(2,1)S(1)} %collective-permute-done.22.refs_0_), channel_id=1, source_target_pairs={{0,1},{1,0},{2,3},{3,2},{4,5},{5,4},{6,7},{7,6},{8,9},{9,8},{10,11... | collective-permute-start | bytes 1572872 | tf_op jit(solution)/shard_map/ppermute | solution.py:25
  126.4 1.4 collective-permute-start.15
  127.8 2.1 %collective-permute-start.18 = (bf16[2048,128]{1,0:T(8,128)(2,1)}, bf16[2048,128]{1,0:T(8,128)(2,1)}, u32[]{:S(2)}, u32[]{:S(2)}) collective-permute-start(bf16[2048,128]{1,0:T(8,128)(2,1)} %collective-permute-done.17.refs_1_), channel_id=1, source_target_pairs={{0,66},{1,67},{2,64},{3,65},{4,70},{5,71},{6,68},{7,69},{8,74},{9,... | collective-permute-start | bytes 1572872 | tf_op jit(solution)/shard_map/ppermute | solution.py:25
  129.8 9.1 %all-to-all-start.2 = ((f32[128,8,128]{2,1,0:T(8,128)}), f32[128,8,128]{2,1,0:T(8,128)S(1)}, u32[]{:S(2)}, u32[]{:S(2)}) async-start(f32[128,8,128]{2,1,0:T(8,128)} %bitcast.14), calls=%async_computation.2 | async-start | bytes 1048576 | tf_op jit(solution)/shard_map/all_to_all | solution.py:387
  138.9 1.1 collective-permute-start.24
  140.2 0.4 collective-permute-start.27
  140.6 0.5 collective-permute-start.16
  141.1 0.5 collective-permute-done.18.refs_1_
  141.6 5.7 %collective-permute-start.19 = (bf16[2048,128]{1,0:T(8,128)(2,1)}, bf16[2048,128]{1,0:T(8,128)(2,1)}, u32[]{:S(2)}, u32[]{:S(2)}) collective-permute-start(bf16[2048,128]{1,0:T(8,128)(2,1)} %collective-permute-done.18.refs_1_), channel_id=1, source_target_pairs={{0,1},{1,0},{2,3},{3,2},{4,5},{5,4},{6,7},{7,6},{8,9},{9,8},{10,11... | collective-permute-start | bytes 1572872 | tf_op jit(solution)/shard_map/ppermute | solution.py:25
  147.3 5.2 %all-to-all-done.2 = f32[128,8,128]{2,1,0:T(8,128)S(1)} async-done(((f32[128,8,128]{2,1,0:T(8,128)}), f32[128,8,128]{2,1,0:T(8,128)S(1)}, u32[]{:S(2)}, u32[]{:S(2)}) %all-to-all-start.2) | async-done | bytes 524320 | tf_op jit(solution)/shard_map/all_to_all | solution.py:387
  152.5 0.1 reduce_sum.19
  152.7 0.7 broadcast_in_dim.5
  153.4 5.9 %all-to-all-start.3 = ((bf16[128,8,128]{2,1,0:T(8,128)(2,1)}), bf16[128,8,128]{2,1,0:T(8,128)(2,1)S(1)}, u32[]{:S(2)}, u32[]{:S(2)}) async-start(bf16[128,8,128]{2,1,0:T(8,128)(2,1)} %broadcast_in_dim.5), calls=%async_computation.3 | async-start | bytes 524288 | tf_op jit(solution)/shard_map/all_to_all | solution.py:389
  159.3 2.3 %own_columns.3.refs_4_ = bf16[16,256,256]{2,1,0:T(8,128)(2,1)} custom-call(s32[1]{0:T(128)} %bitcast.slot_ref.refs_0_, bf16[2048,128]{1,0:T(8,128)(2,1)S(1)} %get-tuple-element.11.refs_0_, bf16[2048,128]{1,0:T(8,128)(2,1)S(1)} %get-tuple-element.12.refs_1_, bf16[2048,128]{1,0:T(8,128)(2,1)S(1)} %collective-permute-done.20.refs_2_, ...), custom_call_target="tpu_custom_call" | custom-call | tf_op jit(solution)/shard_map/own_columns/pallas_call | solution.py:181
  161.7 2.7 %far_columns.3.refs_5_ = bf16[8,256,256]{2,1,0:T(8,128)(2,1)} custom-call(s32[1]{0:T(128)} %bitcast.slot_ref.refs_0_, bf16[2048,128]{1,0:T(8,128)(2,1)} %collective-permute-done.15.refs_0_, bf16[2048,128]{1,0:T(8,128)(2,1)} %collective-permute-done.18.refs_1_), custom_call_target="tpu_custom_call" | custom-call | tf_op jit(solution)/shard_map/far_columns/pallas_call | solution.py:204
  164.4 15.6 %mirror_product.3.refs_13_ = f32[8,256,256]{2,1,0:T(8,128)S(1)} custom-call(s32[1]{0:T(128)} %bitcast.slot_ref.refs_0_, s32[1,8192]{1,0:T(1,128)S(1)} %copy-done, s32[8,8]{1,0:T(8,128)S(1)} %copy-done.2, bf16[2048,128]{1,0:T(8,128)(2,1)} %copy-done.5, bf16[2048,128]{1,0:T(8,128)(2,1)} %collective-permute-done.17.refs_1_, ...), custom_call_target="tpu_custom_call" | custom-call | tf_op jit(solution)/shard_map/mirror_product/pallas_call | solution.py:249
  180.0 12.2 %finish_last.1 = (f32[2048,128]{1,0:T(8,128)}, f32[2048,128]{1,0:T(8,128)}) custom-call(s32[1]{0:T(128)} %bitcast.slot_ref.refs_0_, s32[8,8]{1,0:T(8,128)S(1)} %copy-done.3, bf16[2048,128]{1,0:T(8,128)(2,1)} %collective-permute-done.16.refs_2_, bf16[2048,128]{1,0:T(8,128)(2,1)} %collective-permute-done.19.refs_3_, bf16[16,256,256]{2,1,0:T(8,128)(2,1)} %own_columns.3.refs_4_, ...), custom_call_target="tpu_custom_call" | custom-call | tf_op jit(solution)/shard_map/finish_last/pallas_call | solution.py:359
  (44 shorter events, 0.4 us)
Async XLA Ops:
  2.3 13.6 %collective-permute-start.3 = (bf16[2048,128]{1,0:T(8,128)(2,1)S(1)}, bf16[2048,128]{1,0:T(8,128)(2,1)}, u32[]{:S(2)}, u32[]{:S(2)}) collective-permute-start(bf16[2048,128]{1,0:T(8,128)(2,1)S(1)} %get-tuple-element.10.refs_1_), channel_id=1, source_target_pairs={{0,64},{1,65},{2,66},{3,67},{4,68},{5,69},{6,70},{7,71},{8,72},{9,... | collective-permute-start | bytes 1572872 | tf_op jit(solution)/shard_map/ppermute | solution.py:25
  4.5 14.2 %collective-permute-start = (bf16[2048,128]{1,0:T(8,128)(2,1)S(1)}, bf16[2048,128]{1,0:T(8,128)(2,1)}, u32[]{:S(2)}, u32[]{:S(2)}) collective-permute-start(bf16[2048,128]{1,0:T(8,128)(2,1)S(1)} %get-tuple-element.9.refs_0_), channel_id=1, source_target_pairs={{0,66},{1,67},{2,64},{3,65},{4,70},{5,71},{6,68},{7,69},{8,74},{9,... | collective-permute-start | bytes 1572872 | tf_op jit(solution)/shard_map/ppermute | solution.py:25
  6.4 23.2 %collective-permute-start.11 = (bf16[2048,128]{1,0:T(8,128)(2,1)S(1)}, bf16[2048,128]{1,0:T(8,128)(2,1)}, u32[]{:S(2)}, u32[]{:S(2)}) collective-permute-start(bf16[2048,128]{1,0:T(8,128)(2,1)S(1)} %get-tuple-element.10.refs_1_), channel_id=1, source_target_pairs={{0,66},{1,67},{2,64},{3,65},{4,70},{5,71},{6,68},{7,69},{8,74},{9,... | collective-permute-start | bytes 1572872 | tf_op jit(solution)/shard_map/ppermute | solution.py:25
  7.1 22.4 %collective-permute-start.8 = (bf16[2048,128]{1,0:T(8,128)(2,1)S(1)}, bf16[2048,128]{1,0:T(8,128)(2,1)}, u32[]{:S(2)}, u32[]{:S(2)}) collective-permute-start(bf16[2048,128]{1,0:T(8,128)(2,1)S(1)} %get-tuple-element.9.refs_0_), channel_id=1, source_target_pairs={{0,64},{1,65},{2,66},{3,67},{4,68},{5,69},{6,70},{7,71},{8,72},{9,... | collective-permute-start | bytes 1572872 | tf_op jit(solution)/shard_map/ppermute | solution.py:25
  7.2 40.1 %collective-permute-start.6 = (bf16[2048,128]{1,0:T(8,128)(2,1)S(1)}, bf16[2048,128]{1,0:T(8,128)(2,1)S(1)}, u32[]{:S(2)}, u32[]{:S(2)}) collective-permute-start(bf16[2048,128]{1,0:T(8,128)(2,1)S(1)} %get-tuple-element.9.refs_0_), channel_id=1, source_target_pairs={{0,1},{1,0},{2,3},{3,2},{4,5},{5,4},{6,7},{7,6},{8,9},{9,8},{10,11... | collective-permute-start | bytes 1572872 | tf_op jit(solution)/shard_map/ppermute | solution.py:25
  15.9 32.6 %collective-permute-start.7 = (bf16[2048,128]{1,0:T(8,128)(2,1)S(1)}, bf16[2048,128]{1,0:T(8,128)(2,1)S(1)}, u32[]{:S(2)}, u32[]{:S(2)}) collective-permute-start(bf16[2048,128]{1,0:T(8,128)(2,1)S(1)} %get-tuple-element.10.refs_1_), channel_id=1, source_target_pairs={{0,1},{1,0},{2,3},{3,2},{4,5},{5,4},{6,7},{7,6},{8,9},{9,8},{10,11... | collective-permute-start | bytes 1572872 | tf_op jit(solution)/shard_map/ppermute | solution.py:25
  18.6 29.9 %collective-permute-start.10 = (bf16[2048,128]{1,0:T(8,128)(2,1)}, bf16[2048,128]{1,0:T(8,128)(2,1)}, u32[]{:S(2)}, u32[]{:S(2)}) collective-permute-start(bf16[2048,128]{1,0:T(8,128)(2,1)} %collective-permute-done.3.refs_1_), channel_id=1, source_target_pairs={{0,1},{1,0},{2,3},{3,2},{4,5},{5,4},{6,7},{7,6},{8,9},{9,8},{10,11... | collective-permute-start | bytes 1572872 | tf_op jit(solution)/shard_map/ppermute | solution.py:25
  29.6 19.4 %collective-permute-start.1 = (bf16[2048,128]{1,0:T(8,128)(2,1)}, bf16[2048,128]{1,0:T(8,128)(2,1)S(1)}, u32[]{:S(2)}, u32[]{:S(2)}) collective-permute-start(bf16[2048,128]{1,0:T(8,128)(2,1)} %collective-permute-done.refs_4_), channel_id=1, source_target_pairs={{0,64},{1,65},{2,66},{3,67},{4,68},{5,69},{6,70},{7,71},{8,72},{9,... | collective-permute-start | bytes 1572872 | tf_op jit(solution)/shard_map/ppermute | solution.py:25
  29.6 19.5 %collective-permute-start.4 = (bf16[2048,128]{1,0:T(8,128)(2,1)}, bf16[2048,128]{1,0:T(8,128)(2,1)S(1)}, u32[]{:S(2)}, u32[]{:S(2)}) collective-permute-start(bf16[2048,128]{1,0:T(8,128)(2,1)} %collective-permute-done.3.refs_1_), channel_id=1, source_target_pairs={{0,66},{1,67},{2,64},{3,65},{4,70},{5,71},{6,68},{7,69},{8,74},{9,... | collective-permute-start | bytes 1572872 | tf_op jit(solution)/shard_map/ppermute | solution.py:25
  36.0 24.5 %all-to-all-start = ((f32[128,8,128]{2,1,0:T(8,128)}), f32[128,8,128]{2,1,0:T(8,128)}, u32[]{:S(2)}, u32[]{:S(2)}) async-start(f32[128,8,128]{2,1,0:T(8,128)} %bitcast.13), calls=%async_computation | async-start | bytes 1048576 | tf_op jit(solution)/shard_map/all_to_all | solution.py:387
  47.2 23.8 %collective-permute-start.12 = (bf16[2048,128]{1,0:T(8,128)(2,1)}, bf16[2048,128]{1,0:T(8,128)(2,1)}, u32[]{:S(2)}, u32[]{:S(2)}) collective-permute-start(bf16[2048,128]{1,0:T(8,128)(2,1)} %collective-permute-done.refs_4_), channel_id=1, source_target_pairs={{0,1},{1,0},{2,3},{3,2},{4,5},{5,4},{6,7},{7,6},{8,9},{9,8},{10,11... | collective-permute-start | bytes 1572872 | tf_op jit(solution)/shard_map/ppermute | solution.py:25
  48.5 22.6 %collective-permute-start.13 = (bf16[2048,128]{1,0:T(8,128)(2,1)}, bf16[2048,128]{1,0:T(8,128)(2,1)}, u32[]{:S(2)}, u32[]{:S(2)}) collective-permute-start(bf16[2048,128]{1,0:T(8,128)(2,1)} %collective-permute-done.11.refs_5_), channel_id=1, source_target_pairs={{0,1},{1,0},{2,3},{3,2},{4,5},{5,4},{6,7},{7,6},{8,9},{9,8},{10,11... | collective-permute-start | bytes 1572872 | tf_op jit(solution)/shard_map/ppermute | solution.py:25
  48.6 22.5 %collective-permute-start.9 = (bf16[2048,128]{1,0:T(8,128)(2,1)}, bf16[2048,128]{1,0:T(8,128)(2,1)}, u32[]{:S(2)}, u32[]{:S(2)}) collective-permute-start(bf16[2048,128]{1,0:T(8,128)(2,1)} %collective-permute-done.8.refs_0_), channel_id=1, source_target_pairs={{0,1},{1,0},{2,3},{3,2},{4,5},{5,4},{6,7},{7,6},{8,9},{9,8},{10,11... | collective-permute-start | bytes 1572872 | tf_op jit(solution)/shard_map/ppermute | solution.py:25
  49.0 37.7 %collective-permute-start.2 = (bf16[2048,128]{1,0:T(8,128)(2,1)S(1)}, bf16[2048,128]{1,0:T(8,128)(2,1)}, u32[]{:S(2)}, u32[]{:S(2)}) collective-permute-start(bf16[2048,128]{1,0:T(8,128)(2,1)S(1)} %collective-permute-done.1.refs_0_), channel_id=1, source_target_pairs={{0,1},{1,0},{2,3},{3,2},{4,5},{5,4},{6,7},{7,6},{8,9},{9,8},{10,11... | collective-permute-start | bytes 1572872 | tf_op jit(solution)/shard_map/ppermute | solution.py:25
  49.1 37.6 %collective-permute-start.5 = (bf16[2048,128]{1,0:T(8,128)(2,1)S(1)}, bf16[2048,128]{1,0:T(8,128)(2,1)}, u32[]{:S(2)}, u32[]{:S(2)}) collective-permute-start(bf16[2048,128]{1,0:T(8,128)(2,1)S(1)} %collective-permute-done.4.refs_1_), channel_id=1, source_target_pairs={{0,1},{1,0},{2,3},{3,2},{4,5},{5,4},{6,7},{7,6},{8,9},{9,8},{10,11... | collective-permute-start | bytes 1572872 | tf_op jit(solution)/shard_map/ppermute | solution.py:25
  62.4 24.3 %all-to-all-start.1 = ((bf16[128,8,128]{2,1,0:T(8,128)(2,1)}), bf16[128,8,128]{2,1,0:T(8,128)(2,1)S(1)}, u32[]{:S(2)}, u32[]{:S(2)}) async-start(bf16[128,8,128]{2,1,0:T(8,128)(2,1)} %broadcast_in_dim.4), calls=%async_computation.1 | async-start | bytes 524288 | tf_op jit(solution)/shard_map/all_to_all | solution.py:389
  69.4 1.7 copy-start
  69.4 1.7 copy-start.2
  71.0 15.7 %copy-start.1 = (f32[2048]{0:T(1024)S(1)}, f32[2048]{0:T(1024)}, u32[]{:S(2)}) copy-start(f32[2048]{0:T(1024)} %param.12) | copy-start | bytes 24580
  71.0 15.7 %copy-start.3 = (s32[8,8]{1,0:T(8,128)S(1)}, s32[8,8]{1,0:T(8,128)}, u32[]{:S(2)}) copy-start(s32[8,8]{1,0:T(8,128)} %refs_1_.3) | copy-start | bytes 772
  71.0 15.7 %copy-start.4 = (f32[128]{0:T(128)S(1)}, f32[128]{0:T(128)}, u32[]{:S(2)}) copy-start(f32[128]{0:T(128)} %param.13) | copy-start | bytes 1540
  100.6 12.4 %collective-permute-start.22 = (bf16[2048,128]{1,0:T(8,128)(2,1)S(1)}, bf16[2048,128]{1,0:T(8,128)(2,1)S(1)}, u32[]{:S(2)}, u32[]{:S(2)}) collective-permute-start(bf16[2048,128]{1,0:T(8,128)(2,1)S(1)} %get-tuple-element.11.refs_0_), channel_id=1, source_target_pairs={{0,64},{1,65},{2,66},{3,67},{4,68},{5,69},{6,70},{7,71},{8,72},{9,... | collective-permute-start | bytes 1572872 | tf_op jit(solution)/shard_map/ppermute | solution.py:25
  102.1 22.2 %collective-permute-start.17 = (bf16[2048,128]{1,0:T(8,128)(2,1)S(1)}, bf16[2048,128]{1,0:T(8,128)(2,1)}, u32[]{:S(2)}, u32[]{:S(2)}) collective-permute-start(bf16[2048,128]{1,0:T(8,128)(2,1)S(1)} %get-tuple-element.12.refs_1_), channel_id=1, source_target_pairs={{0,64},{1,65},{2,66},{3,67},{4,68},{5,69},{6,70},{7,71},{8,72},{9,... | collective-permute-start | bytes 1572872 | tf_op jit(solution)/shard_map/ppermute | solution.py:25
  102.2 24.2 %collective-permute-start.14 = (bf16[2048,128]{1,0:T(8,128)(2,1)S(1)}, bf16[2048,128]{1,0:T(8,128)(2,1)}, u32[]{:S(2)}, u32[]{:S(2)}) collective-permute-start(bf16[2048,128]{1,0:T(8,128)(2,1)S(1)} %get-tuple-element.11.refs_0_), channel_id=1, source_target_pairs={{0,66},{1,67},{2,64},{3,65},{4,70},{5,71},{6,68},{7,69},{8,74},{9,... | collective-permute-start | bytes 1572872 | tf_op jit(solution)/shard_map/ppermute | solution.py:25
  104.8 22.9 %collective-permute-start.25 = (bf16[2048,128]{1,0:T(8,128)(2,1)S(1)}, bf16[2048,128]{1,0:T(8,128)(2,1)S(1)}, u32[]{:S(2)}, u32[]{:S(2)}) collective-permute-start(bf16[2048,128]{1,0:T(8,128)(2,1)S(1)} %get-tuple-element.12.refs_1_), channel_id=1, source_target_pairs={{0,66},{1,67},{2,64},{3,65},{4,70},{5,71},{6,68},{7,69},{8,74},{9,... | collective-permute-start | bytes 1572872 | tf_op jit(solution)/shard_map/ppermute | solution.py:25
  104.9 34.0 %collective-permute-start.20 = (bf16[2048,128]{1,0:T(8,128)(2,1)S(1)}, bf16[2048,128]{1,0:T(8,128)(2,1)S(1)}, u32[]{:S(2)}, u32[]{:S(2)}) collective-permute-start(bf16[2048,128]{1,0:T(8,128)(2,1)S(1)} %get-tuple-element.11.refs_0_), channel_id=1, source_target_pairs={{0,1},{1,0},{2,3},{3,2},{4,5},{5,4},{6,7},{7,6},{8,9},{9,8},{10,11... | collective-permute-start | bytes 1572872 | tf_op jit(solution)/shard_map/ppermute | solution.py:25
  113.1 48.6 %copy-start.5 = (bf16[2048,128]{1,0:T(8,128)(2,1)}, bf16[2048,128]{1,0:T(8,128)(2,1)S(1)}, u32[]{:S(2)}) copy-start(bf16[2048,128]{1,0:T(8,128)(2,1)S(1)} %collective-permute-done.22.refs_0_) | copy-start | bytes 1572868
  113.1 27.0 %collective-permute-start.21 = (bf16[2048,128]{1,0:T(8,128)(2,1)S(1)}, bf16[2048,128]{1,0:T(8,128)(2,1)S(1)}, u32[]{:S(2)}, u32[]{:S(2)}) collective-permute-start(bf16[2048,128]{1,0:T(8,128)(2,1)S(1)} %get-tuple-element.12.refs_1_), channel_id=1, source_target_pairs={{0,1},{1,0},{2,3},{3,2},{4,5},{5,4},{6,7},{7,6},{8,9},{9,8},{10,11... | collective-permute-start | bytes 1572872 | tf_op jit(solution)/shard_map/ppermute | solution.py:25
  124.3 15.8 %collective-permute-start.23 = (bf16[2048,128]{1,0:T(8,128)(2,1)S(1)}, bf16[2048,128]{1,0:T(8,128)(2,1)}, u32[]{:S(2)}, u32[]{:S(2)}) collective-permute-start(bf16[2048,128]{1,0:T(8,128)(2,1)S(1)} %collective-permute-done.22.refs_0_), channel_id=1, source_target_pairs={{0,1},{1,0},{2,3},{3,2},{4,5},{5,4},{6,7},{7,6},{8,9},{9,8},{10,11... | collective-permute-start | bytes 1572872 | tf_op jit(solution)/shard_map/ppermute | solution.py:25
  126.4 14.2 %collective-permute-start.15 = (bf16[2048,128]{1,0:T(8,128)(2,1)}, bf16[2048,128]{1,0:T(8,128)(2,1)}, u32[]{:S(2)}, u32[]{:S(2)}) collective-permute-start(bf16[2048,128]{1,0:T(8,128)(2,1)} %collective-permute-done.14.refs_4_), channel_id=1, source_target_pairs={{0,64},{1,65},{2,66},{3,67},{4,68},{5,69},{6,70},{7,71},{8,72},{9,... | collective-permute-start | bytes 1572872 | tf_op jit(solution)/shard_map/ppermute | solution.py:25
  127.8 2.1 %copy-start.6 = (bf16[2048,128]{1,0:T(8,128)(2,1)}, bf16[2048,128]{1,0:T(8,128)(2,1)S(1)}, u32[]{:S(2)}) copy-start(bf16[2048,128]{1,0:T(8,128)(2,1)S(1)} %collective-permute-done.25.refs_5_) | copy-start | bytes 1572868
  127.8 13.8 %collective-permute-start.18 = (bf16[2048,128]{1,0:T(8,128)(2,1)}, bf16[2048,128]{1,0:T(8,128)(2,1)}, u32[]{:S(2)}, u32[]{:S(2)}) collective-permute-start(bf16[2048,128]{1,0:T(8,128)(2,1)} %collective-permute-done.17.refs_1_), channel_id=1, source_target_pairs={{0,66},{1,67},{2,64},{3,65},{4,70},{5,71},{6,68},{7,69},{8,74},{9,... | collective-permute-start | bytes 1572872 | tf_op jit(solution)/shard_map/ppermute | solution.py:25
  129.8 22.7 %all-to-all-start.2 = ((f32[128,8,128]{2,1,0:T(8,128)}), f32[128,8,128]{2,1,0:T(8,128)S(1)}, u32[]{:S(2)}, u32[]{:S(2)}) async-start(f32[128,8,128]{2,1,0:T(8,128)} %bitcast.14), calls=%async_computation.2 | async-start | bytes 1048576 | tf_op jit(solution)/shard_map/all_to_all | solution.py:387
  138.9 25.5 %collective-permute-start.24 = (bf16[2048,128]{1,0:T(8,128)(2,1)}, bf16[2048,128]{1,0:T(8,128)(2,1)}, u32[]{:S(2)}, u32[]{:S(2)}) collective-permute-start(bf16[2048,128]{1,0:T(8,128)(2,1)} %collective-permute-done.17.refs_1_), channel_id=1, source_target_pairs={{0,1},{1,0},{2,3},{3,2},{4,5},{5,4},{6,7},{7,6},{8,9},{9,8},{10,11... | collective-permute-start | bytes 1572872 | tf_op jit(solution)/shard_map/ppermute | solution.py:25
  140.1 24.3 %collective-permute-start.26 = (bf16[2048,128]{1,0:T(8,128)(2,1)}, bf16[2048,128]{1,0:T(8,128)(2,1)}, u32[]{:S(2)}, u32[]{:S(2)}) collective-permute-start(bf16[2048,128]{1,0:T(8,128)(2,1)} %collective-permute-done.14.refs_4_), channel_id=1, source_target_pairs={{0,1},{1,0},{2,3},{3,2},{4,5},{5,4},{6,7},{7,6},{8,9},{9,8},{10,11... | collective-permute-start | bytes 1572872 | tf_op jit(solution)/shard_map/ppermute | solution.py:25
  140.2 24.2 %collective-permute-start.27 = (bf16[2048,128]{1,0:T(8,128)(2,1)}, bf16[2048,128]{1,0:T(8,128)(2,1)}, u32[]{:S(2)}, u32[]{:S(2)}) collective-permute-start(bf16[2048,128]{1,0:T(8,128)(2,1)} %copy-done.6), channel_id=1, source_target_pairs={{0,1},{1,0},{2,3},{3,2},{4,5},{5,4},{6,7},{7,6},{8,9},{9,8},{10,11... | collective-permute-start | bytes 1572872 | tf_op jit(solution)/shard_map/ppermute | solution.py:25
  140.6 39.4 %collective-permute-start.16 = (bf16[2048,128]{1,0:T(8,128)(2,1)}, bf16[2048,128]{1,0:T(8,128)(2,1)}, u32[]{:S(2)}, u32[]{:S(2)}) collective-permute-start(bf16[2048,128]{1,0:T(8,128)(2,1)} %collective-permute-done.15.refs_0_), channel_id=1, source_target_pairs={{0,1},{1,0},{2,3},{3,2},{4,5},{5,4},{6,7},{7,6},{8,9},{9,8},{10,11... | collective-permute-start | bytes 1572872 | tf_op jit(solution)/shard_map/ppermute | solution.py:25
  141.6 38.4 %collective-permute-start.19 = (bf16[2048,128]{1,0:T(8,128)(2,1)}, bf16[2048,128]{1,0:T(8,128)(2,1)}, u32[]{:S(2)}, u32[]{:S(2)}) collective-permute-start(bf16[2048,128]{1,0:T(8,128)(2,1)} %collective-permute-done.18.refs_1_), channel_id=1, source_target_pairs={{0,1},{1,0},{2,3},{3,2},{4,5},{5,4},{6,7},{7,6},{8,9},{9,8},{10,11... | collective-permute-start | bytes 1572872 | tf_op jit(solution)/shard_map/ppermute | solution.py:25
  153.4 26.6 %all-to-all-start.3 = ((bf16[128,8,128]{2,1,0:T(8,128)(2,1)}), bf16[128,8,128]{2,1,0:T(8,128)(2,1)S(1)}, u32[]{:S(2)}, u32[]{:S(2)}) async-start(bf16[128,8,128]{2,1,0:T(8,128)(2,1)} %broadcast_in_dim.5), calls=%async_computation.3 | async-start | bytes 524288 | tf_op jit(solution)/shard_map/all_to_all | solution.py:389
